TPU v7x, 128 devices: a whole 4x4x4 slice. The times are simulated.
128 devices in a mesh: seq: 8 (over y, core), exp: 16 (over z, x).
Axes of the slice: x: 4, y: 4, z: 4, core: 2. Of those that a mesh axis runs over, the one named last changes fastest.
Arguments:
- resid: bfloat16 [16, 1024, 4096], P('exp', 'seq'), may hold values from -1.5 to 1.5
- queries: bfloat16 [16, 1024, 4096], P('exp', 'seq'), may hold values from -8 to 8
- span_rotated_keys: bfloat16 [16, 1024, 512], P('exp', 'seq'), may hold values from -6 to 6
- span_value_rows: bfloat16 [16, 1024, 512], P('exp', 'seq'), may hold values from -6 to 6
- key_cache: bfloat16 [16, 4, 512, 128], P('exp', None, 'seq'), may hold values from -8 to 8
- prefix_value_cache: bfloat16 [16, 4, 512, 128], P('exp', None, 'seq'), may hold values from -6 to 6
- prefix_len: int32 [16], P('exp'), may hold values from 1 to 512, as said below
- out_weight: bfloat16 [4096, 4096], P('seq'), may hold values from -0.09375 to 0.09375
- norm_gain: float32 [4096], replicated, may hold values from 0.1 to 1.9
- router_weight: bfloat16 [4096, 128], replicated
- expert_ids: int32 [16, 1024, 8], P('exp', 'seq'), may hold values from 0 to 127, all different within a row; in each aligned block of 128 rows (0 to 127, 128 to 255, ..., all dimensions but the last counted through in order) at most 9 rows name the same one
- w_gate: bfloat16 [128, 4096, 768], P(('seq', 'exp')), may hold values from -0.09375 to 0.09375
- w_up: bfloat16 [128, 4096, 768], P(('seq', 'exp')), may hold values from -0.09375 to 0.09375
- w_down: bfloat16 [128, 768, 4096], P(('seq', 'exp')), may hold values from -0.21875 to 0.21875
Outputs:
- layer_out: bfloat16 [16, 1024, 4096], P('exp', 'seq')
Inputs may be any that keep to these rules, and one draw needn't show every extreme that they name: `expert_ids`: in the 128 consecutive tokens of one index of seq, no expert is named by more than 9 routes, a bound that some block reaches. `prefix_len`: some prompt's prefix fills the cache.
All inputs are finite; a program needn't handle non-finite values.
Results may differ from a plain program's by a relative error of at most 0.03.
Values may be sent and summed in bfloat16 or wider, within the bound.
No kernel may reach another device: no remote copies, remote signals or barrier semaphores. Data moves between devices by JAX's collectives and lax.ppermute only.
A program may use at most 192 MiB of HBM per device.

v0:
```python
import jax
import jax.numpy as jnp
import numpy as np
from jax import lax
from jax.sharding import PartitionSpec as P

QUERY_HEAD_HALF = 32
KEY_VALUE_HEADS = 4
HEAD_SIZE = 128
TOP = 8


def expert_mlp(token_rows, gate_part, up_part, down_part):
    gate_val = jnp.dot(token_rows, gate_part, preferred_element_type=jnp.float32)
    up_val = jnp.dot(token_rows, up_part, preferred_element_type=jnp.float32)
    activated = (jax.nn.silu(gate_val) * up_val).astype(jnp.bfloat16)
    return jnp.dot(activated, down_part, preferred_element_type=jnp.float32).astype(jnp.bfloat16)


def per_device(
    resid,
    queries,
    span_rotated_keys,
    span_value_rows,
    key_cache,
    prefix_value_cache,
    prefix_len,
    out_weight,
    norm_gain,
    router_weight,
    expert_ids,
    w_gate,
    w_up,
    w_down,
):
    seq_count = lax.axis_size("seq")
    exp_count = lax.axis_size("exp")
    token_row_block = queries.shape[1]
    model_width = resid.shape[2]
    heads_here = QUERY_HEAD_HALF // seq_count
    group_length = QUERY_HEAD_HALF // KEY_VALUE_HEADS
    key_value_choice = np.arange(seq_count) * heads_here // group_length
    query_parts = queries[0].reshape(token_row_block, seq_count, heads_here * HEAD_SIZE)
    newest_keys = span_rotated_keys[0].reshape(token_row_block, KEY_VALUE_HEADS, HEAD_SIZE)[
        :, key_value_choice, :
    ]
    newest_values = span_value_rows[0].reshape(token_row_block, KEY_VALUE_HEADS, HEAD_SIZE)[
        :, key_value_choice, :
    ]
    fresh_pairs = jnp.concatenate([newest_keys, newest_values], axis=2)
    query_heads, span_pairs = (
        lax.all_to_all(query_parts, "seq", split_axis=1, concat_axis=0, tiled=True),
        lax.all_to_all(fresh_pairs, "seq", split_axis=1, concat_axis=0, tiled=True),
    )
    cache_pairs = jnp.concatenate(
        [key_cache[0][key_value_choice], prefix_value_cache[0][key_value_choice]], axis=2
    )
    prefix_pairs = lax.all_to_all(cache_pairs, "seq", split_axis=0, concat_axis=1, tiled=True)[0]
    span_length = query_heads.shape[0]
    prefix_total = prefix_pairs.shape[0]
    all_keys = jnp.concatenate([prefix_pairs[:, :HEAD_SIZE], span_pairs[:, 0, :HEAD_SIZE]], axis=0)
    all_values = jnp.concatenate(
        [prefix_pairs[:, HEAD_SIZE:], span_pairs[:, 0, HEAD_SIZE:]], axis=0
    )
    query_block = query_heads.reshape(span_length, heads_here, HEAD_SIZE)
    scores = jnp.einsum(
        "thd,jd->htj", query_block, all_keys, preferred_element_type=jnp.float32
    ) * HEAD_SIZE ** (-0.5)
    position = jnp.arange(prefix_total + span_length, dtype=jnp.int32)
    query_pos = jnp.arange(span_length, dtype=jnp.int32)
    usable_keys = jnp.where(
        position[None, :] < prefix_total,
        position[None, :] < prefix_len[0],
        position[None, :] - prefix_total <= query_pos[:, None],
    )
    scores = jnp.where(usable_keys[None], scores, -1e30)
    top_score = jnp.max(scores, axis=2, keepdims=True)
    raised = jnp.exp(scores - top_score)
    attn_weights = (raised / jnp.sum(raised, axis=2, keepdims=True)).astype(jnp.bfloat16)
    attended = jnp.einsum(
        "htj,jd->thd", attn_weights, all_values, preferred_element_type=jnp.float32
    ).astype(jnp.bfloat16)
    attended = attended.reshape(span_length, heads_here * HEAD_SIZE)
    projected = lax.psum_scatter(
        jnp.dot(attended, out_weight, preferred_element_type=jnp.float32).astype(jnp.bfloat16),
        "seq",
        scatter_dimension=0,
        tiled=True,
    ).astype(jnp.float32)
    hidden_state = resid[0].astype(jnp.float32) + projected
    mean_square = jnp.mean(hidden_state * hidden_state, axis=1, keepdims=True)
    normed = (hidden_state * lax.rsqrt(mean_square + 1e-06) * norm_gain).astype(jnp.bfloat16)
    logits = jnp.dot(normed, router_weight, preferred_element_type=jnp.float32)
    chosen_ids = expert_ids[0]
    chosen = jnp.take_along_axis(logits, chosen_ids, axis=1)
    route_weight = jax.nn.softmax(chosen, axis=1)
    expert_total = seq_count * exp_count
    capacity = max(2, (token_row_block * TOP * 9 + 8 * expert_total - 1) // (8 * expert_total))
    flat_ids = chosen_ids.reshape(-1)
    one_hot = (flat_ids[:, None] == jnp.arange(expert_total, dtype=jnp.int32)[None, :]).astype(
        jnp.int32
    )
    running_rank = jnp.cumsum(one_hot, axis=0) - 1
    slot_index = jnp.sum(one_hot * running_rank, axis=1)
    target = flat_ids * capacity + slot_index
    source_token = jnp.arange(token_row_block * TOP, dtype=jnp.int32) // TOP
    slot_token = (
        jnp.full((expert_total * capacity,), token_row_block, jnp.int32)
        .at[target]
        .set(source_token)
    )
    padded = jnp.concatenate([normed, jnp.zeros((1, model_width), jnp.bfloat16)], axis=0)
    send_rows = padded[slot_token].reshape(expert_total, capacity, model_width)
    gate_part = w_gate[0]
    up_part = w_up[0]
    down_part = w_down[0]
    received = lax.all_to_all(send_rows, ("seq", "exp"), split_axis=0, concat_axis=0, tiled=True)
    flat_rows = received.reshape(-1, model_width)
    returned = lax.all_to_all(
        expert_mlp(flat_rows, gate_part, up_part, down_part).reshape(received.shape),
        ("seq", "exp"),
        split_axis=0,
        concat_axis=0,
        tiled=True,
    )
    route_rows = (
        returned.reshape(-1, model_width)[target]
        .astype(jnp.float32)
        .reshape(token_row_block, TOP, model_width)
    )
    mixture = jnp.sum(route_weight[:, :, None] * route_rows, axis=1)
    return (hidden_state + mixture).astype(jnp.bfloat16)[None]


def solution(mesh):
    in_specs = (
        P("exp", "seq", None),
        P("exp", "seq", None),
        P("exp", "seq", None),
        P("exp", "seq", None),
        P("exp", None, "seq", None),
        P("exp", None, "seq", None),
        P("exp"),
        P("seq", None),
        P(),
        P(),
        P("exp", "seq", None),
        P(("seq", "exp"), None, None),
        P(("seq", "exp"), None, None),
        P(("seq", "exp"), None, None),
    )
    out_specs = P("exp", "seq", None)
    return jax.shard_map(
        per_device, mesh=mesh, in_specs=in_specs, out_specs=out_specs, check_vma=False
    )
```

profile of v0, /device:TPU:5, one launch (start us, length us, event | category | flops | bytes accessed | tf_op | source)
XLA Modules:
  0.0 744.5 jit_solution(327297994828588374)
XLA Ops:
  6.5 0.7 pad_clamp_fusion.1
  7.3 1.4 gather_fusion.1
  8.7 1.4 gather_fusion
  10.1 0.7 pad_maximum_fusion.1
  10.9 5.1 all-to-all-start
  16.0 1.0 copy.49
  17.0 0.1 copy.50
  17.2 0.6 gather_fusion.2
  17.8 1.0 copy.51
  18.8 0.1 copy.52
  18.9 0.6 gather_fusion.3
  19.6 0.9 pad_maximum_fusion
  20.4 2.1 all-to-all-done
  22.5 4.4 all-to-all-start.1
  27.6 2.3 copy.53
  29.9 6.6 all-to-all-done.1
  36.4 4.3 all-to-all-start.2
  40.8 2.9 fusion.12
  43.7 0.7 fusion.54
  44.3 0.7 slice_bitcast_fusion.1
  45.1 10.8 %all-to-all-done.2 = bf16[128,8,512]{0,2,1:T(8,128)(2,1)S(1)} async-done(((bf16[128,8,512]{0,2,1:T(8,128)(2,1)}), bf16[128,8,512]{0,2,1:T(8,128)(2,1)S(1)}, u32[]{:S(2)}, u32[]{:S(2)}) %all-to-all-start.2) | async-done | bytes 1048608 | tf_op jit(solution)/shard_map/all_to_all | solution.py:52
  55.9 0.7 copy.54
  56.6 0.5 reshape.233
  57.1 10.7 %fusion.55 = f32[4,1024]{1,0:T(4,128)S(1)} fusion(pred[1024,1536]{0,1:T(8,128)(4,1)} %fusion.12, bf16[1024,4,128]{0,2,1:T(8,128)(2,1)S(1)} %reshape.233, bf16[1024,128]{1,0:T(8,128)(2,1)} %get-tuple-element.6, bf16[512,128]{1,0:T(8,128)(2,1)} %get-tuple-element.8), kind=kOutput, calls=%fused_computation.93 | convolution fusion | flops 1636566528 | bytes 3031040 | tf_op jit(solution)/shard_map/sub | solution.py:78
  67.8 14.3 %fusion.21 = bf16[128,4,1024]{2,0,1:T(8,128)(2,1)} fusion(f32[4,1024]{1,0:T(4,128)S(1)} %fusion.55, pred[1024,1536]{0,1:T(8,128)(4,1)} %fusion.12, bf16[1024,4,128]{0,2,1:T(8,128)(2,1)S(1)} %reshape.233, bf16[1024,128]{1,0:T(8,128)(2,1)S(1)} %get-tuple-element.5, bf16[512,128]{1,0:T(8,128)(2,1)S(1)} %get-tuple-element.7, ...), kind=kOutput, calls=%fused_computation.35 | convolution fusion | flops 3254785536 | bytes 4472832 | tf_op jit(solution)/shard_map/htj,jd->thd/dot_general | solution.py:80
  82.1 10.5 %convolution_convert_fusion.1 = bf16[1024,4096]{1,0:T(8,128)(2,1)} fusion(bf16[1024,512]{0,1:T(8,128)(2,1)} %bitcast.126, bf16[512,4096]{1,0:T(8,128)(2,1)} %param.26), kind=kOutput, calls=%fused_computation.20 | convolution fusion | flops 4299161600 | bytes 13631488 | tf_op jit(solution)/shard_map/dot_general | solution.py:85
  92.6 0.0 reduce-scatter.2.cloned.1.call-update
  92.6 0.7 copy-done.7
  93.2 0.1 copy.58
  93.4 0.1 eq.29
  93.4 0.1 eq.25
  93.5 0.1 copy.60
  93.6 0.1 mul.73
  93.7 0.1 copy.63
  93.8 0.2 fusion.24
  94.1 0.1 copy.64
  94.3 0.4 fusion.23
  94.6 4.3 scatter_custom_fusion
  99.0 46.1 %reduce-scatter.2.cloned.1.call-done = bf16[128,4096]{1,0:T(8,128)(2,1)} async-done(((bf16[1024,4096]{1,0:T(8,128)(2,1)}), bf16[128,4096]{1,0:T(8,128)(2,1)}) %reduce-scatter.2.cloned.1.call-update) | async-done | bytes 1048592 | tf_op jit(solution)/shard_map/reduce_scatter | solution.py:84
  145.1 1.6 multiply_reduce_fusion
  146.8 1.6 multiply_convert_fusion
  148.4 0.1 concatenate.19
  148.5 8.0 %gather_fusion.4 = bf16[1152,4096]{1,0:T(8,128)(2,1)} fusion(bf16[129,4096]{1,0:T(8,128)(2,1)S(1)} %concatenate.19, s32[2048]{0:T(1024)S(1)} %pad_clamp_fusion), kind=kCustom, calls=%fused_computation.4 | custom fusion | bytes 18878976 | tf_op jit(solution)/shard_map/gather | solution.py:113
  156.6 15.1 %reshape.236 = bf16[128,9,4096]{2,1,0:T(8,128)(2,1)} reshape(bf16[1152,4096]{1,0:T(8,128)(2,1)} %gather_fusion.4) | data formatting | bytes 18874368 | tf_op jit(solution)/shard_map/reshape | solution.py:113
  171.7 194.6 %all_to_all.52 = bf16[128,9,4096]{2,1,0:T(8,128)(2,1)} all-to-all(bf16[128,9,4096]{2,1,0:T(8,128)(2,1)} %reshape.236), channel_id=1, replica_groups=mesh['seq'=8,'exp'=16] {'seq','exp'}, dimensions={0} | all-to-all | bytes 18874368 | tf_op jit(solution)/shard_map/all_to_all | solution.py:117
  366.3 15.8 %reshape.237 = bf16[1152,4096]{1,0:T(8,128)(2,1)} reshape(bf16[128,9,4096]{2,1,0:T(8,128)(2,1)} %all_to_all.52) | data formatting | bytes 18874368 | tf_op jit(solution)/shard_map/reshape | solution.py:118
  382.1 12.0 %fusion.10 = f32[1152,768]{1,0:T(8,128)S(1)} fusion(bf16[1152,4096]{1,0:T(8,128)(2,1)} %reshape.237, bf16[1,4096,768]{2,1,0:T(8,128)(2,1)} %param.30), kind=kOutput, calls=%fused_computation.24 | convolution fusion | flops 7247757312 | bytes 19267584 | tf_op jit(solution)/shard_map/dot_general | solution.py:14
  394.2 10.3 %fusion.16 = bf16[1152,768]{1,0:T(8,128)(2,1)S(1)} fusion(bf16[1152,4096]{1,0:T(8,128)(2,1)S(1)} %copy-done.1, bf16[1,4096,768]{2,1,0:T(8,128)(2,1)} %param.31, f32[1152,768]{1,0:T(8,128)S(1)} %fusion.10), kind=kOutput, calls=%fused_computation.29 | convolution fusion | flops 7253065728 | bytes 21037056 | tf_op jit(solution)/shard_map/dot_general | solution.py:15
  404.5 9.6 %convolution_convert_fusion = bf16[1152,4096]{1,0:T(8,128)(2,1)} fusion(bf16[1152,768]{1,0:T(8,128)(2,1)S(1)} %fusion.16, bf16[1,768,4096]{2,1,0:T(8,128)(2,1)S(1)} %bitcast.125), kind=kOutput, calls=%fused_computation.15 | convolution fusion | flops 7252475904 | bytes 17498112 | tf_op jit(solution)/shard_map/dot_general | solution.py:17
  414.0 15.1 %reshape.238 = bf16[128,9,4096]{2,1,0:T(8,128)(2,1)} reshape(bf16[1152,4096]{1,0:T(8,128)(2,1)} %convolution_convert_fusion) | data formatting | bytes 18874368 | tf_op jit(solution)/shard_map/reshape | solution.py:120
  429.1 8.1 %all-to-all-start.4 = ((bf16[128,9,4096]{2,1,0:T(8,128)(2,1)}), bf16[128,9,4096]{2,1,0:T(8,128)(2,1)}, u32[]{:S(2)}, u32[]{:S(2)}) async-start(bf16[128,9,4096]{2,1,0:T(8,128)(2,1)} %reshape.238), calls=%async_computation.5 | async-start | bytes 33554432 | tf_op jit(solution)/shard_map/all_to_all | solution.py:119
  437.3 0.1 copy.59
  437.4 0.1 reshape.290
  437.5 0.4 fusion.56
  437.9 6.8 gather_fusion.6
  444.7 0.1 reshape.293
  444.8 0.1 fusion.53
  444.9 0.2 fusion.31
  445.1 0.1 fusion.30
  445.3 239.6 %all-to-all-done.4 = bf16[128,9,4096]{2,1,0:T(8,128)(2,1)} async-done(((bf16[128,9,4096]{2,1,0:T(8,128)(2,1)}), bf16[128,9,4096]{2,1,0:T(8,128)(2,1)}, u32[]{:S(2)}, u32[]{:S(2)}) %all-to-all-start.4) | async-done | bytes 9437216 | tf_op jit(solution)/shard_map/all_to_all | solution.py:119
  684.9 15.8 %reshape.239 = bf16[1152,4096]{1,0:T(8,128)(2,1)} reshape(bf16[128,9,4096]{2,1,0:T(8,128)(2,1)} %all-to-all-done.4) | data formatting | bytes 18874368 | tf_op jit(solution)/shard_map/reshape | solution.py:127
  700.7 20.2 %gather_fusion.5 = bf16[1024,4096]{1,0:T(8,128)(2,1)} fusion(bf16[1152,4096]{1,0:T(8,128)(2,1)} %reshape.239, s32[1024]{0:T(1024)S(1)} %broadcast_clamp_fusion), kind=kCustom, calls=%fused_computation.5 | custom fusion | bytes 16781312 | tf_op jit(solution)/shard_map/gather | solution.py:127
  720.9 13.3 %fusion.2 = f32[128,4096]{1,0:T(8,128)} fusion(bf16[1024,4096]{1,0:T(8,128)(2,1)} %gather_fusion.5, f32[128,8]{1,0:T(8,128)S(1)} %fusion.30), kind=kLoop, calls=%fused_computation.14 | loop fusion | flops 12058624 | bytes 10489856 | tf_op jit(solution)/shard_map/reduce_sum | solution.py:131
  734.3 2.9 fusion.22
  (37 shorter events, 0.2 us)
Async XLA Ops:
  6.5 431.0 %copy-start = (bf16[4096,128]{1,0:T(8,128)(2,1)S(1)}, bf16[4096,128]{1,0:T(8,128)(2,1)}, u32[]{:S(2)}) copy-start(bf16[4096,128]{1,0:T(8,128)(2,1)} %param.28) | copy-start | bytes 3145732
  10.9 11.6 %all-to-all-start = ((bf16[8,64,256]{2,1,0:T(8,128)(2,1)}), bf16[8,64,256]{2,1,0:T(8,128)(2,1)S(1)}, u32[]{:S(2)}, u32[]{:S(2)}) async-start(bf16[8,64,256]{2,1,0:T(8,128)(2,1)} %pad_maximum_fusion.1), calls=%async_computation | async-start | bytes 524288 | tf_op jit(solution)/shard_map/all_to_all | solution.py:58
  22.5 13.9 %all-to-all-start.1 = ((bf16[128,8,256]{2,0,1:T(8,128)(2,1)}), bf16[128,8,256]{2,0,1:T(8,128)(2,1)S(1)}, u32[]{:S(2)}, u32[]{:S(2)}) async-start(bf16[128,8,256]{2,0,1:T(8,128)(2,1)} %pad_maximum_fusion), calls=%async_computation.1 | async-start | bytes 1048576 | tf_op jit(solution)/shard_map/all_to_all | solution.py:53
  36.4 19.5 %all-to-all-start.2 = ((bf16[128,8,512]{0,2,1:T(8,128)(2,1)}), bf16[128,8,512]{0,2,1:T(8,128)(2,1)S(1)}, u32[]{:S(2)}, u32[]{:S(2)}) async-start(bf16[128,8,512]{0,2,1:T(8,128)(2,1)} %bitcast.18), calls=%async_computation.2 | async-start | bytes 2097152 | tf_op jit(solution)/shard_map/all_to_all | solution.py:52
  40.8 104.3 %reduce-scatter.2.cloned.1.call-start = ((), (), s32[]{:S(2)}) async-start(), calls=%async_computation.6 | async-start | bytes 9437184 | tf_op jit(solution)/shard_map/reduce_scatter | solution.py:84
  57.1 10.7 %copy-start.5 = (bf16[1024,128]{1,0:T(8,128)(2,1)S(1)}, bf16[1024,128]{1,0:T(8,128)(2,1)}, u32[]{:S(2)}) copy-start(bf16[1024,128]{1,0:T(8,128)(2,1)} %get-tuple-element.6) | copy-start | bytes 786436
  57.1 10.7 %copy-start.6 = (bf16[512,128]{1,0:T(8,128)(2,1)S(1)}, bf16[512,128]{1,0:T(8,128)(2,1)}, u32[]{:S(2)}) copy-start(bf16[512,128]{1,0:T(8,128)(2,1)} %get-tuple-element.8) | copy-start | bytes 393220
  92.6 0.7 copy-start.7
  92.6 52.6 %copy-start.2 = (bf16[1,128,4096]{2,1,0:T(8,128)(2,1)S(1)}, bf16[1,128,4096]{2,1,0:T(8,128)(2,1)}, u32[]{:S(2)}) copy-start(bf16[1,128,4096]{2,1,0:T(8,128)(2,1)} %param.19) | copy-start | bytes 3145732
  92.6 54.2 %copy-start.8 = (f32[4096]{0:T(1024)S(1)}, f32[4096]{0:T(1024)}, u32[]{:S(2)}) copy-start(f32[4096]{0:T(1024)} %param.27) | copy-start | bytes 49156
  382.1 12.0 %copy-start.1 = (bf16[1152,4096]{1,0:T(8,128)(2,1)S(1)}, bf16[1152,4096]{1,0:T(8,128)(2,1)}, u32[]{:S(2)}) copy-start(bf16[1152,4096]{1,0:T(8,128)(2,1)} %reshape.237) | copy-start | bytes 28311556
  382.1 22.3 %slice-start = ((s8[6291456]{0:T(1024)(128)(4,1)}), s8[4194304]{0:T(1024)(128)(4,1)S(1)}, s32[]{:S(2)}) async-start(s8[6291456]{0:T(1024)(128)(4,1)} %bitcast.124), calls=%async_computation.7 | async-start | bytes 8388608
  394.1 10.3 %slice-start.1 = ((s8[6291456]{0:T(1024)(128)(4,1)}), s8[2097152]{0:T(1024)(128)(4,1)S(1)}, s32[]{:S(2)}) async-start(s8[6291456]{0:T(1024)(128)(4,1)} %bitcast.124), calls=%async_computation.8 | async-start | bytes 4194304
  429.1 255.7 %all-to-all-start.4 = ((bf16[128,9,4096]{2,1,0:T(8,128)(2,1)}), bf16[128,9,4096]{2,1,0:T(8,128)(2,1)}, u32[]{:S(2)}, u32[]{:S(2)}) async-start(bf16[128,9,4096]{2,1,0:T(8,128)(2,1)} %reshape.238), calls=%async_computation.5 | async-start | bytes 33554432 | tf_op jit(solution)/shard_map/all_to_all | solution.py:119
  720.9 13.4 %copy-start.3 = (bf16[1,128,4096]{2,1,0:T(8,128)(2,1)S(1)}, bf16[1,128,4096]{2,1,0:T(8,128)(2,1)}, u32[]{:S(2)}) copy-start(bf16[1,128,4096]{2,1,0:T(8,128)(2,1)} %param.19) | copy-start | bytes 3145732
  720.9 13.3 %copy-start.4 = (bf16[128,4096]{1,0:T(8,128)(2,1)S(1)}, bf16[128,4096]{1,0:T(8,128)(2,1)}, u32[]{:S(2)}) copy-start(bf16[128,4096]{1,0:T(8,128)(2,1)} %reduce-scatter.2.cloned.1.call-done) | copy-start | bytes 3145732
Sparse Core Ops, SparseCore 0:
  92.7 52.3 reduce-scatter.1
where the time goes:
time: 752 us; the launch traced here: 744 us
  waiting for transfers between devices  305 us (41%)
  blocking collectives  195 us (26%)
  local copies, waits for them, and re-layouts  114 us (15%)
  matrix products  67.7 us (9%)
  other arithmetic  25.8 us (3%)
  starting transfers between devices  22 us (3%)
  between operations  14.9 us (2%)
    all_to_all x1, waiting for transfers between devices, per_device(): lax.all_to_all(expert_mlp(flat_rows, gate_part, up_part, down_part).resha...  240 us
    all_to_all x1, blocking collectives, per_device(): lax.all_to_all(send_rows, ('seq', 'exp'), split_axis=0, concat_axis=0, ti...  195 us
    reduce_scatter x1, waiting for transfers between devices, per_device(): lax.psum_scatter(jnp.dot(attended, out_weight, preferred_element_type=jnp...  46.1 us
    gather x1, local copies, waits for them, and re-layouts, per_device(): returned.reshape(-1, model_width)[target].astype(jnp.float32)  20.2 us
    reshape x1, local copies, waits for them, and re-layouts, per_device(): flat_rows = received.reshape(-1, model_width)  15.8 us
    reshape x1, local copies, waits for them, and re-layouts, per_device(): returned.reshape(-1, model_width)[target].astype(jnp.float32)  15.8 us
    reshape x1, local copies, waits for them, and re-layouts, per_device(): send_rows = padded[slot_token].reshape(expert_total, capacity, model_width)  15.1 us
    reshape x1, local copies, waits for them, and re-layouts, per_device(): expert_mlp(flat_rows, gate_part, up_part, down_part).reshape(received.shape)  15.1 us
  transfers between devices with their start and end apart: 5, of which 5 were waited for; matrix products, arithmetic and copies ran while one was open for 3% of the time, Pallas kernels for 0%

commit v1 on v0

--- a/solution.py
+++ b/solution.py
@@ -1,20 +1,269 @@
+import functools
+
 import jax
 import jax.numpy as jnp
 import numpy as np
 from jax import lax
+from jax.experimental import pallas as pl
+from jax.experimental.pallas import tpu as pltpu
 from jax.sharding import PartitionSpec as P
 
 QUERY_HEAD_HALF = 32
 KEY_VALUE_HEADS = 4
 HEAD_SIZE = 128
 TOP = 8
-
-
-def expert_mlp(token_rows, gate_part, up_part, down_part):
-    gate_val = jnp.dot(token_rows, gate_part, preferred_element_type=jnp.float32)
-    up_val = jnp.dot(token_rows, up_part, preferred_element_type=jnp.float32)
-    activated = (jax.nn.silu(gate_val) * up_val).astype(jnp.bfloat16)
-    return jnp.dot(activated, down_part, preferred_element_type=jnp.float32).astype(jnp.bfloat16)
+SLOTS = 8
+MIB = 1 << 20
+
+
+def dot(a, b):
+    return jnp.dot(a, b, preferred_element_type=jnp.float32)
+
+
+def dot_nt(a, b):
+    return lax.dot_general(a, b, (((1,), (1,)), ((), ())), preferred_element_type=jnp.float32)
+
+
+def spread(experts):
+    rows = lax.broadcasted_iota(jnp.int32, (experts * SLOTS, experts), 0)
+    cols = lax.broadcasted_iota(jnp.int32, (experts * SLOTS, experts), 1)
+    return jnp.where(rows // SLOTS == cols, 1.0, 0.0).astype(jnp.bfloat16)
+
+
+def route_kernel(
+    resid_ref, proj_ref, gain_ref, router_ref, ids_ref,
+    send_ref, rank_ref, weight_ref,
+    normed_ref, pick_ref,
+):
+    step = pl.program_id(0)
+    tokens, width = resid_ref.shape
+    experts = router_ref.shape[1]
+    cols = send_ref.shape[1]
+    extra = width // cols
+
+    @pl.when(step == 0)
+    def _():
+        hidden = resid_ref[...].astype(jnp.float32) + proj_ref[...].astype(jnp.float32)
+        mean_square = jnp.mean(hidden * hidden, axis=1, keepdims=True)
+        normed = (hidden * lax.rsqrt(mean_square + 1e-06) * gain_ref[...]).astype(jnp.bfloat16)
+        for j in range(extra):
+            normed_ref[pl.ds(j * tokens, tokens), :] = normed[:, j * cols : (j + 1) * cols]
+        logits = dot(normed, router_ref[...])
+        lane = lax.broadcasted_iota(jnp.int32, (tokens, experts), 1)
+        named = jnp.zeros((tokens, experts), jnp.bool_)
+        for k in range(TOP):
+            named = named | (ids_ref[:, k : k + 1] == lane)
+        masked = jnp.where(named, logits, -jnp.inf)
+        top = jnp.max(masked, axis=1, keepdims=True)
+        raised = jnp.where(named, jnp.exp(logits - top), 0.0)
+        weight_ref[...] = raised / jnp.sum(raised, axis=1, keepdims=True)
+        earlier = jnp.where(
+            lax.broadcasted_iota(jnp.int32, (tokens, tokens), 0)
+            > lax.broadcasted_iota(jnp.int32, (tokens, tokens), 1),
+            1.0,
+            0.0,
+        ).astype(jnp.bfloat16)
+        member = jnp.where(named, 1.0, 0.0).astype(jnp.bfloat16)
+        rank = jnp.where(named, dot(earlier, member) + 1.0, 0.0)
+        rank_ref[...] = rank
+        wide_rank = dot_nt(spread(experts), rank.astype(jnp.bfloat16))
+        slot = (
+            lax.broadcasted_iota(jnp.int32, (experts * SLOTS, tokens), 0) % SLOTS
+        ).astype(jnp.float32)
+        pick_ref[:, pl.ds(0, tokens)] = jnp.where(wide_rank == slot + 1.0, 1.0, 0.0).astype(
+            jnp.bfloat16
+        )
+        for j in range(extra):
+            pick_ref[:, pl.ds((j + 1) * tokens, tokens)] = jnp.where(
+                (wide_rank == SLOTS + 1.0) & (slot == j), 1.0, 0.0
+            ).astype(jnp.bfloat16)
+
+    @pl.when(step < extra)
+    def _():
+        start = pl.multiple_of(jnp.minimum(step, extra - 1) * tokens, tokens)
+        send_ref[...] = dot(
+            pick_ref[:, pl.ds(0, tokens)], normed_ref[pl.ds(start, tokens), :]
+        ).astype(jnp.bfloat16)
+
+    @pl.when(step == extra)
+    def _():
+        send_ref[...] = dot(
+            pick_ref[:, pl.ds(tokens, extra * tokens)], normed_ref[...]
+        ).astype(jnp.bfloat16)
+
+
+def route(resid, projected, gain, router, ids):
+    tokens, width = resid.shape
+    experts = router.shape[1]
+    cols = width // SLOTS
+    whole = lambda shape: pl.BlockSpec(shape, lambda j: (0, 0))
+    return pl.pallas_call(
+        route_kernel,
+        grid=(SLOTS + 1,),
+        in_specs=[
+            whole((tokens, width)),
+            whole((tokens, width)),
+            whole((1, width)),
+            whole((width, experts)),
+            whole((tokens, TOP)),
+        ],
+        out_specs=[
+            pl.BlockSpec((experts * SLOTS, cols), lambda j: (0, j)),
+            whole((tokens, experts)),
+            whole((tokens, experts)),
+        ],
+        out_shape=[
+            jax.ShapeDtypeStruct((experts * SLOTS, width + cols), jnp.bfloat16),
+            jax.ShapeDtypeStruct((tokens, experts), jnp.float32),
+            jax.ShapeDtypeStruct((tokens, experts), jnp.float32),
+        ],
+        scratch_shapes=[
+            pltpu.VMEM((SLOTS * tokens, cols), jnp.bfloat16),
+            pltpu.VMEM((experts * SLOTS, (SLOTS + 1) * tokens), jnp.bfloat16),
+        ],
+        compiler_params=pltpu.CompilerParams(vmem_limit_bytes=48 * MIB),
+        name="route",
+    )(resid, projected, gain, router, ids)
+
+
+def expert_kernel(
+    rows_ref, extra_ref, gate_ref, up_ref, down_ref, out_ref, gate_acc, up_acc, act_ref, last_ref
+):
+    step = pl.program_id(0)
+    blocks = SLOTS
+    main, cols = rows_ref.shape
+    sources = main // SLOTS
+
+    def lane_pick(j):
+        source = lax.broadcasted_iota(jnp.int32, (sources, main), 0)
+        column = lax.broadcasted_iota(jnp.int32, (sources, main), 1)
+        return jnp.where(column == source * SLOTS + j, 1.0, 0.0).astype(jnp.bfloat16)
+
+    @pl.when(step < blocks)
+    def _():
+        ninth = dot(lane_pick(step), extra_ref[...]).astype(jnp.bfloat16)
+        rows = jnp.concatenate([rows_ref[...], ninth], axis=0)
+        gate_part, up_part = dot(rows, gate_ref[0]), dot(rows, up_ref[0])
+
+        @pl.when(step == 0)
+        def _():
+            gate_acc[...] = gate_part
+            up_acc[...] = up_part
+
+        @pl.when(step > 0)
+        def _():
+            gate_acc[...] += gate_part
+            up_acc[...] += up_part
+
+    @pl.when(step == blocks - 1)
+    def _():
+        gate_val = gate_acc[...]
+        act_ref[...] = (gate_val / (1.0 + jnp.exp(-gate_val)) * up_acc[...]).astype(jnp.bfloat16)
+        last_ref[...] = jnp.zeros_like(last_ref)
+
+    @pl.when((step >= blocks) & (step < 2 * blocks))
+    def _():
+        result = dot(act_ref[...], down_ref[0]).astype(jnp.bfloat16)
+        out_ref[...] = result[:main]
+        j = step - blocks
+        row = lax.broadcasted_iota(jnp.int32, (main, sources), 0)
+        source = lax.broadcasted_iota(jnp.int32, (main, sources), 1)
+        place = jnp.where(row == source * SLOTS + j, 1.0, 0.0).astype(jnp.bfloat16)
+        last_ref[...] += dot(place, result[main:])
+
+    @pl.when(step == 2 * blocks)
+    def _():
+        out_ref[...] = last_ref[...].astype(jnp.bfloat16)
+
+
+def expert(rows, w_gate, w_up, w_down):
+    main = rows.shape[0]
+    _, width, hidden = w_gate.shape
+    cols = width // SLOTS
+    tall = main + main // SLOTS
+    first = lambda s: jnp.minimum(s, SLOTS - 1)
+    second = lambda s: jnp.clip(s - SLOTS, 0, SLOTS - 1)
+    return pl.pallas_call(
+        expert_kernel,
+        grid=(2 * SLOTS + 1,),
+        in_specs=[
+            pl.BlockSpec((main, cols), lambda s: (0, first(s))),
+            pl.BlockSpec((main, cols), lambda s: (0, SLOTS)),
+            pl.BlockSpec((1, cols, hidden), lambda s: (0, first(s), 0)),
+            pl.BlockSpec((1, cols, hidden), lambda s: (0, first(s), 0)),
+            pl.BlockSpec((1, hidden, cols), lambda s: (0, 0, second(s))),
+        ],
+        out_specs=pl.BlockSpec((main, cols), lambda s: (0, jnp.clip(s - SLOTS, 0, SLOTS))),
+        out_shape=jax.ShapeDtypeStruct(rows.shape, jnp.bfloat16),
+        scratch_shapes=[
+            pltpu.VMEM((tall, hidden), jnp.float32),
+            pltpu.VMEM((tall, hidden), jnp.float32),
+            pltpu.VMEM((tall, hidden), jnp.bfloat16),
+            pltpu.VMEM((main, cols), jnp.float32),
+        ],
+        compiler_params=pltpu.CompilerParams(vmem_limit_bytes=52 * MIB),
+        name="expert",
+    )(rows, rows, w_gate, w_up, w_down)
+
+
+def combine_kernel(
+    rows_ref, extra_ref, rank_ref, weight_ref, resid_ref, proj_ref, out_ref, main_ref, ninth_ref
+):
+    step = pl.program_id(0)
+    tokens, experts = rank_ref.shape
+
+    @pl.when(step == 0)
+    def _():
+        rank = rank_ref[...]
+        weight = weight_ref[...]
+        high = weight.astype(jnp.bfloat16)
+        low = (weight - high.astype(jnp.float32)).astype(jnp.bfloat16)
+        picks = spread(experts)
+        wide_rank = dot_nt(rank.astype(jnp.bfloat16), picks)
+        slot = (
+            lax.broadcasted_iota(jnp.int32, wide_rank.shape, 1) % SLOTS
+        ).astype(jnp.float32)
+        for half, part in enumerate((high, low)):
+            wide = dot_nt(part, picks)
+            rows = pl.ds(half * tokens, tokens)
+            main_ref[rows, :] = jnp.where(wide_rank == slot + 1.0, wide, 0.0).astype(jnp.bfloat16)
+            ninth_ref[rows, :] = jnp.where(wide_rank == SLOTS + 1.0, wide, 0.0).astype(
+                jnp.bfloat16
+            )
+
+    slot = lax.broadcasted_iota(jnp.int32, ninth_ref.shape, 1) % SLOTS
+    ninth = ninth_ref[...]
+    ninth = jnp.where(slot == step, ninth, jnp.zeros_like(ninth))
+    both = dot(main_ref[...], rows_ref[...]) + dot(ninth, extra_ref[...])
+    hidden = resid_ref[...].astype(jnp.float32) + proj_ref[...].astype(jnp.float32)
+    out_ref[...] = (hidden + (both[:tokens] + both[tokens:])).astype(jnp.bfloat16)
+
+
+def combine(rows, rank, weight, resid, projected):
+    tokens, width = resid.shape
+    main = rows.shape[0]
+    experts = rank.shape[1]
+    cols = width // SLOTS
+    return pl.pallas_call(
+        combine_kernel,
+        grid=(SLOTS,),
+        in_specs=[
+            pl.BlockSpec((main, cols), lambda j: (0, j)),
+            pl.BlockSpec((main, cols), lambda j: (0, SLOTS)),
+            pl.BlockSpec((tokens, experts), lambda j: (0, 0)),
+            pl.BlockSpec((tokens, experts), lambda j: (0, 0)),
+            pl.BlockSpec((tokens, cols), lambda j: (0, j)),
+            pl.BlockSpec((tokens, cols), lambda j: (0, j)),
+        ],
+        out_specs=pl.BlockSpec((tokens, cols), lambda j: (0, j)),
+        out_shape=jax.ShapeDtypeStruct((tokens, width), jnp.bfloat16),
+        scratch_shapes=[
+            pltpu.VMEM((2 * tokens, main), jnp.bfloat16),
+            pltpu.VMEM((2 * tokens, main), jnp.bfloat16),
+        ],
+        compiler_params=pltpu.CompilerParams(vmem_limit_bytes=48 * MIB),
+        name="combine",
+    )(rows, rows, rank, weight, resid, projected)
 
 
 def per_device(
@@ -34,7 +283,6 @@
     w_down,
 ):
     seq_count = lax.axis_size("seq")
-    exp_count = lax.axis_size("exp")
     token_row_block = queries.shape[1]
     model_width = resid.shape[2]
     heads_here = QUERY_HEAD_HALF // seq_count
@@ -86,50 +334,21 @@
         "seq",
         scatter_dimension=0,
         tiled=True,
-    ).astype(jnp.float32)
-    hidden_state = resid[0].astype(jnp.float32) + projected
-    mean_square = jnp.mean(hidden_state * hidden_state, axis=1, keepdims=True)
-    normed = (hidden_state * lax.rsqrt(mean_square + 1e-06) * norm_gain).astype(jnp.bfloat16)
-    logits = jnp.dot(normed, router_weight, preferred_element_type=jnp.float32)
-    chosen_ids = expert_ids[0]
-    chosen = jnp.take_along_axis(logits, chosen_ids, axis=1)
-    route_weight = jax.nn.softmax(chosen, axis=1)
-    expert_total = seq_count * exp_count
-    capacity = max(2, (token_row_block * TOP * 9 + 8 * expert_total - 1) // (8 * expert_total))
-    flat_ids = chosen_ids.reshape(-1)
-    one_hot = (flat_ids[:, None] == jnp.arange(expert_total, dtype=jnp.int32)[None, :]).astype(
-        jnp.int32
-    )
-    running_rank = jnp.cumsum(one_hot, axis=0) - 1
-    slot_index = jnp.sum(one_hot * running_rank, axis=1)
-    target = flat_ids * capacity + slot_index
-    source_token = jnp.arange(token_row_block * TOP, dtype=jnp.int32) // TOP
-    slot_token = (
-        jnp.full((expert_total * capacity,), token_row_block, jnp.int32)
-        .at[target]
-        .set(source_token)
-    )
-    padded = jnp.concatenate([normed, jnp.zeros((1, model_width), jnp.bfloat16)], axis=0)
-    send_rows = padded[slot_token].reshape(expert_total, capacity, model_width)
-    gate_part = w_gate[0]
-    up_part = w_up[0]
-    down_part = w_down[0]
-    received = lax.all_to_all(send_rows, ("seq", "exp"), split_axis=0, concat_axis=0, tiled=True)
-    flat_rows = received.reshape(-1, model_width)
-    returned = lax.all_to_all(
-        expert_mlp(flat_rows, gate_part, up_part, down_part).reshape(received.shape),
-        ("seq", "exp"),
-        split_axis=0,
-        concat_axis=0,
-        tiled=True,
-    )
-    route_rows = (
-        returned.reshape(-1, model_width)[target]
-        .astype(jnp.float32)
-        .reshape(token_row_block, TOP, model_width)
-    )
-    mixture = jnp.sum(route_weight[:, :, None] * route_rows, axis=1)
-    return (hidden_state + mixture).astype(jnp.bfloat16)[None]
+    )
+    experts = router_weight.shape[1]
+    send, rank, weight = route(
+        resid[0], projected, norm_gain.reshape(1, model_width), router_weight, expert_ids[0]
+    )
+
+    def exchange(rows):
+        blocks = rows.reshape(experts, SLOTS, rows.shape[1])
+        return lax.all_to_all(
+            blocks, ("seq", "exp"), split_axis=0, concat_axis=0, tiled=True
+        ).reshape(rows.shape)
+
+    received = exchange(send)
+    returned = exchange(expert(received, w_gate, w_up, w_down))
+    return combine(returned, rank, weight, resid[0], projected)[None]
 
 
 def solution(mesh):

time: 752 us -> 445 us (0.59)
  waiting for transfers between devices: 305 us -> 73.2 us
  local copies, waits for them, and re-layouts: 114 us -> 10.5 us
  Pallas kernels: 0 us -> 60.5 us
  blocking collectives: 195 us -> 231 us
  matrix products: 67.7 us -> 32.8 us
  other arithmetic: 25.8 us -> 5.19 us
  starting transfers between devices: 22 us -> 13.9 us
    all_to_all x1 -> x0, waiting for transfers between devices: 240 us -> none  [per_device(): lax.all_to_all(expert_mlp(flat_rows, gate_part, up_part, down_part).resha...]
    reshape x4 -> x0, local copies, waits for them, and re-layouts: 61.9 us -> none  [the longest x1 15.8 us: per_device(): flat_rows = received.reshape(-1, model_width)]
    pallas_call x0 -> x3, Pallas kernels: none -> 60.5 us  [the longest x1 40.3 us: expert(): pl.pallas_call(expert_kernel, grid=(2 * SLOTS + 1,), in_specs=[pl.BlockSp...]
    all_to_all x1 -> x2, blocking collectives: 195 us -> 231 us  [exchange(): lax.all_to_all(blocks, ('seq', 'exp'), split_axis=0, concat_axis=0, tiled...]
    gather x6 -> x0, local copies, waits for them, and re-layouts: 35.3 us -> none  [the longest x1 20.2 us: per_device(): returned.reshape(-1, model_width)[target].astype(jnp.float32)]
    dot_general x4 -> x0, matrix products: 32.2 us -> none  [the longest x1 12 us: expert_mlp(): jnp.dot(token_rows, gate_part, preferred_element_type=jnp.float32)]
    reduce_sum x4 -> x0, other arithmetic: 15.5 us -> none  [the longest x1 13.3 us: per_device(): mixture = jnp.sum(route_weight[:, :, None] * route_rows, axis=1)]
    all_to_all x1 -> x0, starting transfers between devices: 8.13 us -> none  [per_device(): lax.all_to_all(expert_mlp(flat_rows, gate_part, up_part, down_part).resha...]
  transfers between devices with their start and end apart: 5 -> 4, of which waited for: 5 -> 4; matrix products, arithmetic and copies ran while one was open for 3% -> 2% of each run, Pallas kernels for 0% -> 0%
where the time goes in v1:
time: 445 us; the launch traced here: 441 us
  blocking collectives  231 us (52%)
  waiting for transfers between devices  73.2 us (16%)
  Pallas kernels  60.5 us (14%)
  matrix products  32.8 us (7%)
  between operations  14.2 us (3%)
  starting transfers between devices  13.9 us (3%)
  local copies, waits for them, and re-layouts  10.5 us (2%)
  other arithmetic  5.19 us (1%)
    all_to_all x2, blocking collectives, exchange(): lax.all_to_all(blocks, ('seq', 'exp'), split_axis=0, concat_axis=0, tiled...  231 us
    reduce_scatter x1, waiting for transfers between devices, per_device(): lax.psum_scatter(jnp.dot(attended, out_weight, preferred_element_type=jnp...  52.4 us
    pallas_call x1, Pallas kernels, expert(): pl.pallas_call(expert_kernel, grid=(2 * SLOTS + 1,), in_specs=[pl.BlockSp...  40.3 us
    dot_general x1, matrix products, per_device(): jnp.einsum('htj,jd->thd', attn_weights, all_values, preferred_element_typ...  13.3 us
    all_to_all x1, waiting for transfers between devices, per_device(): lax.all_to_all(query_parts, 'seq', split_axis=1, concat_axis=0, tiled=True)  12.2 us
    pallas_call x1, Pallas kernels, combine(): pl.pallas_call(combine_kernel, grid=(SLOTS,), in_specs=[pl.BlockSpec((mai...  10.4 us
    sub x1, matrix products, per_device(): raised = jnp.exp(scores - top_score)  10.2 us
    pallas_call x1, Pallas kernels, route(): pl.pallas_call(route_kernel, grid=(SLOTS + 1,), in_specs=[whole((tokens,...  9.84 us
  transfers between devices with their start and end apart: 4, of which 4 were waited for; matrix products, arithmetic and copies ran while one was open for 2% of the time, Pallas kernels for 0%

profile of v1, /device:TPU:5, one launch (start us, length us, event | category | flops | bytes accessed | tf_op | source)
XLA Modules:
  0.0 441.4 jit_solution(9340946540638619995)
XLA Ops:
  6.5 0.0 copy-start
  6.5 0.7 pad_clamp_fusion
  7.2 0.1 copy-done
  7.4 0.6 gather_fusion.1
  8.0 1.4 gather_fusion
  9.4 0.7 pad_maximum_fusion.1
  10.1 5.1 %all-to-all-start = ((bf16[8,64,256]{2,1,0:T(8,128)(2,1)}), bf16[8,64,256]{2,1,0:T(8,128)(2,1)S(1)}, u32[]{:S(2)}, u32[]{:S(2)}) async-start(bf16[8,64,256]{2,1,0:T(8,128)(2,1)} %pad_maximum_fusion.1), calls=%async_computation | async-start | bytes 524288 | tf_op jit(solution)/shard_map/all_to_all | solution.py:306
  15.3 1.0 copy.37
  16.3 0.1 copy.38
  16.4 0.6 gather_fusion.2
  17.0 1.0 copy.39
  18.1 0.1 copy.40
  18.2 0.6 gather_fusion.3
  18.8 0.9 pad_maximum_fusion
  19.7 2.1 all-to-all-done
  21.8 4.4 %all-to-all-start.1 = ((bf16[128,8,256]{2,0,1:T(8,128)(2,1)}), bf16[128,8,256]{2,0,1:T(8,128)(2,1)S(1)}, u32[]{:S(2)}, u32[]{:S(2)}) async-start(bf16[128,8,256]{2,0,1:T(8,128)(2,1)} %pad_maximum_fusion), calls=%async_computation.1 | async-start | bytes 1048576 | tf_op jit(solution)/shard_map/all_to_all | solution.py:301
  26.8 2.3 copy.41
  29.1 6.6 %all-to-all-done.1 = bf16[128,8,256]{2,0,1:T(8,128)(2,1)S(1)} async-done(((bf16[128,8,256]{2,0,1:T(8,128)(2,1)}), bf16[128,8,256]{2,0,1:T(8,128)(2,1)S(1)}, u32[]{:S(2)}, u32[]{:S(2)}) %all-to-all-start.1) | async-done | bytes 524320 | tf_op jit(solution)/shard_map/all_to_all | solution.py:301
  35.7 4.3 all-to-all-start.2
  40.0 0.0 reduce-scatter.2.cloned.1.call-start
  40.0 2.9 fusion.6
  43.0 12.2 %all-to-all-done.2 = bf16[128,8,512]{0,2,1:T(8,128)(2,1)S(1)} async-done(((bf16[128,8,512]{0,2,1:T(8,128)(2,1)}), bf16[128,8,512]{0,2,1:T(8,128)(2,1)S(1)}, u32[]{:S(2)}, u32[]{:S(2)}) %all-to-all-start.2) | async-done | bytes 1048608 | tf_op jit(solution)/shard_map/all_to_all | solution.py:300
  55.1 0.7 copy.42
  55.8 0.5 reshape.92
  56.3 10.2 %fusion.27 = f32[4,1024]{1,0:T(4,128)S(1)} fusion(pred[1024,1536]{0,1:T(8,128)(4,1)} %fusion.6, bf16[1024,4,128]{0,2,1:T(8,128)(2,1)S(1)} %reshape.92, bf16[1024,128]{1,0:T(8,128)(2,1)S(1)} %get-tuple-element.12, bf16[512,128]{1,0:T(8,128)(2,1)S(1)} %get-tuple-element.14), kind=kOutput, calls=%fused_computation.40 | convolution fusion | flops 1636566528 | bytes 3031040 | tf_op jit(solution)/shard_map/sub | solution.py:326
  66.6 13.3 %fusion.9 = bf16[128,4,1024]{2,0,1:T(8,128)(2,1)S(1)} fusion(f32[4,1024]{1,0:T(4,128)S(1)} %fusion.27, pred[1024,1536]{0,1:T(8,128)(4,1)} %fusion.6, bf16[1024,4,128]{0,2,1:T(8,128)(2,1)S(1)} %reshape.92, bf16[1024,128]{1,0:T(8,128)(2,1)S(1)} %get-tuple-element.11, bf16[512,128]{1,0:T(8,128)(2,1)S(1)} %get-tuple-element.13, ...), kind=kOutput, calls=%fused_computation.17 | convolution fusion | flops 3254785536 | bytes 4472832 | tf_op jit(solution)/shard_map/htj,jd->thd/dot_general | solution.py:328
  79.9 0.0 copy-start.7
  79.9 0.0 copy-start.2
  79.9 0.0 copy-start.5
  79.9 0.0 copy-start.6
  79.9 9.3 %convolution_convert_fusion = bf16[1024,4096]{1,0:T(8,128)(2,1)} fusion(bf16[1024,512]{0,1:T(8,128)(2,1)S(1)} %bitcast.86, bf16[512,4096]{1,0:T(8,128)(2,1)} %param.26), kind=kOutput, calls=%fused_computation.13 | convolution fusion | flops 4299161600 | bytes 13631488 | tf_op jit(solution)/shard_map/dot_general | solution.py:333
  89.2 0.0 reduce-scatter.2.cloned.1.call-update
  89.2 0.0 copy-done.7
  89.3 0.1 copy.46
  89.4 52.4 %reduce-scatter.2.cloned.1.call-done.proj_ref = bf16[128,4096]{1,0:T(8,128)(2,1)} async-done(((bf16[1024,4096]{1,0:T(8,128)(2,1)}), bf16[128,4096]{1,0:T(8,128)(2,1)}) %reduce-scatter.2.cloned.1.call-update) | async-done | bytes 1048592 | tf_op jit(solution)/shard_map/reduce_scatter | solution.py:332
  141.8 0.0 copy-done.2
  141.8 0.0 copy-done.5
  141.8 0.0 copy-done.6
  141.8 0.0 copy-start.3
  141.8 1.2 copy-done.3
  143.0 9.8 %route.1 = (bf16[1024,4608]{1,0:T(8,128)(2,1)}, f32[128,128]{1,0:T(8,128)S(1)}, f32[128,128]{1,0:T(8,128)S(1)}) custom-call(bf16[128,4096]{1,0:T(8,128)(2,1)S(1)} %bitcast.68, bf16[128,4096]{1,0:T(8,128)(2,1)S(1)} %copy-done.3, f32[1,4096]{1,0:T(1,128)S(1)} %bitcast.71, bf16[4096,128]{1,0:T(8,128)(2,1)S(1)} %copy-done.5, s32[128,8]{1,0:T(8,128)S(1)} %bitcast.70), custom_call_target="tpu_custom_call" | custom-call | tf_op jit(solution)/shard_map/route/pallas_call | solution.py:100
  152.8 116.2 %all_to_all.52 = bf16[128,8,4608]{2,1,0:T(8,128)(2,1)} all-to-all(bf16[128,8,4608]{2,1,0:T(8,128)(2,1)} %bitcast.77), channel_id=1, replica_groups=mesh['seq'=8,'exp'=16] {'seq','exp'}, dimensions={0} | all-to-all | bytes 18874368 | tf_op jit(solution)/shard_map/all_to_all | solution.py:345
  269.0 40.3 %expert.1 = bf16[1024,4608]{1,0:T(8,128)(2,1)} custom-call(bf16[1024,4608]{1,0:T(8,128)(2,1)} %bitcast.74, bf16[1024,4608]{1,0:T(8,128)(2,1)} %bitcast.75, bf16[1,4096,768]{2,1,0:T(8,128)(2,1)} %gate_ref.1, bf16[1,4096,768]{2,1,0:T(8,128)(2,1)} %up_ref.1, bf16[1,768,4096]{2,1,0:T(8,128)(2,1)} %down_ref.1), custom_call_target="tpu_custom_call" | custom-call | tf_op jit(solution)/shard_map/expert/pallas_call | solution.py:186
  309.4 0.0 copy-start.4
  309.4 114.9 %all_to_all.53 = bf16[128,8,4608]{2,1,0:T(8,128)(2,1)} all-to-all(bf16[128,8,4608]{2,1,0:T(8,128)(2,1)} %bitcast.76), channel_id=1, replica_groups=mesh['seq'=8,'exp'=16] {'seq','exp'}, dimensions={0} | all-to-all | bytes 18874368 | tf_op jit(solution)/shard_map/all_to_all | solution.py:345
  424.2 0.0 copy-start.1
  424.2 0.0 copy-done.4
  424.2 10.4 %combine.1 = bf16[128,4096]{1,0:T(8,128)(2,1)} custom-call(bf16[1024,4608]{1,0:T(8,128)(2,1)} %bitcast.72, bf16[1024,4608]{1,0:T(8,128)(2,1)} %bitcast.73, f32[128,128]{1,0:T(8,128)S(1)} %get-tuple-element.9.rank_ref, f32[128,128]{1,0:T(8,128)S(1)} %get-tuple-element.10.weight_ref, bf16[128,4096]{1,0:T(8,128)(2,1)S(1)} %bitcast.69, ...), custom_call_target="tpu_custom_call" | custom-call | tf_op jit(solution)/shard_map/combine/pallas_call | solution.py:247
  434.6 0.0 copy-done.1
  (4 shorter events, 0.1 us)
Async XLA Ops:
  6.5 0.8 copy-start
  10.1 11.6 %all-to-all-start = ((bf16[8,64,256]{2,1,0:T(8,128)(2,1)}), bf16[8,64,256]{2,1,0:T(8,128)(2,1)S(1)}, u32[]{:S(2)}, u32[]{:S(2)}) async-start(bf16[8,64,256]{2,1,0:T(8,128)(2,1)} %pad_maximum_fusion.1), calls=%async_computation | async-start | bytes 524288 | tf_op jit(solution)/shard_map/all_to_all | solution.py:306
  21.8 13.9 %all-to-all-start.1 = ((bf16[128,8,256]{2,0,1:T(8,128)(2,1)}), bf16[128,8,256]{2,0,1:T(8,128)(2,1)S(1)}, u32[]{:S(2)}, u32[]{:S(2)}) async-start(bf16[128,8,256]{2,0,1:T(8,128)(2,1)} %pad_maximum_fusion), calls=%async_computation.1 | async-start | bytes 1048576 | tf_op jit(solution)/shard_map/all_to_all | solution.py:301
  35.7 19.5 %all-to-all-start.2 = ((bf16[128,8,512]{0,2,1:T(8,128)(2,1)}), bf16[128,8,512]{0,2,1:T(8,128)(2,1)S(1)}, u32[]{:S(2)}, u32[]{:S(2)}) async-start(bf16[128,8,512]{0,2,1:T(8,128)(2,1)} %bitcast.18), calls=%async_computation.2 | async-start | bytes 2097152 | tf_op jit(solution)/shard_map/all_to_all | solution.py:300
  40.0 101.7 %reduce-scatter.2.cloned.1.call-start = ((), (), s32[]{:S(2)}) async-start(), calls=%async_computation.6 | async-start | bytes 9437184 | tf_op jit(solution)/shard_map/reduce_scatter | solution.py:332
  79.9 9.4 %copy-start.7 = (s32[1,128,8]{1,2,0:T(8,128)S(1)}, s32[1,128,8]{1,2,0:T(8,128)}, u32[]{:S(2)}) copy-start(s32[1,128,8]{1,2,0:T(8,128)} %param.29) | copy-start | bytes 12292
  79.9 61.9 %copy-start.2 = (bf16[1,128,4096]{2,1,0:T(8,128)(2,1)S(1)}, bf16[1,128,4096]{2,1,0:T(8,128)(2,1)}, u32[]{:S(2)}) copy-start(bf16[1,128,4096]{2,1,0:T(8,128)(2,1)} %param.19) | copy-start | bytes 3145732
  79.9 61.9 %copy-start.5 = (bf16[4096,128]{1,0:T(8,128)(2,1)S(1)}, bf16[4096,128]{1,0:T(8,128)(2,1)}, u32[]{:S(2)}) copy-start(bf16[4096,128]{1,0:T(8,128)(2,1)} %router_ref.1) | copy-start | bytes 3145732
  79.9 61.9 %copy-start.6 = (f32[4096]{0:T(1024)S(1)}, f32[4096]{0:T(1024)}, u32[]{:S(2)}) copy-start(f32[4096]{0:T(1024)} %param.27) | copy-start | bytes 49156
  141.8 1.2 copy-start.3
  309.4 114.9 %copy-start.4 = (bf16[128,4096]{1,0:T(8,128)(2,1)S(1)}, bf16[128,4096]{1,0:T(8,128)(2,1)}, u32[]{:S(2)}) copy-start(bf16[128,4096]{1,0:T(8,128)(2,1)} %reduce-scatter.2.cloned.1.call-done.proj_ref) | copy-start | bytes 3145732
  424.2 10.4 %copy-start.1 = (bf16[1,4,64,128]{3,2,1,0:T(8,128)(2,1)S(1)}, bf16[1,4,64,128]{3,2,1,0:T(8,128)(2,1)}, u32[]{:S(2)}) copy-start(bf16[1,4,64,128]{3,2,1,0:T(8,128)(2,1)} %param.24) | copy-start | bytes 196612
Sparse Core Ops, SparseCore 0:
  89.4 52.3 reduce-scatter.1

commit v2 on v1

v2 whole, which is shorter than its diff:
```python
import functools

import jax
import jax.numpy as jnp
import numpy as np
from jax import lax
from jax.experimental import pallas as pl
from jax.experimental.pallas import tpu as pltpu
from jax.sharding import PartitionSpec as P

QUERY_HEAD_HALF = 32
KEY_VALUE_HEADS = 4
HEAD_SIZE = 128
TOP = 8
SLOTS = 8
EXTRA = 512
MIB = 1 << 20


def dot(a, b):
    return jnp.dot(a, b, preferred_element_type=jnp.float32)


def dot_nt(a, b):
    return lax.dot_general(a, b, (((1,), (1,)), ((), ())), preferred_element_type=jnp.float32)


def pack_kernel(query_ref, key_ref, value_ref, key_cache_ref, value_cache_ref, out_ref):
    cached = key_cache_ref.shape[2]
    lanes = query_ref.shape[2]
    out_ref[0, :, :lanes] = query_ref[0]
    out_ref[0, :, lanes : lanes + HEAD_SIZE] = key_ref[0]
    out_ref[0, :, lanes + HEAD_SIZE : lanes + 2 * HEAD_SIZE] = value_ref[0]
    out_ref[0, :cached, lanes + 2 * HEAD_SIZE :] = key_cache_ref[0, 0]
    out_ref[0, cached:, lanes + 2 * HEAD_SIZE :] = value_cache_ref[0, 0]


def pack(queries, keys, values, key_cache, value_cache, seq_count):
    tokens, width = queries.shape[1:]
    cached = key_cache.shape[2]
    assert 2 * cached == tokens
    lanes = width // seq_count
    sharers = seq_count // KEY_VALUE_HEADS
    cache_spec = pl.BlockSpec((1, 1, cached, HEAD_SIZE), lambda s: (0, s // sharers, 0, 0))
    head_spec = pl.BlockSpec((1, tokens, HEAD_SIZE), lambda s: (0, 0, s // sharers))
    return pl.pallas_call(
        pack_kernel,
        grid=(seq_count,),
        in_specs=[
            pl.BlockSpec((1, tokens, lanes), lambda s: (0, 0, s)),
            head_spec,
            head_spec,
            cache_spec,
            cache_spec,
        ],
        out_specs=pl.BlockSpec((1, tokens, lanes + 3 * HEAD_SIZE), lambda s: (s, 0, 0)),
        out_shape=jax.ShapeDtypeStruct(
            (seq_count, tokens, lanes + 3 * HEAD_SIZE), jnp.bfloat16
        ),
        name="pack",
    )(queries, keys, values, key_cache, value_cache)


def attend_kernel(length_ref, packed_ref, out_weight_ref, out_ref, key_ref, value_ref, att_ref):
    step = pl.program_id(0)
    parts, tokens, _ = packed_ref.shape
    lanes = out_weight_ref.shape[0]
    heads = lanes // HEAD_SIZE
    cached = tokens // 2
    prefix = parts * cached
    rows = out_ref.shape[0]
    per_step = rows // tokens
    rate = HEAD_SIZE ** (-0.5) * float(np.log2(np.e))

    @pl.when(step == 0)
    def _():
        for t in range(parts):
            old = pl.ds(t * cached, cached)
            new = pl.ds(prefix + t * tokens, tokens)
            key_ref[old, :] = packed_ref[t, :cached, lanes + 2 * HEAD_SIZE :]
            value_ref[old, :] = packed_ref[t, cached:, lanes + 2 * HEAD_SIZE :]
            key_ref[new, :] = packed_ref[t, :, lanes : lanes + HEAD_SIZE]
            value_ref[new, :] = packed_ref[t, :, lanes + HEAD_SIZE : lanes + 2 * HEAD_SIZE]

    in_prefix = lax.broadcasted_iota(jnp.int32, (rows, prefix), 1) < length_ref[0]
    causal = lax.broadcasted_iota(jnp.int32, (rows, rows), 1) <= lax.broadcasted_iota(
        jnp.int32, (rows, rows), 0
    )

    def block(i):
        spans = [(0, prefix)]
        if i:
            spans.append((prefix, i * rows))
        spans.append((prefix + i * rows, rows))
        for h in range(heads):
            query = jnp.concatenate(
                [
                    packed_ref[i * per_step + t, :, h * HEAD_SIZE : (h + 1) * HEAD_SIZE]
                    for t in range(per_step)
                ],
                axis=0,
            )
            scores = [dot_nt(query, key_ref[pl.ds(start, size), :]) for start, size in spans]
            scores[0] = jnp.where(in_prefix, scores[0], -1e30)
            scores[-1] = jnp.where(causal, scores[-1], -1e30)
            top = functools.reduce(
                jnp.maximum, [jnp.max(s, axis=1, keepdims=True) for s in scores]
            )
            total, result = 0.0, 0.0
            for s, (start, size) in zip(scores, spans, strict=True):
                raised = jnp.exp2((s - top) * rate)
                total = total + jnp.sum(raised, axis=1, keepdims=True)
                result = result + dot(
                    raised.astype(jnp.bfloat16), value_ref[pl.ds(start, size), :]
                )
            att_ref[:, h * HEAD_SIZE : (h + 1) * HEAD_SIZE] = (result / total).astype(
                jnp.bfloat16
            )

    for i in range(parts // per_step):
        pl.when(step == i)(functools.partial(block, i))
    out_ref[...] = dot(att_ref[...], out_weight_ref[...]).astype(jnp.bfloat16)


def attend(length, packed, out_weight, rows=256):
    parts, tokens, columns = packed.shape
    lanes, width = out_weight.shape
    span = parts * tokens
    total = span + parts * tokens // 2
    return pl.pallas_call(
        attend_kernel,
        grid=(span // rows,),
        in_specs=[
            pl.BlockSpec(memory_space=pltpu.SMEM),
            pl.BlockSpec((parts, tokens, columns), lambda i: (0, 0, 0)),
            pl.BlockSpec((lanes, width), lambda i: (0, 0)),
        ],
        out_specs=pl.BlockSpec((rows, width), lambda i: (i, 0)),
        out_shape=jax.ShapeDtypeStruct((span, width), jnp.bfloat16),
        scratch_shapes=[
            pltpu.VMEM((total, HEAD_SIZE), jnp.bfloat16),
            pltpu.VMEM((total, HEAD_SIZE), jnp.bfloat16),
            pltpu.VMEM((rows, lanes), jnp.bfloat16),
        ],
        compiler_params=pltpu.CompilerParams(vmem_limit_bytes=48 * MIB),
        name="attend",
    )(length, packed, out_weight)


def named_mask(ids_ref, experts):
    tokens = ids_ref.shape[0]
    lane = lax.broadcasted_iota(jnp.int32, (tokens, experts), 1)
    named = ids_ref[:, 0:1] == lane
    for k in range(1, TOP):
        named = named | (ids_ref[:, k : k + 1] == lane)
    return named


def flags(condition):
    return jnp.where(condition, 1.0, 0.0).astype(jnp.bfloat16)


def plan_kernel(ids_ref, rank_ref, pick_ref, ninth_ref):
    tokens, experts = rank_ref.shape
    named = named_mask(ids_ref, experts)
    earlier = flags(
        lax.broadcasted_iota(jnp.int32, (tokens, tokens), 0)
        > lax.broadcasted_iota(jnp.int32, (tokens, tokens), 1)
    )
    rank = jnp.where(named, dot(earlier, flags(named)) + 1.0, 0.0)
    rank_ref[...] = rank
    narrow = rank.astype(jnp.bfloat16)
    row = lax.broadcasted_iota(jnp.int32, (experts * SLOTS, experts), 0)
    spread = flags(row // SLOTS == lax.broadcasted_iota(jnp.int32, row.shape, 1))
    slot = (lax.broadcasted_iota(jnp.int32, (experts * SLOTS, tokens), 0) % SLOTS).astype(
        jnp.float32
    )
    pick_ref[...] = flags(dot_nt(spread, narrow) == slot + 1.0)
    same = flags(
        lax.broadcasted_iota(jnp.int32, (experts, experts), 0)
        == lax.broadcasted_iota(jnp.int32, (experts, experts), 1)
    )
    ninth_ref[...] = flags(dot_nt(same, narrow) == SLOTS + 1.0)


def plan(ids, experts):
    tokens = ids.shape[0]
    return pl.pallas_call(
        plan_kernel,
        out_shape=[
            jax.ShapeDtypeStruct((tokens, experts), jnp.float32),
            jax.ShapeDtypeStruct((experts * SLOTS, tokens), jnp.bfloat16),
            jax.ShapeDtypeStruct((experts, tokens), jnp.bfloat16),
        ],
        name="plan",
    )(ids)


def route_kernel(
    resid_ref, proj_ref, gain_ref, pick_ref, ninth_ref, send_ref, normed_ref, extra_ref
):
    step = pl.program_id(0)
    cols = send_ref.shape[1]
    blocks = resid_ref.shape[1] // cols
    experts = ninth_ref.shape[0]

    @pl.when(step == 0)
    def _():
        hidden = resid_ref[...].astype(jnp.float32) + proj_ref[...].astype(jnp.float32)
        mean_square = jnp.mean(hidden * hidden, axis=1, keepdims=True)
        normed_ref[...] = (
            hidden * lax.rsqrt(mean_square + 1e-06) * gain_ref[...]
        ).astype(jnp.bfloat16)

    for j in range(blocks):

        @pl.when(step == j)
        def _():
            part = normed_ref[:, j * cols : (j + 1) * cols]
            send_ref[...] = dot(pick_ref[...], part).astype(jnp.bfloat16)
            ninth = dot(ninth_ref[...], part)
            for a in range(cols // EXTRA):
                piece = j * (cols // EXTRA) + a
                for b in range(EXTRA // 128):
                    extra_ref[b, pl.ds(piece, experts, stride=SLOTS), :] = ninth[
                        :, a * EXTRA + b * 128 : a * EXTRA + (b + 1) * 128
                    ]

    @pl.when(step == blocks)
    def _():
        for b in range(EXTRA // 128):
            send_ref[:, b * 128 : (b + 1) * 128] = extra_ref[b].astype(jnp.bfloat16)


def route(resid, projected, gain, pick, ninth):
    tokens, width = resid.shape
    experts = ninth.shape[0]
    cols = width // SLOTS
    whole = lambda shape: pl.BlockSpec(shape, lambda j: (0, 0))
    return pl.pallas_call(
        route_kernel,
        grid=(SLOTS + 1,),
        in_specs=[
            whole((tokens, width)),
            whole((tokens, width)),
            whole((1, width)),
            whole(pick.shape),
            whole(ninth.shape),
        ],
        out_specs=[
            pl.BlockSpec((experts * SLOTS, cols), lambda j: (0, j)),
            whole((tokens, width)),
        ],
        out_shape=[
            jax.ShapeDtypeStruct((experts * SLOTS, width + cols), jnp.bfloat16),
            jax.ShapeDtypeStruct((tokens, width), jnp.bfloat16),
        ],
        scratch_shapes=[pltpu.VMEM((EXTRA // 128, experts * SLOTS, 128), jnp.float32)],
        compiler_params=pltpu.CompilerParams(vmem_limit_bytes=48 * MIB),
        name="route",
    )(resid, projected, gain, pick, ninth)


def weights_kernel(normed_ref, router_ref, rank_ref, main_ref, ninth_ref):
    tokens, experts = rank_ref.shape
    rank = rank_ref[...]
    named = rank > 0.0
    logits = dot(normed_ref[...], router_ref[...])
    top = jnp.max(jnp.where(named, logits, -jnp.inf), axis=1, keepdims=True)
    raised = jnp.where(named, jnp.exp(jnp.where(named, logits, top) - top), 0.0)
    weight = raised / jnp.sum(raised, axis=1, keepdims=True)
    high = weight.astype(jnp.bfloat16)
    low = (weight - high.astype(jnp.float32)).astype(jnp.bfloat16)
    column = lax.broadcasted_iota(jnp.int32, (experts, experts * SLOTS), 1)
    spread = flags(column // SLOTS == lax.broadcasted_iota(jnp.int32, column.shape, 0))
    wide_rank = dot(rank.astype(jnp.bfloat16), spread)
    slot = (lax.broadcasted_iota(jnp.int32, wide_rank.shape, 1) % SLOTS).astype(jnp.float32)
    for half, part in enumerate((high, low)):
        rows = pl.ds(half * tokens, tokens)
        main_ref[rows, :] = jnp.where(wide_rank == slot + 1.0, dot(part, spread), 0.0).astype(
            jnp.bfloat16
        )
        ninth_ref[rows, :] = jnp.where(
            rank == SLOTS + 1.0, part.astype(jnp.float32), 0.0
        ).astype(jnp.bfloat16)


def weights(normed, router, rank):
    tokens, experts = rank.shape
    return pl.pallas_call(
        weights_kernel,
        out_shape=[
            jax.ShapeDtypeStruct((2 * tokens, experts * SLOTS), jnp.bfloat16),
            jax.ShapeDtypeStruct((2 * tokens, experts), jnp.bfloat16),
        ],
        compiler_params=pltpu.CompilerParams(vmem_limit_bytes=32 * MIB),
        name="weights",
    )(normed, router, rank)


def expert_kernel(
    rows_ref, extra_ref, gate_ref, up_ref, *refs, deep, wide
):
    down_refs, (out_ref, ninth_ref, gate_acc, up_acc, act_ref, piece_ref) = (
        refs[:wide],
        refs[wide:],
    )
    step = pl.program_id(0)
    main, cols = rows_ref.shape
    sources = main // SLOTS

    @pl.when(step == 0)
    def _():
        for b in range(EXTRA // 128):
            piece_ref[b] = extra_ref[:, b * 128 : (b + 1) * 128].astype(jnp.float32)
        for j in range(SLOTS):
            for b in range(EXTRA // 128):
                lane = (j * EXTRA + b * 128) % cols
                ninth_ref[(j * EXTRA) // cols, :, lane : lane + 128] = piece_ref[
                    b, pl.ds(j, sources, stride=SLOTS), :
                ].astype(jnp.bfloat16)

    @pl.when(step < deep)
    def _():
        ninth = ninth_ref[jnp.minimum(step, deep - 1)]
        rows = jnp.concatenate([rows_ref[...], ninth], axis=0)

        @pl.when(step == 0)
        def _():
            gate_acc[...] = dot(rows, gate_ref[0])
            up_acc[...] = dot(rows, up_ref[0])

        @pl.when(step > 0)
        def _():
            gate_acc[...] += dot(rows, gate_ref[0])
            up_acc[...] += dot(rows, up_ref[0])

    @pl.when(step == deep - 1)
    def _():
        gate_val = gate_acc[...]
        act_ref[...] = (gate_val / (1.0 + jnp.exp(-gate_val)) * up_acc[...]).astype(jnp.bfloat16)

    last = (SLOTS + 1) // wide
    for s in range(last):

        @pl.when(step == deep + s)
        def _():
            for a in range(wide):
                j = s * wide + a
                lanes = slice(a * EXTRA, (a + 1) * EXTRA)
                if j < SLOTS:
                    result = dot(act_ref[...], down_refs[a][0])
                    out_ref[:, lanes] = result[:main].astype(jnp.bfloat16)
                    for b in range(EXTRA // 128):
                        piece_ref[b, pl.ds(j, sources, stride=SLOTS), :] = result[
                            main:, b * 128 : (b + 1) * 128
                        ]
                else:
                    for b in range(EXTRA // 128):
                        out_ref[:, a * EXTRA + b * 128 : a * EXTRA + (b + 1) * 128] = piece_ref[
                            b
                        ].astype(jnp.bfloat16)


def expert(rows, w_gate, w_up, w_down, deep=4, wide=3):
    main = rows.shape[0]
    _, width, hidden = w_gate.shape
    cols = width // deep
    tall = main + main // SLOTS
    last = (SLOTS + 1) // wide
    first = lambda s: jnp.minimum(s, deep - 1)

    def down_spec(a):
        return pl.BlockSpec(
            (1, hidden, EXTRA),
            lambda s: (0, 0, jnp.minimum(jnp.clip(s - deep, 0, last - 1) * wide + a, SLOTS - 1)),
        )

    return pl.pallas_call(
        functools.partial(expert_kernel, deep=deep, wide=wide),
        grid=(deep + last,),
        in_specs=[
            pl.BlockSpec((main, cols), lambda s: (0, first(s))),
            pl.BlockSpec((main, EXTRA), lambda s: (0, SLOTS)),
            pl.BlockSpec((1, cols, hidden), lambda s: (0, first(s), 0)),
            pl.BlockSpec((1, cols, hidden), lambda s: (0, first(s), 0)),
            *[down_spec(a) for a in range(wide)],
        ],
        out_specs=pl.BlockSpec((main, wide * EXTRA), lambda s: (0, jnp.clip(s - deep, 0, last - 1))),
        out_shape=jax.ShapeDtypeStruct(rows.shape, jnp.bfloat16),
        scratch_shapes=[
            pltpu.VMEM((deep, main // SLOTS, cols), jnp.bfloat16),
            pltpu.VMEM((tall, hidden), jnp.float32),
            pltpu.VMEM((tall, hidden), jnp.float32),
            pltpu.VMEM((tall, hidden), jnp.bfloat16),
            pltpu.VMEM((EXTRA // 128, main, 128), jnp.float32),
        ],
        compiler_params=pltpu.CompilerParams(vmem_limit_bytes=56 * MIB),
        name="expert",
    )(rows, rows, w_gate, w_up, *[w_down] * wide)


def combine_kernel(
    rows_ref, extra_ref, main_ref, ninth_ref, resid_ref, proj_ref, out_ref, piece_ref, row_ref
):
    step = pl.program_id(0)
    tokens = resid_ref.shape[0]
    sources = rows_ref.shape[0] // SLOTS

    @pl.when(step == 0)
    def _():
        for b in range(EXTRA // 128):
            piece_ref[b] = extra_ref[:, b * 128 : (b + 1) * 128].astype(jnp.float32)
        for j in range(SLOTS):
            for b in range(EXTRA // 128):
                row_ref[j, :, b * 128 : (b + 1) * 128] = piece_ref[
                    b, pl.ds(j, sources, stride=SLOTS), :
                ].astype(jnp.bfloat16)

    both = dot(main_ref[...], rows_ref[...]) + dot(ninth_ref[...], row_ref[step])
    hidden = resid_ref[...].astype(jnp.float32) + proj_ref[...].astype(jnp.float32)
    out_ref[...] = (hidden + (both[:tokens] + both[tokens:])).astype(jnp.bfloat16)


def combine(rows, main_weight, ninth_weight, resid, projected):
    tokens, width = resid.shape
    main = rows.shape[0]
    cols = width // SLOTS
    whole = lambda shape: pl.BlockSpec(shape, lambda j: (0, 0))
    part = pl.BlockSpec((tokens, cols), lambda j: (0, j))
    return pl.pallas_call(
        combine_kernel,
        grid=(SLOTS,),
        in_specs=[
            pl.BlockSpec((main, cols), lambda j: (0, j)),
            pl.BlockSpec((main, cols), lambda j: (0, SLOTS)),
            whole(main_weight.shape),
            whole(ninth_weight.shape),
            part,
            part,
        ],
        out_specs=part,
        out_shape=jax.ShapeDtypeStruct((tokens, width), jnp.bfloat16),
        scratch_shapes=[
            pltpu.VMEM((EXTRA // 128, main, 128), jnp.float32),
            pltpu.VMEM((SLOTS, main // SLOTS, cols), jnp.bfloat16),
        ],
        compiler_params=pltpu.CompilerParams(vmem_limit_bytes=48 * MIB),
        name="combine",
    )(rows, rows, main_weight, ninth_weight, resid, projected)


def per_device(
    resid,
    queries,
    span_rotated_keys,
    span_value_rows,
    key_cache,
    prefix_value_cache,
    prefix_len,
    out_weight,
    norm_gain,
    router_weight,
    expert_ids,
    w_gate,
    w_up,
    w_down,
):
    seq_count = lax.axis_size("seq")
    width = resid.shape[2]
    experts = router_weight.shape[1]
    packed = pack(
        queries, span_rotated_keys, span_value_rows, key_cache, prefix_value_cache, seq_count
    )
    packed = lax.all_to_all(packed, "seq", split_axis=0, concat_axis=0, tiled=True)
    projected = lax.psum_scatter(
        attend(prefix_len, packed, out_weight), "seq", scatter_dimension=0, tiled=True
    )
    rank, pick, ninth = plan(expert_ids[0], experts)
    send, normed = route(resid[0], projected, norm_gain.reshape(1, width), pick, ninth)

    def exchange(rows):
        blocks = rows.reshape(experts, SLOTS, rows.shape[1])
        return lax.all_to_all(
            blocks, ("seq", "exp"), split_axis=0, concat_axis=0, tiled=True
        ).reshape(rows.shape)

    received = exchange(send)
    main_weight, ninth_weight = weights(normed, router_weight, rank)
    returned = exchange(expert(received, w_gate, w_up, w_down))
    return combine(returned, main_weight, ninth_weight, resid[0], projected)[None]


def solution(mesh):
    in_specs = (
        P("exp", "seq", None),
        P("exp", "seq", None),
        P("exp", "seq", None),
        P("exp", "seq", None),
        P("exp", None, "seq", None),
        P("exp", None, "seq", None),
        P("exp"),
        P("seq", None),
        P(),
        P(),
        P("exp", "seq", None),
        P(("seq", "exp"), None, None),
        P(("seq", "exp"), None, None),
        P(("seq", "exp"), None, None),
    )
    out_specs = P("exp", "seq", None)
    return jax.shard_map(
        per_device, mesh=mesh, in_specs=in_specs, out_specs=out_specs, check_vma=False
    )
```

time: 445 us -> 423 us (0.951)
  waiting for transfers between devices: 73.2 us -> 196 us
  blocking collectives: 231 us -> 116 us
  matrix products: 32.8 us -> 0 us
  Pallas kernels: 60.5 us -> 73.5 us
  other arithmetic: 5.19 us -> 0 us
    all_to_all x3 -> x2, waiting for transfers between devices: 20.8 us -> 147 us  [the longest x1 124 us: exchange(): lax.all_to_all(blocks, ('seq', 'exp'), split_axis=0, concat_axis=0, tiled...]
    all_to_all x2 -> x1, blocking collectives: 231 us -> 116 us  [exchange(): lax.all_to_all(blocks, ('seq', 'exp'), split_axis=0, concat_axis=0, tiled...]
    dot_general x2 -> x0, matrix products: 22.6 us -> none  [the longest x1 13.3 us: per_device(): jnp.einsum('htj,jd->thd', attn_weights, all_values, preferred_element_typ...]
    pallas_call x1 -> x5, Pallas kernels: 40.3 us -> 56 us  [the longest x1 31.8 us: expert(): pl.pallas_call(functools.partial(expert_kernel, deep=deep, wide=wide), gr...]
    sub x1 -> x0, matrix products: 10.2 us -> none  [per_device(): raised = jnp.exp(scores - top_score)]
    unnamed x20 -> x29, local copies, waits for them, and re-layouts: 5.82 us -> 9.57 us
    all_to_all x3 -> x2, starting transfers between devices: 13.9 us -> 12.5 us  [the longest x1 7.35 us: exchange(): lax.all_to_all(blocks, ('seq', 'exp'), split_axis=0, concat_axis=0, tiled...]
  transfers between devices with their start and end apart: 4 -> 3, of which waited for: 4 -> 3; matrix products, arithmetic and copies ran while one was open for 2% -> 0% of each run, Pallas kernels for 0% -> 1%
where the time goes in v2:
time: 423 us; the launch traced here: 422 us
  waiting for transfers between devices  196 us (46%)
  blocking collectives  116 us (27%)
  Pallas kernels  73.5 us (17%)
  between operations  14.1 us (3%)
  starting transfers between devices  12.5 us (3%)
  local copies, waits for them, and re-layouts  9.57 us (2%)
    all_to_all x1, waiting for transfers between devices, exchange(): lax.all_to_all(blocks, ('seq', 'exp'), split_axis=0, concat_axis=0, tiled...  124 us
    all_to_all x1, blocking collectives, exchange(): lax.all_to_all(blocks, ('seq', 'exp'), split_axis=0, concat_axis=0, tiled...  116 us
    reduce_scatter x1, waiting for transfers between devices, per_device(): lax.psum_scatter(attend(prefix_len, packed, out_weight), 'seq', scatter_d...  49 us
    pallas_call x1, Pallas kernels, expert(): pl.pallas_call(functools.partial(expert_kernel, deep=deep, wide=wide), gr...  31.8 us
    all_to_all x1, waiting for transfers between devices, per_device(): lax.all_to_all(packed, 'seq', split_axis=0, concat_axis=0, tiled=True)  22.9 us
    pallas_call x1, Pallas kernels, attend(): pl.pallas_call(attend_kernel, grid=(span // rows,), in_specs=[pl.BlockSpe...  15.6 us
    unnamed x29, local copies, waits for them, and re-layouts  9.57 us
    pallas_call x1, Pallas kernels, combine(): pl.pallas_call(combine_kernel, grid=(SLOTS,), in_specs=[pl.BlockSpec((mai...  9.48 us
  transfers between devices with their start and end apart: 3, of which 3 were waited for; matrix products, arithmetic and copies ran while one was open for 0% of the time, Pallas kernels for 1%

profile of v2, /device:TPU:5, one launch (start us, length us, event | category | flops | bytes accessed | tf_op | source)
XLA Modules:
  0.0 422.2 jit_solution(16045897097492611808)
XLA Ops:
  6.5 5.6 %pack.1 = bf16[8,128,896]{2,1,0:T(8,128)(2,1)} custom-call(bf16[1,128,4096]{2,1,0:T(8,128)(2,1)} %query_ref.1, bf16[1,128,512]{2,1,0:T(8,128)(2,1)} %key_ref.1, bf16[1,128,512]{2,1,0:T(8,128)(2,1)} %value_ref.1, bf16[1,4,64,128]{3,2,1,0:T(8,128)(2,1)} %key_cache_ref.1, bf16[1,4,64,128]{3,2,1,0:T(8,128)(2,1)} %value_cache_ref.1), custom_call_target="tpu_custom_call" | custom-call | tf_op jit(solution)/shard_map/pack/pallas_call | solution.py:46
  12.1 5.1 %all-to-all-start = ((bf16[8,128,896]{2,1,0:T(8,128)(2,1)}), bf16[8,128,896]{2,1,0:T(8,128)(2,1)S(1)}, u32[]{:S(2)}, u32[]{:S(2)}) async-start(bf16[8,128,896]{2,1,0:T(8,128)(2,1)} %pack.1), calls=%async_computation | async-start | bytes 3670016 | tf_op jit(solution)/shard_map/all_to_all | solution.py:475
  17.2 0.0 reduce-scatter.2.cloned.1.call-start
  17.9 22.9 %all-to-all-done.packed_ref = bf16[8,128,896]{2,1,0:T(8,128)(2,1)S(1)} async-done(((bf16[8,128,896]{2,1,0:T(8,128)(2,1)}), bf16[8,128,896]{2,1,0:T(8,128)(2,1)S(1)}, u32[]{:S(2)}, u32[]{:S(2)}) %all-to-all-start) | async-done | bytes 1835040 | tf_op jit(solution)/shard_map/all_to_all | solution.py:475
  40.8 0.0 copy-start.3
  40.8 2.2 copy-done.3
  42.9 15.6 %attend.1 = bf16[1024,4096]{1,0:T(8,128)(2,1)} custom-call(s32[1]{0:T(128)S(6)} %copy.16.length_ref, bf16[8,128,896]{2,1,0:T(8,128)(2,1)S(1)} %all-to-all-done.packed_ref, bf16[512,4096]{1,0:T(8,128)(2,1)S(1)} %copy-done.3), custom_call_target="tpu_custom_call" | custom-call | tf_op jit(solution)/shard_map/attend/pallas_call | solution.py:130
  58.5 0.0 copy-start.13
  58.5 0.0 copy-start
  58.5 0.0 copy-start.12
  58.5 0.0 reduce-scatter.2.cloned.1.call-update
  58.5 0.7 copy-done.13
  59.2 0.7 copy.15
  59.9 2.2 plan.1
  62.1 49.0 %reduce-scatter.2.cloned.1.call-done.proj_ref = bf16[128,4096]{1,0:T(8,128)(2,1)} async-done(((bf16[1024,4096]{1,0:T(8,128)(2,1)}), bf16[128,4096]{1,0:T(8,128)(2,1)}) %reduce-scatter.2.cloned.1.call-update) | async-done | bytes 1048592 | tf_op jit(solution)/shard_map/reduce_scatter | solution.py:476
  111.1 0.0 copy-done
  111.1 0.0 copy-done.12
  111.1 0.0 copy-start.1
  111.1 1.2 copy-done.1
  112.3 0.0 copy-start.9
  112.3 0.9 copy-done.9
  113.3 0.0 copy-start.11
  113.3 0.8 copy-done.11
  114.0 8.0 %route.1 = (bf16[1024,4608]{1,0:T(8,128)(2,1)}, bf16[128,4096]{1,0:T(8,128)(2,1)S(1)}) custom-call(bf16[128,4096]{1,0:T(8,128)(2,1)S(1)} %bitcast.8, bf16[128,4096]{1,0:T(8,128)(2,1)S(1)} %copy-done.1, f32[1,4096]{1,0:T(1,128)S(1)} %bitcast.10, bf16[1024,128]{1,0:T(8,128)(2,1)S(1)} %copy-done.9, bf16[128,128]{1,0:T(8,128)(2,1)S(1)} %copy-done.11), custom_call_target="tpu_custom_call" | custom-call | tf_op jit(solution)/shard_map/route/pallas_call | solution.py:240
  122.1 0.0 copy-start.5
  122.1 116.2 %all_to_all.15 = bf16[128,8,4608]{2,1,0:T(8,128)(2,1)} all-to-all(bf16[128,8,4608]{2,1,0:T(8,128)(2,1)} %bitcast.14), channel_id=1, replica_groups=mesh['seq'=8,'exp'=16] {'seq','exp'}, dimensions={0} | all-to-all | bytes 18874368 | tf_op jit(solution)/shard_map/all_to_all | solution.py:484
  238.3 0.0 copy-done.5
  238.3 31.8 %expert.1 = bf16[1024,4608]{1,0:T(8,128)(2,1)} custom-call(bf16[1024,4608]{1,0:T(8,128)(2,1)} %bitcast.11, bf16[1024,4608]{1,0:T(8,128)(2,1)} %bitcast.12, bf16[1,4096,768]{2,1,0:T(8,128)(2,1)} %gate_ref.1, bf16[1,4096,768]{2,1,0:T(8,128)(2,1)} %up_ref.1, bf16[1,768,4096]{2,1,0:T(8,128)(2,1)} %refs_2_.1, bf16[1,768,4096]{2,1,0:T(8,128)(2,1)} %refs_2_.1, ...), custom_call_target="tpu_custom_call" | custom-call | tf_op jit(solution)/shard_map/expert/pallas_call | solution.py:379
  270.1 0.0 copy-start.4
  270.1 0.0 copy-start.10
  270.1 0.0 copy-start.2
  270.1 7.4 %all-to-all-start.2 = ((bf16[128,8,4608]{2,1,0:T(8,128)(2,1)}), bf16[128,8,4608]{2,1,0:T(8,128)(2,1)}, u32[]{:S(2)}, u32[]{:S(2)}) async-start(bf16[128,8,4608]{2,1,0:T(8,128)(2,1)} %bitcast.13), calls=%async_computation.3 | async-start | bytes 18874368 | tf_op jit(solution)/shard_map/all_to_all | solution.py:484
  277.5 0.0 copy-done.4
  277.5 0.0 copy-done.10
  277.5 0.0 copy-start.6
  277.5 1.2 copy-done.6
  278.7 0.9 weights.1
  279.6 0.0 copy-start.7
  279.6 0.8 copy-done.7
  280.4 124.5 %all-to-all-done.2 = bf16[128,8,4608]{2,1,0:T(8,128)(2,1)} async-done(((bf16[128,8,4608]{2,1,0:T(8,128)(2,1)}), bf16[128,8,4608]{2,1,0:T(8,128)(2,1)}, u32[]{:S(2)}, u32[]{:S(2)}) %all-to-all-start.2) | async-done | bytes 9437216 | tf_op jit(solution)/shard_map/all_to_all | solution.py:484
  404.9 0.0 copy-done.2
  404.9 0.0 copy-start.8
  404.9 1.0 copy-done.8
  405.9 9.5 %combine.1 = bf16[128,4096]{1,0:T(8,128)(2,1)} custom-call(bf16[1024,4608]{1,0:T(8,128)(2,1)} %bitcast.6.rows_ref.extra_ref, bf16[1024,4608]{1,0:T(8,128)(2,1)} %bitcast.6.rows_ref.extra_ref, bf16[256,1024]{1,0:T(8,128)(2,1)S(1)} %copy-done.8, bf16[256,128]{1,0:T(8,128)(2,1)S(1)} %get-tuple-element.18.ninth_ref, bf16[128,4096]{1,0:T(8,128)(2,1)S(1)} %bitcast.9, ...), custom_call_target="tpu_custom_call" | custom-call | tf_op jit(solution)/shard_map/combine/pallas_call | solution.py:431
Async XLA Ops:
  12.1 28.7 %all-to-all-start = ((bf16[8,128,896]{2,1,0:T(8,128)(2,1)}), bf16[8,128,896]{2,1,0:T(8,128)(2,1)S(1)}, u32[]{:S(2)}, u32[]{:S(2)}) async-start(bf16[8,128,896]{2,1,0:T(8,128)(2,1)} %pack.1), calls=%async_computation | async-start | bytes 3670016 | tf_op jit(solution)/shard_map/all_to_all | solution.py:475
  17.2 93.9 %reduce-scatter.2.cloned.1.call-start = ((), (), s32[]{:S(2)}) async-start(), calls=%async_computation.4 | async-start | bytes 9437184 | tf_op jit(solution)/shard_map/reduce_scatter | solution.py:476
  40.8 2.2 copy-start.3
  58.5 0.7 copy-start.13
  58.5 52.6 %copy-start = (bf16[1,128,4096]{2,1,0:T(8,128)(2,1)S(1)}, bf16[1,128,4096]{2,1,0:T(8,128)(2,1)}, u32[]{:S(2)}) copy-start(bf16[1,128,4096]{2,1,0:T(8,128)(2,1)} %param.14) | copy-start | bytes 3145732
  58.5 52.6 %copy-start.12 = (f32[4096]{0:T(1024)S(1)}, f32[4096]{0:T(1024)}, u32[]{:S(2)}) copy-start(f32[4096]{0:T(1024)} %param.22) | copy-start | bytes 49156
  111.1 1.2 copy-start.1
  112.3 0.9 copy-start.9
  113.3 0.8 copy-start.11
  122.1 116.2 %copy-start.5 = (bf16[128,4096]{1,0:T(8,128)(2,1)}, bf16[128,4096]{1,0:T(8,128)(2,1)S(1)}, u32[]{:S(2)}) copy-start(bf16[128,4096]{1,0:T(8,128)(2,1)S(1)} %get-tuple-element.15.normed_ref) | copy-start | bytes 3145732
  270.1 7.4 %copy-start.4 = (bf16[4096,128]{1,0:T(8,128)(2,1)S(1)}, bf16[4096,128]{1,0:T(8,128)(2,1)}, u32[]{:S(2)}) copy-start(bf16[4096,128]{1,0:T(8,128)(2,1)} %router_ref.1) | copy-start | bytes 3145732
  270.1 7.4 %copy-start.10 = (f32[128,128]{1,0:T(8,128)S(1)}, f32[128,128]{1,0:T(8,128)}, u32[]{:S(2)}) copy-start(f32[128,128]{1,0:T(8,128)} %get-tuple-element.16.rank_ref) | copy-start | bytes 196612
  270.1 134.8 %copy-start.2 = (bf16[128,4096]{1,0:T(8,128)(2,1)S(1)}, bf16[128,4096]{1,0:T(8,128)(2,1)}, u32[]{:S(2)}) copy-start(bf16[128,4096]{1,0:T(8,128)(2,1)} %reduce-scatter.2.cloned.1.call-done.proj_ref) | copy-start | bytes 3145732
  270.1 134.8 %all-to-all-start.2 = ((bf16[128,8,4608]{2,1,0:T(8,128)(2,1)}), bf16[128,8,4608]{2,1,0:T(8,128)(2,1)}, u32[]{:S(2)}, u32[]{:S(2)}) async-start(bf16[128,8,4608]{2,1,0:T(8,128)(2,1)} %bitcast.13), calls=%async_computation.3 | async-start | bytes 18874368 | tf_op jit(solution)/shard_map/all_to_all | solution.py:484
  277.5 1.2 copy-start.6
  279.6 0.8 copy-start.7
  404.9 1.0 copy-start.8
Sparse Core Ops, SparseCore 0:
  58.7 52.3 reduce-scatter.1

commit v3 on v2

v3 whole, which is shorter than its diff:
```python
import functools

import jax
import jax.numpy as jnp
import numpy as np
from jax import lax
from jax.experimental import pallas as pl
from jax.experimental.pallas import tpu as pltpu
from jax.sharding import PartitionSpec as P

QUERY_HEAD_HALF = 32
KEY_VALUE_HEADS = 4
HEAD_SIZE = 128
TOP = 8
SLOTS = 8
HALF = SLOTS // 2
GROUP = 256
MIB = 1 << 20


def dot(a, b):
    return jnp.dot(a, b, preferred_element_type=jnp.float32)


def in_hbm(x):
    return pltpu.with_memory_space_constraint(x, pltpu.HBM)


def dot_nt(a, b):
    return lax.dot_general(a, b, (((1,), (1,)), ((), ())), preferred_element_type=jnp.float32)


def pack_kernel(query_ref, key_ref, value_ref, key_cache_ref, value_cache_ref, out_ref, sems):
    parts = out_ref.shape[0]
    cached, tokens = key_cache_ref.shape[2], query_ref.shape[1]
    lanes = query_ref.shape[2] // parts
    ends = [lanes + i * HEAD_SIZE for i in range(4)]
    copies = []
    for s in range(parts):
        head = s * KEY_VALUE_HEADS // parts
        heads = pl.ds(head * HEAD_SIZE, HEAD_SIZE)
        moves = [
            (query_ref.at[0, :, pl.ds(s * lanes, lanes)], out_ref.at[s, :, pl.ds(0, lanes)]),
            (key_ref.at[0, :, heads], out_ref.at[s, :, pl.ds(ends[0], HEAD_SIZE)]),
            (value_ref.at[0, :, heads], out_ref.at[s, :, pl.ds(ends[1], HEAD_SIZE)]),
            (
                key_cache_ref.at[0, head],
                out_ref.at[s, pl.ds(0, cached), pl.ds(ends[2], HEAD_SIZE)],
            ),
            (
                value_cache_ref.at[0, head],
                out_ref.at[s, pl.ds(cached, tokens - cached), pl.ds(ends[2], HEAD_SIZE)],
            ),
        ]
        for i, (source, target) in enumerate(moves):
            copies.append(pltpu.make_async_copy(source, target, sems.at[s, i]))
    for copy in copies:
        copy.start()
    for copy in copies:
        copy.wait()


def pack(queries, keys, values, key_cache, value_cache, seq_count):
    tokens, width = queries.shape[1:]
    cached = key_cache.shape[2]
    assert 2 * cached == tokens
    lanes = width // seq_count
    return pl.pallas_call(
        pack_kernel,
        in_specs=[pl.BlockSpec(memory_space=pltpu.HBM)] * 5,
        out_specs=pl.BlockSpec(memory_space=pltpu.HBM),
        out_shape=jax.ShapeDtypeStruct(
            (seq_count, tokens, lanes + 3 * HEAD_SIZE), jnp.bfloat16
        ),
        scratch_shapes=[pltpu.SemaphoreType.DMA((seq_count, 5))],
        name="pack",
    )(queries, keys, values, key_cache, value_cache)


def attend_kernel(
    length_ref, packed_ref, out_weight_hbm, out_ref,
    key_ref, value_ref, att_ref, out_weight_ref, sem,
):
    step = pl.program_id(0)
    parts, tokens, _ = packed_ref.shape
    lanes = out_weight_ref.shape[0]
    heads = lanes // HEAD_SIZE
    cached = tokens // 2
    prefix = parts * cached
    rows = out_ref.shape[0]
    per_step = rows // tokens
    rate = HEAD_SIZE ** (-0.5) * float(np.log2(np.e))
    fetch = pltpu.make_async_copy(out_weight_hbm, out_weight_ref, sem)

    @pl.when(step == 0)
    def _():
        fetch.start()
        for t in range(parts):
            old = pl.ds(t * cached, cached)
            new = pl.ds(prefix + t * tokens, tokens)
            key_ref[old, :] = packed_ref[t, :cached, lanes + 2 * HEAD_SIZE :]
            value_ref[old, :] = packed_ref[t, cached:, lanes + 2 * HEAD_SIZE :]
            key_ref[new, :] = packed_ref[t, :, lanes : lanes + HEAD_SIZE]
            value_ref[new, :] = packed_ref[t, :, lanes + HEAD_SIZE : lanes + 2 * HEAD_SIZE]

    in_prefix = lax.broadcasted_iota(jnp.int32, (rows, prefix), 1) < length_ref[0]
    causal = lax.broadcasted_iota(jnp.int32, (rows, rows), 1) <= lax.broadcasted_iota(
        jnp.int32, (rows, rows), 0
    )

    def block(i):
        spans = [(0, prefix)]
        if i:
            spans.append((prefix, i * rows))
        spans.append((prefix + i * rows, rows))
        for h in range(heads):
            query = jnp.concatenate(
                [
                    packed_ref[i * per_step + t, :, h * HEAD_SIZE : (h + 1) * HEAD_SIZE]
                    for t in range(per_step)
                ],
                axis=0,
            )
            scores = [dot_nt(query, key_ref[pl.ds(start, size), :]) for start, size in spans]
            scores[0] = jnp.where(in_prefix, scores[0], -1e30)
            scores[-1] = jnp.where(causal, scores[-1], -1e30)
            top = functools.reduce(
                jnp.maximum, [jnp.max(s, axis=1, keepdims=True) for s in scores]
            )
            total, result = 0.0, 0.0
            for s, (start, size) in zip(scores, spans, strict=True):
                raised = jnp.exp2((s - top) * rate)
                total = total + jnp.sum(raised, axis=1, keepdims=True)
                result = result + dot(
                    raised.astype(jnp.bfloat16), value_ref[pl.ds(start, size), :]
                )
            att_ref[:, h * HEAD_SIZE : (h + 1) * HEAD_SIZE] = (result / total).astype(
                jnp.bfloat16
            )

    for i in range(parts // per_step):
        pl.when(step == i)(functools.partial(block, i))
    pl.when(step == 0)(fetch.wait)
    out_ref[...] = dot(att_ref[...], out_weight_ref[...]).astype(jnp.bfloat16)


def attend(length, packed, out_weight, rows=256):
    parts, tokens, columns = packed.shape
    lanes, width = out_weight.shape
    span = parts * tokens
    total = span + parts * tokens // 2
    return pl.pallas_call(
        attend_kernel,
        grid=(span // rows,),
        in_specs=[
            pl.BlockSpec(memory_space=pltpu.SMEM),
            pl.BlockSpec((parts, tokens, columns), lambda i: (0, 0, 0)),
            pl.BlockSpec(memory_space=pltpu.HBM),
        ],
        out_specs=pl.BlockSpec((rows, width), lambda i: (i, 0)),
        out_shape=jax.ShapeDtypeStruct((span, width), jnp.bfloat16),
        scratch_shapes=[
            pltpu.VMEM((total, HEAD_SIZE), jnp.bfloat16),
            pltpu.VMEM((total, HEAD_SIZE), jnp.bfloat16),
            pltpu.VMEM((rows, lanes), jnp.bfloat16),
            pltpu.VMEM((lanes, width), jnp.bfloat16),
            pltpu.SemaphoreType.DMA,
        ],
        compiler_params=pltpu.CompilerParams(vmem_limit_bytes=48 * MIB),
        name="attend",
    )(length, packed, out_weight)


def named_mask(ids_ref, experts):
    tokens = ids_ref.shape[0]
    lane = lax.broadcasted_iota(jnp.int32, (tokens, experts), 1)
    named = ids_ref[:, 0:1] == lane
    for k in range(1, TOP):
        named = named | (ids_ref[:, k : k + 1] == lane)
    return named


def flags(condition):
    return jnp.where(condition, 1.0, 0.0).astype(jnp.bfloat16)


def spread_flags(experts, axis):
    shape = (experts * SLOTS, experts) if axis == 0 else (experts, experts * SLOTS)
    owner = lax.broadcasted_iota(jnp.int32, shape, axis) // SLOTS
    return flags(owner == lax.broadcasted_iota(jnp.int32, shape, 1 - axis))


def plan_kernel(ids_ref, rank_ref, pick_ref, ninth_ref):
    tokens, experts = rank_ref.shape
    named = named_mask(ids_ref, experts)
    earlier = flags(
        lax.broadcasted_iota(jnp.int32, (tokens, tokens), 0)
        > lax.broadcasted_iota(jnp.int32, (tokens, tokens), 1)
    )
    rank = jnp.where(named, dot(earlier, flags(named)) + 1.0, 0.0)
    rank_ref[...] = rank
    narrow = rank.astype(jnp.bfloat16)
    wide = dot_nt(spread_flags(experts, 0), narrow)
    row = lax.broadcasted_iota(jnp.int32, wide.shape, 0) % SLOTS
    slot = (row % HALF).astype(jnp.float32)
    for chunk in range(2):
        hit = wide == slot + float(1 + HALF * chunk)
        pick_ref[chunk, :, :tokens] = flags(hit & (row < HALF))
        pick_ref[chunk, :, tokens:] = flags(hit & (row >= HALF))
    same = flags(
        lax.broadcasted_iota(jnp.int32, (experts, experts), 0)
        == lax.broadcasted_iota(jnp.int32, (experts, experts), 1)
    )
    ninth_ref[...] = flags(dot_nt(same, narrow) == SLOTS + 1.0)


def plan(ids, experts):
    tokens = ids.shape[0]
    return pl.pallas_call(
        plan_kernel,
        out_shape=[
            pltpu.HBM((tokens, experts), jnp.float32),
            pltpu.HBM((2, experts * SLOTS, 2 * tokens), jnp.bfloat16),
            pltpu.HBM((experts, tokens), jnp.bfloat16),
        ],
        name="plan",
    )(ids)


def route_first_kernel(resid_ref, proj_ref, gain_ref, pick_ref, send_ref, halves_ref):
    step = pl.program_id(0)
    tokens, width = resid_ref.shape
    cols = send_ref.shape[1]
    half = width // 2

    @pl.when(step == 0)
    def _():
        hidden = resid_ref[...].astype(jnp.float32) + proj_ref[...].astype(jnp.float32)
        mean_square = jnp.mean(hidden * hidden, axis=1, keepdims=True)
        normed = (hidden * lax.rsqrt(mean_square + 1e-06) * gain_ref[...]).astype(jnp.bfloat16)
        halves_ref[:tokens, :] = normed[:, :half]
        halves_ref[tokens:, :] = normed[:, half:]

    for j in range(half // cols):

        @pl.when(step == j)
        def _():
            send_ref[...] = dot(
                pick_ref[0], halves_ref[:, j * cols : (j + 1) * cols]
            ).astype(jnp.bfloat16)


def route_first(resid, projected, gain, pick, cols=512):
    tokens, width = resid.shape
    rows, twice = pick.shape[1:]
    half = width // 2
    whole = lambda shape: pl.BlockSpec(shape, lambda j: (0,) * len(shape))
    return pl.pallas_call(
        route_first_kernel,
        grid=(half // cols,),
        in_specs=[
            whole((tokens, width)),
            whole((tokens, width)),
            whole((1, width)),
            whole((1, rows, twice)),
        ],
        out_specs=[pl.BlockSpec((rows, cols), lambda j: (0, j)), whole((twice, half))],
        out_shape=[
            pltpu.HBM((rows, half), jnp.bfloat16),
            pltpu.HBM((twice, half), jnp.bfloat16),
        ],
        compiler_params=pltpu.CompilerParams(vmem_limit_bytes=32 * MIB),
        name="route_first",
    )(resid, projected, gain, pick)


def route_second_kernel(halves_ref, pick_ref, ninth_ref, send_ref, extra_ref):
    step = pl.program_id(0)
    twice, half = halves_ref.shape
    cols = send_ref.shape[1]
    experts, tokens = ninth_ref.shape
    steps = half // cols

    for j in range(steps):

        @pl.when(step == j)
        def _():
            part = halves_ref[:, j * cols : (j + 1) * cols]
            send_ref[...] = dot(pick_ref[0], part).astype(jnp.bfloat16)
            for side in range(2):
                piece = dot(ninth_ref[...], part[side * tokens : (side + 1) * tokens])
                for b in range(cols // 128):
                    extra_ref[b, pl.ds(side * steps + j, experts, stride=SLOTS), :] = piece[
                        :, b * 128 : (b + 1) * 128
                    ]

    @pl.when(step == steps)
    def _():
        for b in range(cols // 128):
            send_ref[:, b * 128 : (b + 1) * 128] = extra_ref[b].astype(jnp.bfloat16)


def route_second(halves, pick, ninth):
    twice, half = halves.shape
    rows = pick.shape[1]
    cols = 2 * half // SLOTS
    whole = lambda shape: pl.BlockSpec(shape, lambda j: (0,) * len(shape))
    return pl.pallas_call(
        route_second_kernel,
        grid=(half // cols + 1,),
        in_specs=[
            whole((twice, half)),
            pl.BlockSpec((1, rows, twice), lambda j: (1, 0, 0)),
            whole(ninth.shape),
        ],
        out_specs=pl.BlockSpec((rows, cols), lambda j: (0, j)),
        out_shape=pltpu.HBM((rows, half + cols), jnp.bfloat16),
        scratch_shapes=[pltpu.VMEM((cols // 128, rows, 128), jnp.float32)],
        compiler_params=pltpu.CompilerParams(vmem_limit_bytes=32 * MIB),
        name="route_second",
    )(halves, pick, ninth)


def weights_kernel(halves_ref, router_ref, rank_ref, main_ref, ninth_ref):
    tokens, experts = rank_ref.shape
    half = halves_ref.shape[1]
    rank = rank_ref[...]
    named = rank > 0.0
    logits = dot(halves_ref[:tokens, :], router_ref[:half, :]) + dot(
        halves_ref[tokens:, :], router_ref[half:, :]
    )
    top = jnp.max(jnp.where(named, logits, -jnp.inf), axis=1, keepdims=True)
    raised = jnp.where(named, jnp.exp(jnp.where(named, logits, top) - top), 0.0)
    weight = raised / jnp.sum(raised, axis=1, keepdims=True)
    high = weight.astype(jnp.bfloat16)
    low = (weight - high.astype(jnp.float32)).astype(jnp.bfloat16)
    spread = spread_flags(experts, 1)
    wide_rank = dot(rank.astype(jnp.bfloat16), spread)
    row = lax.broadcasted_iota(jnp.int32, wide_rank.shape, 1) % SLOTS
    slot = (row % HALF).astype(jnp.float32)
    for term, part in enumerate((high, low)):
        place = pl.ds(term * tokens, tokens)
        wide = dot(part, spread)
        for chunk in range(2):
            kept = jnp.where(wide_rank == slot + float(1 + HALF * chunk), wide, 0.0)
            main_ref[chunk, 0, place, :] = jnp.where(row < HALF, kept, 0.0).astype(jnp.bfloat16)
            main_ref[chunk, 1, place, :] = jnp.where(row >= HALF, kept, 0.0).astype(jnp.bfloat16)
        ninth_ref[place, :] = jnp.where(
            rank == SLOTS + 1.0, part.astype(jnp.float32), 0.0
        ).astype(jnp.bfloat16)


def weights(halves, router, rank):
    tokens, experts = rank.shape
    return pl.pallas_call(
        weights_kernel,
        out_shape=[
            pltpu.HBM((2, 2, 2 * tokens, experts * SLOTS), jnp.bfloat16),
            pltpu.HBM((2 * tokens, experts), jnp.bfloat16),
        ],
        compiler_params=pltpu.CompilerParams(vmem_limit_bytes=32 * MIB),
        name="weights",
    )(halves, router, rank)


def sort_rows():
    to = lax.broadcasted_iota(jnp.int32, (GROUP, GROUP), 0)
    source = lax.broadcasted_iota(jnp.int32, (GROUP, GROUP), 1)
    count = GROUP // 2
    side, index = to // count, to % count
    return flags(source == index // HALF * SLOTS + side * HALF + index % HALF)


def sort_pieces():
    to = lax.broadcasted_iota(jnp.int32, (GROUP, GROUP), 0)
    source = lax.broadcasted_iota(jnp.int32, (GROUP, GROUP), 1)
    count = GROUP // SLOTS
    return flags(source == to % count * SLOTS + to // count)


def dot_tn(a, b):
    return lax.dot_general(a, b, (((0,), (0,)), ((), ())), preferred_element_type=jnp.float32)


def expert_kernel(*refs, deep, ninth):
    rows_ref, refs = refs[0], refs[1:]
    gate_ref, up_ref, first_ref, second_ref, out_ref = refs[:5]
    token_ref, gate_acc, up_acc, act_ref, piece_ref = refs[5:]
    step = pl.program_id(0)
    groups = out_ref.shape[0] // GROUP
    count = GROUP // 2
    few = GROUP // SLOTS
    main = groups * count
    cols = out_ref.shape[1]
    half = rows_ref.shape[1] - (cols if ninth else 0)
    deep_cols = gate_ref.shape[1]
    steps = half // cols

    @pl.when(step < groups)
    def _():
        g = jnp.minimum(step, groups - 1)
        place = pl.ds(pl.multiple_of(g * count, count), count)
        lined = dot(sort_rows(), rows_ref[:, :half]).astype(jnp.bfloat16)
        for k in range(deep):
            side, lane = divmod(k * deep_cols, half)
            token_ref[k, place, :] = lined[
                side * count : (side + 1) * count, lane : lane + deep_cols
            ]
        if ninth:
            place = pl.ds(pl.multiple_of(main + g * few, few), few)
            pieces = dot(sort_pieces(), rows_ref[:, half:]).astype(jnp.bfloat16)
            for j in range(SLOTS):
                k, lane = divmod(j * cols, deep_cols)
                token_ref[k, place, lane : lane + cols] = pieces[j * few : (j + 1) * few]

    start = groups

    @pl.when(step == start)
    def _():
        gate_acc[...] = dot(token_ref[0], gate_ref[0])
        up_acc[...] = dot(token_ref[0], up_ref[0])

    @pl.when((step > start) & (step < start + deep))
    def _():
        rows = token_ref[jnp.clip(step - start, 0, deep - 1)]
        gate_acc[...] += dot(rows, gate_ref[0])
        up_acc[...] += dot(rows, up_ref[0])

    @pl.when(step == start + deep - 1)
    def _():
        gate_val = gate_acc[...]
        act_ref[...] = (gate_val / (1.0 + jnp.exp(-gate_val)) * up_acc[...]).astype(jnp.bfloat16)

    start = groups + deep

    @pl.when((step >= start) & (step < start + steps))
    def _():
        act = act_ref[...]
        sides = [dot(act, ref[0]).astype(jnp.bfloat16) for ref in (first_ref, second_ref)]
        order = sort_rows()
        for g in range(groups):
            part = jnp.concatenate([side[g * count : (g + 1) * count] for side in sides], axis=0)
            out_ref[g * GROUP : (g + 1) * GROUP, :] = dot_tn(order, part).astype(jnp.bfloat16)
        if ninth:
            j = jnp.clip(step - start, 0, steps - 1)
            for which, side in enumerate(sides):
                piece_ref[j + which * steps] = side[main:]

    if ninth:

        @pl.when(step == start + steps)
        def _():
            order = sort_pieces()
            for g in range(groups):
                part = jnp.concatenate(
                    [piece_ref[j, g * few : (g + 1) * few, :] for j in range(SLOTS)], axis=0
                )
                out_ref[g * GROUP : (g + 1) * GROUP, :] = dot_tn(order, part).astype(jnp.bfloat16)


def expert(rows, w_gate, w_up, w_down, ninth, deep=4):
    tall, columns = rows.shape
    _, width, hidden = w_gate.shape
    half, cols = width // 2, width // SLOTS
    assert columns == half + (cols if ninth else 0) and tall % GROUP == 0
    groups, steps = tall // GROUP, half // cols
    main = tall // 2 + (tall // SLOTS if ninth else 0)
    at = groups + deep
    inner = lambda s, begin, count: jnp.clip(s - begin, 0, count - 1)
    weight = pl.BlockSpec((1, width // deep, hidden), lambda s: (0, inner(s, groups, deep), 0))
    return pl.pallas_call(
        functools.partial(expert_kernel, deep=deep, ninth=ninth),
        grid=(at + steps + ninth,),
        in_specs=[
            pl.BlockSpec((GROUP, columns), lambda s: (inner(s, 0, groups), 0)),
            weight,
            weight,
            pl.BlockSpec((1, hidden, cols), lambda s: (0, 0, inner(s, at, steps))),
            pl.BlockSpec((1, hidden, cols), lambda s: (0, 0, steps + inner(s, at, steps))),
        ],
        out_specs=pl.BlockSpec((tall, cols), lambda s: (0, inner(s, at, steps + ninth))),
        out_shape=pltpu.HBM(rows.shape, jnp.bfloat16),
        scratch_shapes=[
            pltpu.VMEM((deep, main, width // deep), jnp.bfloat16),
            pltpu.VMEM((main, hidden), jnp.float32),
            pltpu.VMEM((main, hidden), jnp.float32),
            pltpu.VMEM((main, hidden), jnp.bfloat16),
            pltpu.VMEM((SLOTS, tall // SLOTS, cols), jnp.bfloat16),
        ],
        compiler_params=pltpu.CompilerParams(vmem_limit_bytes=40 * MIB),
        name="expert_second" if ninth else "expert_first",
    )(rows, w_gate, w_up, w_down, w_down)


def combine_first_kernel(rows_ref, weight_ref, *refs):
    resids, projs, outs = refs[:2], refs[2:4], refs[4:]
    tokens = outs[0].shape[0]
    for side in range(2):
        both = dot(weight_ref[0, side], rows_ref[...])
        hidden = resids[side][...].astype(jnp.float32) + projs[side][...].astype(jnp.float32)
        outs[side][...] = hidden + (both[:tokens] + both[tokens:])


def combine_first(rows, main_weight, resid, projected):
    tokens, width = resid.shape
    tall, half = rows.shape
    cols = width // SLOTS
    steps = half // cols
    first = pl.BlockSpec((tokens, cols), lambda j: (0, j))
    second = pl.BlockSpec((tokens, cols), lambda j: (0, steps + j))
    shape = pltpu.HBM((tokens, half), jnp.float32)
    return pl.pallas_call(
        combine_first_kernel,
        grid=(steps,),
        in_specs=[
            pl.BlockSpec((tall, cols), lambda j: (0, j)),
            pl.BlockSpec((1,) + main_weight.shape[1:], lambda j: (0, 0, 0, 0)),
            first,
            second,
            first,
            second,
        ],
        out_specs=[first, first],
        out_shape=[shape, shape],
        compiler_params=pltpu.CompilerParams(vmem_limit_bytes=32 * MIB),
        name="combine_first",
    )(rows, main_weight, resid, resid, projected, projected)


def combine_second_kernel(
    rows_ref, extra_ref, weight_ref, ninth_ref, first_ref, second_ref, out_ref, piece_ref
):
    step = pl.program_id(0)
    tall, cols = rows_ref.shape
    tokens = out_ref.shape[0]
    groups, few = tall // GROUP, GROUP // SLOTS
    steps = SLOTS // 2

    @pl.when(step == 0)
    def _():
        order = sort_pieces()
        for g in range(groups):
            pieces = dot(order, extra_ref[g * GROUP : (g + 1) * GROUP, :]).astype(jnp.bfloat16)
            for j in range(SLOTS):
                piece_ref[j, g * few : (g + 1) * few, :] = pieces[j * few : (j + 1) * few]

    for j in range(steps):

        @pl.when(step == j)
        def _():
            for side, ref in enumerate((first_ref, second_ref)):
                piece = side * steps + j
                both = dot(weight_ref[0, side], rows_ref[...]) + dot(
                    ninth_ref[...], piece_ref[piece]
                )
                out_ref[:, piece * cols : (piece + 1) * cols] = (
                    ref[...] + (both[:tokens] + both[tokens:])
                ).astype(jnp.bfloat16)


def combine_second(rows, main_weight, ninth_weight, first, second):
    tokens, half = first.shape
    tall = rows.shape[0]
    cols = 2 * half // SLOTS
    steps = half // cols
    part = pl.BlockSpec((tokens, cols), lambda j: (0, j))
    return pl.pallas_call(
        combine_second_kernel,
        grid=(steps,),
        in_specs=[
            pl.BlockSpec((tall, cols), lambda j: (0, j)),
            pl.BlockSpec((tall, cols), lambda j: (0, steps)),
            pl.BlockSpec((1,) + main_weight.shape[1:], lambda j: (1, 0, 0, 0)),
            pl.BlockSpec(ninth_weight.shape, lambda j: (0, 0)),
            part,
            part,
        ],
        out_specs=pl.BlockSpec((tokens, 2 * half), lambda j: (0, 0)),
        out_shape=jax.ShapeDtypeStruct((tokens, 2 * half), jnp.bfloat16),
        scratch_shapes=[pltpu.VMEM((SLOTS, tall // SLOTS, cols), jnp.bfloat16)],
        compiler_params=pltpu.CompilerParams(vmem_limit_bytes=32 * MIB),
        name="combine_second",
    )(rows, rows, main_weight, ninth_weight, first, second)


def per_device(
    resid,
    queries,
    span_rotated_keys,
    span_value_rows,
    key_cache,
    prefix_value_cache,
    prefix_len,
    out_weight,
    norm_gain,
    router_weight,
    expert_ids,
    w_gate,
    w_up,
    w_down,
):
    seq_count = lax.axis_size("seq")
    width = resid.shape[2]
    experts = router_weight.shape[1]
    packed = pack(
        queries, span_rotated_keys, span_value_rows, key_cache, prefix_value_cache, seq_count
    )
    packed = lax.all_to_all(packed, "seq", split_axis=0, concat_axis=0, tiled=True)
    projected = lax.psum_scatter(
        attend(prefix_len, packed, in_hbm(out_weight)), "seq", scatter_dimension=0, tiled=True
    )
    projected = in_hbm(projected)
    rank, pick, ninth = [in_hbm(x) for x in plan(expert_ids[0], experts)]
    send_first, halves = route_first(resid[0], projected, norm_gain.reshape(1, width), pick)

    def exchange(rows):
        blocks = rows.reshape(experts, SLOTS, rows.shape[1])
        return in_hbm(
            lax.all_to_all(
                blocks, ("seq", "exp"), split_axis=0, concat_axis=0, tiled=True
            ).reshape(rows.shape)
        )

    halves = in_hbm(halves)
    w_gate, w_up, w_down = in_hbm(w_gate), in_hbm(w_up), in_hbm(w_down)
    got_first = exchange(send_first)
    got_second = exchange(route_second(halves, pick, ninth))
    main_weight, ninth_weight = [in_hbm(x) for x in weights(halves, router_weight, rank)]
    back_first = exchange(expert(got_first, w_gate, w_up, w_down, False))
    back_second = exchange(expert(got_second, w_gate, w_up, w_down, True))
    first, second = combine_first(back_first, main_weight, resid[0], projected)
    return combine_second(
        back_second, main_weight, ninth_weight, in_hbm(first), in_hbm(second)
    )[None]


def solution(mesh):
    in_specs = (
        P("exp", "seq", None),
        P("exp", "seq", None),
        P("exp", "seq", None),
        P("exp", "seq", None),
        P("exp", None, "seq", None),
        P("exp", None, "seq", None),
        P("exp"),
        P("seq", None),
        P(),
        P(),
        P("exp", "seq", None),
        P(("seq", "exp"), None, None),
        P(("seq", "exp"), None, None),
        P(("seq", "exp"), None, None),
    )
    out_specs = P("exp", "seq", None)
    return jax.shard_map(
        per_device, mesh=mesh, in_specs=in_specs, out_specs=out_specs, check_vma=False
    )
```

time: 423 us -> 436 us (1.031)
  blocking collectives: 116 us -> 0 us
  Pallas kernels: 73.5 us -> 149 us
  waiting for transfers between devices: 196 us -> 237 us
  starting transfers between devices: 12.5 us -> 33.2 us
  local copies, waits for them, and re-layouts: 9.57 us -> 1.38 us
    all_to_all x1 -> x0, blocking collectives: 116 us -> none  [exchange(): lax.all_to_all(blocks, ('seq', 'exp'), split_axis=0, concat_axis=0, tiled...]
    pallas_call x6 -> x9, Pallas kernels: 57.9 us -> 133 us  [the longest x1 57 us: pack(): pl.pallas_call(pack_kernel, in_specs=[pl.BlockSpec(memory_space=pltpu.HBM...]
    all_to_all x1 -> x4, waiting for transfers between devices: 124 us -> 166 us  [exchange(): lax.all_to_all(blocks, ('seq', 'exp'), split_axis=0, concat_axis=0, tiled...]
    all_to_all x1 -> x4, starting transfers between devices: 7.35 us -> 28.1 us  [exchange(): lax.all_to_all(blocks, ('seq', 'exp'), split_axis=0, concat_axis=0, tiled...]
    unnamed x29 -> x9, local copies, waits for them, and re-layouts: 9.57 us -> 1.38 us
  transfers between devices with their start and end apart: 3 -> 6, of which waited for: 3 -> 6; matrix products, arithmetic and copies ran while one was open for 0% -> 0% of each run, Pallas kernels for 1% -> 14%
where the time goes in v3:
time: 436 us; the launch traced here: 434 us
  waiting for transfers between devices  237 us (54%)
  Pallas kernels  149 us (34%)
  starting transfers between devices  33.2 us (8%)
  between operations  14.1 us (3%)
    all_to_all x4, waiting for transfers between devices, exchange(): lax.all_to_all(blocks, ('seq', 'exp'), split_axis=0, concat_axis=0, tiled...  166 us
    pallas_call x1, Pallas kernels, pack(): pl.pallas_call(pack_kernel, in_specs=[pl.BlockSpec(memory_space=pltpu.HBM...  57 us
    reduce_scatter x1, waiting for transfers between devices, per_device(): lax.psum_scatter(attend(prefix_len, packed, in_hbm(out_weight)), 'seq', s...  48.5 us
    pallas_call x2, Pallas kernels, expert(): pl.pallas_call(functools.partial(expert_kernel, deep=deep, ninth=ninth),...  44.1 us
    all_to_all x4, starting transfers between devices, exchange(): lax.all_to_all(blocks, ('seq', 'exp'), split_axis=0, concat_axis=0, tiled...  28.1 us
    all_to_all x1, waiting for transfers between devices, per_device(): lax.all_to_all(packed, 'seq', split_axis=0, concat_axis=0, tiled=True)  22.9 us
    pallas_call x1, Pallas kernels, attend(): pl.pallas_call(attend_kernel, grid=(span // rows,), in_specs=[pl.BlockSpe...  15.9 us
  transfers between devices with their start and end apart: 6, of which 6 were waited for; matrix products, arithmetic and copies ran while one was open for 0% of the time, Pallas kernels for 14%

profile of v3, /device:TPU:5, one launch (start us, length us, event | category | flops | bytes accessed | tf_op | source)
XLA Modules:
  0.0 434.4 jit_solution(1360581398892719478)
XLA Ops:
  6.5 57.0 %pack.1 = bf16[8,128,896]{2,1,0:T(8,128)(2,1)} custom-call(bf16[1,128,4096]{2,1,0:T(8,128)(2,1)} %query_ref.1, bf16[1,128,512]{2,1,0:T(8,128)(2,1)} %key_ref.1, bf16[1,128,512]{2,1,0:T(8,128)(2,1)} %value_ref.1, bf16[1,4,64,128]{3,2,1,0:T(8,128)(2,1)} %key_cache_ref.1, bf16[1,4,64,128]{3,2,1,0:T(8,128)(2,1)} %value_cache_ref.1), custom_call_target="tpu_custom_call" | custom-call | tf_op jit(solution)/shard_map/pack/pallas_call | solution.py:68
  63.6 5.2 %all-to-all-start = ((bf16[8,128,896]{2,1,0:T(8,128)(2,1)}), bf16[8,128,896]{2,1,0:T(8,128)(2,1)S(1)}, u32[]{:S(2)}, u32[]{:S(2)}) async-start(bf16[8,128,896]{2,1,0:T(8,128)(2,1)} %pack.1), calls=%async_computation | async-start | bytes 3670016 | tf_op jit(solution)/shard_map/all_to_all | solution.py:608
  68.7 0.0 reduce-scatter.2.cloned.1.call-start
  69.4 22.9 %all-to-all-done.packed_ref = bf16[8,128,896]{2,1,0:T(8,128)(2,1)S(1)} async-done(((bf16[8,128,896]{2,1,0:T(8,128)(2,1)}), bf16[8,128,896]{2,1,0:T(8,128)(2,1)S(1)}, u32[]{:S(2)}, u32[]{:S(2)}) %all-to-all-start) | async-done | bytes 1835040 | tf_op jit(solution)/shard_map/all_to_all | solution.py:608
  92.3 15.9 %attend.1 = bf16[1024,4096]{1,0:T(8,128)(2,1)} custom-call(s32[1]{0:T(128)S(6)} %copy.16.length_ref, bf16[8,128,896]{2,1,0:T(8,128)(2,1)S(1)} %all-to-all-done.packed_ref, bf16[512,4096]{1,0:T(8,128)(2,1)} %out_weight_hbm.1), custom_call_target="tpu_custom_call" | custom-call | tf_op jit(solution)/shard_map/attend/pallas_call | solution.py:152
  108.1 0.0 copy-start.3
  108.1 0.0 copy-start
  108.2 0.0 copy-start.2
  108.2 0.0 reduce-scatter.2.cloned.1.call-update
  108.2 0.6 copy-done.3
  108.8 0.7 copy.15
  109.6 2.7 plan.1
  112.2 48.5 %reduce-scatter.2.cloned.1.call-done.proj_ref.refs_2_.refs_3_ = bf16[128,4096]{1,0:T(8,128)(2,1)} async-done(((bf16[1024,4096]{1,0:T(8,128)(2,1)}), bf16[128,4096]{1,0:T(8,128)(2,1)}) %reduce-scatter.2.cloned.1.call-update) | async-done | bytes 1048592 | tf_op jit(solution)/shard_map/reduce_scatter | solution.py:609
  160.7 0.0 copy-done
  160.7 0.0 copy-done.2
  160.7 5.8 %route_first.1 = (bf16[1024,2048]{1,0:T(8,128)(2,1)}, bf16[256,2048]{1,0:T(8,128)(2,1)}) custom-call(bf16[128,4096]{1,0:T(8,128)(2,1)S(1)} %bitcast.12, bf16[128,4096]{1,0:T(8,128)(2,1)} %reduce-scatter.2.cloned.1.call-done.proj_ref.refs_2_.refs_3_, f32[1,4096]{1,0:T(1,128)S(1)} %bitcast.15, bf16[2,1024,256]{2,1,0:T(8,128)(2,1)} %get-tuple-element.14.pick_ref), custom_call_target="tpu_custom_call" | custom-call | tf_op jit(solution)/shard_map/route_first/pallas_call | solution.py:258
  166.5 9.1 %all-to-all-start.3 = ((bf16[128,8,2048]{2,1,0:T(8,128)(2,1)}), bf16[128,8,2048]{2,1,0:T(8,128)(2,1)}, u32[]{:S(2)}, u32[]{:S(2)}) async-start(bf16[128,8,2048]{2,1,0:T(8,128)(2,1)} %bitcast.19), calls=%async_computation.4 | async-start | bytes 8388608 | tf_op jit(solution)/shard_map/all_to_all | solution.py:619
  175.6 6.0 %route_second.1 = bf16[1024,2560]{1,0:T(8,128)(2,1)} custom-call(bf16[256,2048]{1,0:T(8,128)(2,1)} %get-tuple-element.15.halves_ref, bf16[2,1024,256]{2,1,0:T(8,128)(2,1)} %get-tuple-element.14.pick_ref, bf16[128,128]{1,0:T(8,128)(2,1)} %get-tuple-element.16.ninth_ref), custom_call_target="tpu_custom_call" | custom-call | tf_op jit(solution)/shard_map/route_second/pallas_call | solution.py:308
  181.5 44.6 %all-to-all-done.3 = bf16[128,8,2048]{2,1,0:T(8,128)(2,1)} async-done(((bf16[128,8,2048]{2,1,0:T(8,128)(2,1)}), bf16[128,8,2048]{2,1,0:T(8,128)(2,1)}, u32[]{:S(2)}, u32[]{:S(2)}) %all-to-all-start.3) | async-done | bytes 4194336 | tf_op jit(solution)/shard_map/all_to_all | solution.py:619
  226.1 6.2 %all-to-all-start.1 = ((bf16[128,8,2560]{2,1,0:T(8,128)(2,1)}), bf16[128,8,2560]{2,1,0:T(8,128)(2,1)}, u32[]{:S(2)}, u32[]{:S(2)}) async-start(bf16[128,8,2560]{2,1,0:T(8,128)(2,1)} %bitcast.17), calls=%async_computation.2 | async-start | bytes 10485760 | tf_op jit(solution)/shard_map/all_to_all | solution.py:619
  232.3 20.4 %expert_first.1 = bf16[1024,2048]{1,0:T(8,128)(2,1)} custom-call(bf16[1024,2048]{1,0:T(8,128)(2,1)} %bitcast.8.refs_0_, bf16[1,4096,768]{2,1,0:T(8,128)(2,1)} %refs_1_.3, bf16[1,4096,768]{2,1,0:T(8,128)(2,1)} %refs_2_.3, bf16[1,768,4096]{2,1,0:T(8,128)(2,1)} %refs_4_.3, bf16[1,768,4096]{2,1,0:T(8,128)(2,1)} %refs_4_.3), custom_call_target="tpu_custom_call" | custom-call | tf_op jit(solution)/shard_map/expert_first/pallas_call | solution.py:471
  252.7 41.8 %all-to-all-done.1 = bf16[128,8,2560]{2,1,0:T(8,128)(2,1)} async-done(((bf16[128,8,2560]{2,1,0:T(8,128)(2,1)}), bf16[128,8,2560]{2,1,0:T(8,128)(2,1)}, u32[]{:S(2)}, u32[]{:S(2)}) %all-to-all-start.1) | async-done | bytes 5242912 | tf_op jit(solution)/shard_map/all_to_all | solution.py:619
  294.5 6.6 %all-to-all-start.4 = ((bf16[128,8,2048]{2,1,0:T(8,128)(2,1)}), bf16[128,8,2048]{2,1,0:T(8,128)(2,1)}, u32[]{:S(2)}, u32[]{:S(2)}) async-start(bf16[128,8,2048]{2,1,0:T(8,128)(2,1)} %bitcast.18), calls=%async_computation.5 | async-start | bytes 8388608 | tf_op jit(solution)/shard_map/all_to_all | solution.py:619
  301.1 23.6 %expert_second.1 = bf16[1024,2560]{1,0:T(8,128)(2,1)} custom-call(bf16[1024,2560]{1,0:T(8,128)(2,1)} %bitcast.4.refs_0_, bf16[1,4096,768]{2,1,0:T(8,128)(2,1)} %refs_1_.3, bf16[1,4096,768]{2,1,0:T(8,128)(2,1)} %refs_2_.3, bf16[1,768,4096]{2,1,0:T(8,128)(2,1)} %refs_4_.3, bf16[1,768,4096]{2,1,0:T(8,128)(2,1)} %refs_4_.3), custom_call_target="tpu_custom_call" | custom-call | tf_op jit(solution)/shard_map/expert_second/pallas_call | solution.py:471
  324.7 26.9 %all-to-all-done.4 = bf16[128,8,2048]{2,1,0:T(8,128)(2,1)} async-done(((bf16[128,8,2048]{2,1,0:T(8,128)(2,1)}), bf16[128,8,2048]{2,1,0:T(8,128)(2,1)}, u32[]{:S(2)}, u32[]{:S(2)}) %all-to-all-start.4) | async-done | bytes 4194336 | tf_op jit(solution)/shard_map/all_to_all | solution.py:619
  351.6 0.0 copy-start.1
  351.6 6.2 %all-to-all-start.2 = ((bf16[128,8,2560]{2,1,0:T(8,128)(2,1)}), bf16[128,8,2560]{2,1,0:T(8,128)(2,1)}, u32[]{:S(2)}, u32[]{:S(2)}) async-start(bf16[128,8,2560]{2,1,0:T(8,128)(2,1)} %bitcast.16), calls=%async_computation.3 | async-start | bytes 10485760 | tf_op jit(solution)/shard_map/all_to_all | solution.py:619
  357.8 0.0 copy-done.1
  357.8 3.7 weights.1
  361.6 6.0 %combine_first.1 = (f32[128,2048]{1,0:T(8,128)}, f32[128,2048]{1,0:T(8,128)}) custom-call(bf16[1024,2048]{1,0:T(8,128)(2,1)} %bitcast.10.rows_ref, bf16[2,2,256,1024]{3,2,1,0:T(8,128)(2,1)} %get-tuple-element.18.weight_ref, bf16[128,4096]{1,0:T(8,128)(2,1)S(1)} %bitcast.13, bf16[128,4096]{1,0:T(8,128)(2,1)S(1)} %bitcast.14, ...), custom_call_target="tpu_custom_call" | custom-call | tf_op jit(solution)/shard_map/combine_first/pallas_call | solution.py:512
  367.6 52.4 %all-to-all-done.2 = bf16[128,8,2560]{2,1,0:T(8,128)(2,1)} async-done(((bf16[128,8,2560]{2,1,0:T(8,128)(2,1)}), bf16[128,8,2560]{2,1,0:T(8,128)(2,1)}, u32[]{:S(2)}, u32[]{:S(2)}) %all-to-all-start.2) | async-done | bytes 5242912 | tf_op jit(solution)/shard_map/all_to_all | solution.py:619
  420.0 7.5 %combine_second.1 = bf16[128,4096]{1,0:T(8,128)(2,1)} custom-call(bf16[1024,2560]{1,0:T(8,128)(2,1)} %bitcast.6.rows_ref.extra_ref, bf16[1024,2560]{1,0:T(8,128)(2,1)} %bitcast.6.rows_ref.extra_ref, bf16[2,2,256,1024]{3,2,1,0:T(8,128)(2,1)} %get-tuple-element.18.weight_ref, bf16[256,128]{1,0:T(8,128)(2,1)} %get-tuple-element.19.ninth_ref, ...), custom_call_target="tpu_custom_call" | custom-call | tf_op jit(solution)/shard_map/combine_second/pallas_call | solution.py:567
Async XLA Ops:
  63.6 28.7 %all-to-all-start = ((bf16[8,128,896]{2,1,0:T(8,128)(2,1)}), bf16[8,128,896]{2,1,0:T(8,128)(2,1)S(1)}, u32[]{:S(2)}, u32[]{:S(2)}) async-start(bf16[8,128,896]{2,1,0:T(8,128)(2,1)} %pack.1), calls=%async_computation | async-start | bytes 3670016 | tf_op jit(solution)/shard_map/all_to_all | solution.py:608
  68.7 92.0 %reduce-scatter.2.cloned.1.call-start = ((), (), s32[]{:S(2)}) async-start(), calls=%async_computation.6 | async-start | bytes 9437184 | tf_op jit(solution)/shard_map/reduce_scatter | solution.py:609
  108.1 0.7 copy-start.3
  108.1 52.6 %copy-start = (bf16[1,128,4096]{2,1,0:T(8,128)(2,1)S(1)}, bf16[1,128,4096]{2,1,0:T(8,128)(2,1)}, u32[]{:S(2)}) copy-start(bf16[1,128,4096]{2,1,0:T(8,128)(2,1)} %param.14) | copy-start | bytes 3145732
  108.2 52.6 %copy-start.2 = (f32[4096]{0:T(1024)S(1)}, f32[4096]{0:T(1024)}, u32[]{:S(2)}) copy-start(f32[4096]{0:T(1024)} %param.22) | copy-start | bytes 49156
  166.5 59.6 %all-to-all-start.3 = ((bf16[128,8,2048]{2,1,0:T(8,128)(2,1)}), bf16[128,8,2048]{2,1,0:T(8,128)(2,1)}, u32[]{:S(2)}, u32[]{:S(2)}) async-start(bf16[128,8,2048]{2,1,0:T(8,128)(2,1)} %bitcast.19), calls=%async_computation.4 | async-start | bytes 8388608 | tf_op jit(solution)/shard_map/all_to_all | solution.py:619
  226.1 68.4 %all-to-all-start.1 = ((bf16[128,8,2560]{2,1,0:T(8,128)(2,1)}), bf16[128,8,2560]{2,1,0:T(8,128)(2,1)}, u32[]{:S(2)}, u32[]{:S(2)}) async-start(bf16[128,8,2560]{2,1,0:T(8,128)(2,1)} %bitcast.17), calls=%async_computation.2 | async-start | bytes 10485760 | tf_op jit(solution)/shard_map/all_to_all | solution.py:619
  294.5 57.1 %all-to-all-start.4 = ((bf16[128,8,2048]{2,1,0:T(8,128)(2,1)}), bf16[128,8,2048]{2,1,0:T(8,128)(2,1)}, u32[]{:S(2)}, u32[]{:S(2)}) async-start(bf16[128,8,2048]{2,1,0:T(8,128)(2,1)} %bitcast.18), calls=%async_computation.5 | async-start | bytes 8388608 | tf_op jit(solution)/shard_map/all_to_all | solution.py:619
  351.6 6.2 %copy-start.1 = (bf16[4096,128]{1,0:T(8,128)(2,1)S(1)}, bf16[4096,128]{1,0:T(8,128)(2,1)}, u32[]{:S(2)}) copy-start(bf16[4096,128]{1,0:T(8,128)(2,1)} %router_ref.1) | copy-start | bytes 3145732
  351.6 68.4 %all-to-all-start.2 = ((bf16[128,8,2560]{2,1,0:T(8,128)(2,1)}), bf16[128,8,2560]{2,1,0:T(8,128)(2,1)}, u32[]{:S(2)}, u32[]{:S(2)}) async-start(bf16[128,8,2560]{2,1,0:T(8,128)(2,1)} %bitcast.16), calls=%async_computation.3 | async-start | bytes 10485760 | tf_op jit(solution)/shard_map/all_to_all | solution.py:619
Sparse Core Ops, SparseCore 0:
  108.3 52.3 reduce-scatter.1

commit v4 on v3

--- a/solution.py
+++ b/solution.py
@@ -67,11 +67,9 @@
     lanes = width // seq_count
     return pl.pallas_call(
         pack_kernel,
-        in_specs=[pl.BlockSpec(memory_space=pltpu.HBM)] * 5,
+        in_specs=[pl.BlockSpec(memory_space=pltpu.VMEM)] * 5,
         out_specs=pl.BlockSpec(memory_space=pltpu.HBM),
-        out_shape=jax.ShapeDtypeStruct(
-            (seq_count, tokens, lanes + 3 * HEAD_SIZE), jnp.bfloat16
-        ),
+        out_shape=pltpu.HBM((seq_count, tokens, lanes + 3 * HEAD_SIZE), jnp.bfloat16),
         scratch_shapes=[pltpu.SemaphoreType.DMA((seq_count, 5))],
         name="pack",
     )(queries, keys, values, key_cache, value_cache)

time: 436 us -> 382 us (0.88)
  Pallas kernels: 149 us -> 94.6 us
    pallas_call x1, Pallas kernels: 57 us -> 2.97 us  [pack(): pl.pallas_call(pack_kernel, in_specs=[pl.BlockSpec(memory_space=pltpu.VME...]
  transfers between devices with their start and end apart: 6 -> 6, of which waited for: 6 -> 6; matrix products, arithmetic and copies ran while one was open for 0% -> 0% of each run, Pallas kernels for 14% -> 16%
where the time goes in v4:
time: 382 us; the launch traced here: 380 us
  waiting for transfers between devices  237 us (62%)
  Pallas kernels  94.6 us (25%)
  starting transfers between devices  33.2 us (9%)
  between operations  14.1 us (4%)
    all_to_all x4, waiting for transfers between devices, exchange(): lax.all_to_all(blocks, ('seq', 'exp'), split_axis=0, concat_axis=0, tiled...  166 us
    reduce_scatter x1, waiting for transfers between devices, per_device(): lax.psum_scatter(attend(prefix_len, packed, in_hbm(out_weight)), 'seq', s...  48.5 us
    pallas_call x2, Pallas kernels, expert(): pl.pallas_call(functools.partial(expert_kernel, deep=deep, ninth=ninth),...  44.1 us
    all_to_all x4, starting transfers between devices, exchange(): lax.all_to_all(blocks, ('seq', 'exp'), split_axis=0, concat_axis=0, tiled...  28.1 us
    all_to_all x1, waiting for transfers between devices, per_device(): lax.all_to_all(packed, 'seq', split_axis=0, concat_axis=0, tiled=True)  22.9 us
    pallas_call x1, Pallas kernels, attend(): pl.pallas_call(attend_kernel, grid=(span // rows,), in_specs=[pl.BlockSpe...  15.9 us
  transfers between devices with their start and end apart: 6, of which 6 were waited for; matrix products, arithmetic and copies ran while one was open for 0% of the time, Pallas kernels for 16%

profile of v4, /device:TPU:5, one launch (start us, length us, event | category | flops | bytes accessed | tf_op | source)
XLA Modules:
  0.0 380.3 jit_solution(14353981550154976120)
XLA Ops:
  6.5 3.0 pack.1
  9.5 5.2 %all-to-all-start = ((bf16[8,128,896]{2,1,0:T(8,128)(2,1)}), bf16[8,128,896]{2,1,0:T(8,128)(2,1)S(1)}, u32[]{:S(2)}, u32[]{:S(2)}) async-start(bf16[8,128,896]{2,1,0:T(8,128)(2,1)} %pack.1), calls=%async_computation | async-start | bytes 3670016 | tf_op jit(solution)/shard_map/all_to_all | solution.py:606
  14.7 0.0 reduce-scatter.2.cloned.1.call-start
  15.3 22.9 %all-to-all-done.packed_ref = bf16[8,128,896]{2,1,0:T(8,128)(2,1)S(1)} async-done(((bf16[8,128,896]{2,1,0:T(8,128)(2,1)}), bf16[8,128,896]{2,1,0:T(8,128)(2,1)S(1)}, u32[]{:S(2)}, u32[]{:S(2)}) %all-to-all-start) | async-done | bytes 1835040 | tf_op jit(solution)/shard_map/all_to_all | solution.py:606
  38.2 15.9 %attend.1 = bf16[1024,4096]{1,0:T(8,128)(2,1)} custom-call(s32[1]{0:T(128)S(6)} %copy.16.length_ref, bf16[8,128,896]{2,1,0:T(8,128)(2,1)S(1)} %all-to-all-done.packed_ref, bf16[512,4096]{1,0:T(8,128)(2,1)} %out_weight_hbm.1), custom_call_target="tpu_custom_call" | custom-call | tf_op jit(solution)/shard_map/attend/pallas_call | solution.py:150
  54.1 0.0 copy-start.3
  54.1 0.0 copy-start
  54.1 0.0 copy-start.2
  54.1 0.0 reduce-scatter.2.cloned.1.call-update
  54.1 0.6 copy-done.3
  54.8 0.7 copy.15
  55.5 2.7 plan.1
  58.2 48.5 %reduce-scatter.2.cloned.1.call-done.proj_ref.refs_2_.refs_3_ = bf16[128,4096]{1,0:T(8,128)(2,1)} async-done(((bf16[1024,4096]{1,0:T(8,128)(2,1)}), bf16[128,4096]{1,0:T(8,128)(2,1)}) %reduce-scatter.2.cloned.1.call-update) | async-done | bytes 1048592 | tf_op jit(solution)/shard_map/reduce_scatter | solution.py:607
  106.7 0.0 copy-done
  106.7 0.0 copy-done.2
  106.7 5.8 %route_first.1 = (bf16[1024,2048]{1,0:T(8,128)(2,1)}, bf16[256,2048]{1,0:T(8,128)(2,1)}) custom-call(bf16[128,4096]{1,0:T(8,128)(2,1)S(1)} %bitcast.12, bf16[128,4096]{1,0:T(8,128)(2,1)} %reduce-scatter.2.cloned.1.call-done.proj_ref.refs_2_.refs_3_, f32[1,4096]{1,0:T(1,128)S(1)} %bitcast.15, bf16[2,1024,256]{2,1,0:T(8,128)(2,1)} %get-tuple-element.14.pick_ref), custom_call_target="tpu_custom_call" | custom-call | tf_op jit(solution)/shard_map/route_first/pallas_call | solution.py:256
  112.4 9.0 %all-to-all-start.3 = ((bf16[128,8,2048]{2,1,0:T(8,128)(2,1)}), bf16[128,8,2048]{2,1,0:T(8,128)(2,1)}, u32[]{:S(2)}, u32[]{:S(2)}) async-start(bf16[128,8,2048]{2,1,0:T(8,128)(2,1)} %bitcast.19), calls=%async_computation.4 | async-start | bytes 8388608 | tf_op jit(solution)/shard_map/all_to_all | solution.py:617
  121.5 6.0 %route_second.1 = bf16[1024,2560]{1,0:T(8,128)(2,1)} custom-call(bf16[256,2048]{1,0:T(8,128)(2,1)} %get-tuple-element.15.halves_ref, bf16[2,1024,256]{2,1,0:T(8,128)(2,1)} %get-tuple-element.14.pick_ref, bf16[128,128]{1,0:T(8,128)(2,1)} %get-tuple-element.16.ninth_ref), custom_call_target="tpu_custom_call" | custom-call | tf_op jit(solution)/shard_map/route_second/pallas_call | solution.py:306
  127.4 44.6 %all-to-all-done.3 = bf16[128,8,2048]{2,1,0:T(8,128)(2,1)} async-done(((bf16[128,8,2048]{2,1,0:T(8,128)(2,1)}), bf16[128,8,2048]{2,1,0:T(8,128)(2,1)}, u32[]{:S(2)}, u32[]{:S(2)}) %all-to-all-start.3) | async-done | bytes 4194336 | tf_op jit(solution)/shard_map/all_to_all | solution.py:617
  172.0 6.2 %all-to-all-start.1 = ((bf16[128,8,2560]{2,1,0:T(8,128)(2,1)}), bf16[128,8,2560]{2,1,0:T(8,128)(2,1)}, u32[]{:S(2)}, u32[]{:S(2)}) async-start(bf16[128,8,2560]{2,1,0:T(8,128)(2,1)} %bitcast.17), calls=%async_computation.2 | async-start | bytes 10485760 | tf_op jit(solution)/shard_map/all_to_all | solution.py:617
  178.2 20.4 %expert_first.1 = bf16[1024,2048]{1,0:T(8,128)(2,1)} custom-call(bf16[1024,2048]{1,0:T(8,128)(2,1)} %bitcast.8.refs_0_, bf16[1,4096,768]{2,1,0:T(8,128)(2,1)} %refs_1_.3, bf16[1,4096,768]{2,1,0:T(8,128)(2,1)} %refs_2_.3, bf16[1,768,4096]{2,1,0:T(8,128)(2,1)} %refs_4_.3, bf16[1,768,4096]{2,1,0:T(8,128)(2,1)} %refs_4_.3), custom_call_target="tpu_custom_call" | custom-call | tf_op jit(solution)/shard_map/expert_first/pallas_call | solution.py:469
  198.6 41.8 %all-to-all-done.1 = bf16[128,8,2560]{2,1,0:T(8,128)(2,1)} async-done(((bf16[128,8,2560]{2,1,0:T(8,128)(2,1)}), bf16[128,8,2560]{2,1,0:T(8,128)(2,1)}, u32[]{:S(2)}, u32[]{:S(2)}) %all-to-all-start.1) | async-done | bytes 5242912 | tf_op jit(solution)/shard_map/all_to_all | solution.py:617
  240.4 6.6 %all-to-all-start.4 = ((bf16[128,8,2048]{2,1,0:T(8,128)(2,1)}), bf16[128,8,2048]{2,1,0:T(8,128)(2,1)}, u32[]{:S(2)}, u32[]{:S(2)}) async-start(bf16[128,8,2048]{2,1,0:T(8,128)(2,1)} %bitcast.18), calls=%async_computation.5 | async-start | bytes 8388608 | tf_op jit(solution)/shard_map/all_to_all | solution.py:617
  247.0 23.6 %expert_second.1 = bf16[1024,2560]{1,0:T(8,128)(2,1)} custom-call(bf16[1024,2560]{1,0:T(8,128)(2,1)} %bitcast.4.refs_0_, bf16[1,4096,768]{2,1,0:T(8,128)(2,1)} %refs_1_.3, bf16[1,4096,768]{2,1,0:T(8,128)(2,1)} %refs_2_.3, bf16[1,768,4096]{2,1,0:T(8,128)(2,1)} %refs_4_.3, bf16[1,768,4096]{2,1,0:T(8,128)(2,1)} %refs_4_.3), custom_call_target="tpu_custom_call" | custom-call | tf_op jit(solution)/shard_map/expert_second/pallas_call | solution.py:469
  270.7 26.9 %all-to-all-done.4 = bf16[128,8,2048]{2,1,0:T(8,128)(2,1)} async-done(((bf16[128,8,2048]{2,1,0:T(8,128)(2,1)}), bf16[128,8,2048]{2,1,0:T(8,128)(2,1)}, u32[]{:S(2)}, u32[]{:S(2)}) %all-to-all-start.4) | async-done | bytes 4194336 | tf_op jit(solution)/shard_map/all_to_all | solution.py:617
  297.5 0.0 copy-start.1
  297.5 6.2 %all-to-all-start.2 = ((bf16[128,8,2560]{2,1,0:T(8,128)(2,1)}), bf16[128,8,2560]{2,1,0:T(8,128)(2,1)}, u32[]{:S(2)}, u32[]{:S(2)}) async-start(bf16[128,8,2560]{2,1,0:T(8,128)(2,1)} %bitcast.16), calls=%async_computation.3 | async-start | bytes 10485760 | tf_op jit(solution)/shard_map/all_to_all | solution.py:617
  303.8 0.0 copy-done.1
  303.8 3.7 weights.1
  307.5 6.0 %combine_first.1 = (f32[128,2048]{1,0:T(8,128)}, f32[128,2048]{1,0:T(8,128)}) custom-call(bf16[1024,2048]{1,0:T(8,128)(2,1)} %bitcast.10.rows_ref, bf16[2,2,256,1024]{3,2,1,0:T(8,128)(2,1)} %get-tuple-element.18.weight_ref, bf16[128,4096]{1,0:T(8,128)(2,1)S(1)} %bitcast.13, bf16[128,4096]{1,0:T(8,128)(2,1)S(1)} %bitcast.14, ...), custom_call_target="tpu_custom_call" | custom-call | tf_op jit(solution)/shard_map/combine_first/pallas_call | solution.py:510
  313.5 52.4 %all-to-all-done.2 = bf16[128,8,2560]{2,1,0:T(8,128)(2,1)} async-done(((bf16[128,8,2560]{2,1,0:T(8,128)(2,1)}), bf16[128,8,2560]{2,1,0:T(8,128)(2,1)}, u32[]{:S(2)}, u32[]{:S(2)}) %all-to-all-start.2) | async-done | bytes 5242912 | tf_op jit(solution)/shard_map/all_to_all | solution.py:617
  365.9 7.5 %combine_second.1 = bf16[128,4096]{1,0:T(8,128)(2,1)} custom-call(bf16[1024,2560]{1,0:T(8,128)(2,1)} %bitcast.6.rows_ref.extra_ref, bf16[1024,2560]{1,0:T(8,128)(2,1)} %bitcast.6.rows_ref.extra_ref, bf16[2,2,256,1024]{3,2,1,0:T(8,128)(2,1)} %get-tuple-element.18.weight_ref, bf16[256,128]{1,0:T(8,128)(2,1)} %get-tuple-element.19.ninth_ref, ...), custom_call_target="tpu_custom_call" | custom-call | tf_op jit(solution)/shard_map/combine_second/pallas_call | solution.py:565
Async XLA Ops:
  9.5 28.7 %all-to-all-start = ((bf16[8,128,896]{2,1,0:T(8,128)(2,1)}), bf16[8,128,896]{2,1,0:T(8,128)(2,1)S(1)}, u32[]{:S(2)}, u32[]{:S(2)}) async-start(bf16[8,128,896]{2,1,0:T(8,128)(2,1)} %pack.1), calls=%async_computation | async-start | bytes 3670016 | tf_op jit(solution)/shard_map/all_to_all | solution.py:606
  14.7 92.0 %reduce-scatter.2.cloned.1.call-start = ((), (), s32[]{:S(2)}) async-start(), calls=%async_computation.6 | async-start | bytes 9437184 | tf_op jit(solution)/shard_map/reduce_scatter | solution.py:607
  54.1 0.7 copy-start.3
  54.1 52.6 %copy-start = (bf16[1,128,4096]{2,1,0:T(8,128)(2,1)S(1)}, bf16[1,128,4096]{2,1,0:T(8,128)(2,1)}, u32[]{:S(2)}) copy-start(bf16[1,128,4096]{2,1,0:T(8,128)(2,1)} %param.14) | copy-start | bytes 3145732
  54.1 52.6 %copy-start.2 = (f32[4096]{0:T(1024)S(1)}, f32[4096]{0:T(1024)}, u32[]{:S(2)}) copy-start(f32[4096]{0:T(1024)} %param.22) | copy-start | bytes 49156
  112.4 59.6 %all-to-all-start.3 = ((bf16[128,8,2048]{2,1,0:T(8,128)(2,1)}), bf16[128,8,2048]{2,1,0:T(8,128)(2,1)}, u32[]{:S(2)}, u32[]{:S(2)}) async-start(bf16[128,8,2048]{2,1,0:T(8,128)(2,1)} %bitcast.19), calls=%async_computation.4 | async-start | bytes 8388608 | tf_op jit(solution)/shard_map/all_to_all | solution.py:617
  172.0 68.4 %all-to-all-start.1 = ((bf16[128,8,2560]{2,1,0:T(8,128)(2,1)}), bf16[128,8,2560]{2,1,0:T(8,128)(2,1)}, u32[]{:S(2)}, u32[]{:S(2)}) async-start(bf16[128,8,2560]{2,1,0:T(8,128)(2,1)} %bitcast.17), calls=%async_computation.2 | async-start | bytes 10485760 | tf_op jit(solution)/shard_map/all_to_all | solution.py:617
  240.4 57.1 %all-to-all-start.4 = ((bf16[128,8,2048]{2,1,0:T(8,128)(2,1)}), bf16[128,8,2048]{2,1,0:T(8,128)(2,1)}, u32[]{:S(2)}, u32[]{:S(2)}) async-start(bf16[128,8,2048]{2,1,0:T(8,128)(2,1)} %bitcast.18), calls=%async_computation.5 | async-start | bytes 8388608 | tf_op jit(solution)/shard_map/all_to_all | solution.py:617
  297.5 6.2 %copy-start.1 = (bf16[4096,128]{1,0:T(8,128)(2,1)S(1)}, bf16[4096,128]{1,0:T(8,128)(2,1)}, u32[]{:S(2)}) copy-start(bf16[4096,128]{1,0:T(8,128)(2,1)} %router_ref.1) | copy-start | bytes 3145732
  297.5 68.4 %all-to-all-start.2 = ((bf16[128,8,2560]{2,1,0:T(8,128)(2,1)}), bf16[128,8,2560]{2,1,0:T(8,128)(2,1)}, u32[]{:S(2)}, u32[]{:S(2)}) async-start(bf16[128,8,2560]{2,1,0:T(8,128)(2,1)} %bitcast.16), calls=%async_computation.3 | async-start | bytes 10485760 | tf_op jit(solution)/shard_map/all_to_all | solution.py:617
Sparse Core Ops, SparseCore 0:
  54.3 52.3 reduce-scatter.1

commit v5 on v4

--- a/solution.py
+++ b/solution.py
@@ -142,7 +142,7 @@
     out_ref[...] = dot(att_ref[...], out_weight_ref[...]).astype(jnp.bfloat16)
 
 
-def attend(length, packed, out_weight, rows=256):
+def attend(length, packed, out_weight, rows=512):
     parts, tokens, columns = packed.shape
     lanes, width = out_weight.shape
     span = parts * tokens
@@ -152,7 +152,7 @@
         grid=(span // rows,),
         in_specs=[
             pl.BlockSpec(memory_space=pltpu.SMEM),
-            pl.BlockSpec((parts, tokens, columns), lambda i: (0, 0, 0)),
+            pl.BlockSpec(memory_space=pltpu.VMEM),
             pl.BlockSpec(memory_space=pltpu.HBM),
         ],
         out_specs=pl.BlockSpec((rows, width), lambda i: (i, 0)),
@@ -248,7 +248,7 @@
             ).astype(jnp.bfloat16)
 
 
-def route_first(resid, projected, gain, pick, cols=512):
+def route_first(resid, projected, gain, pick, cols=1024):
     tokens, width = resid.shape
     rows, twice = pick.shape[1:]
     half = width // 2
@@ -530,9 +530,10 @@
 ):
     step = pl.program_id(0)
     tall, cols = rows_ref.shape
-    tokens = out_ref.shape[0]
+    small = extra_ref.shape[1]
+    tokens, width = out_ref.shape
     groups, few = tall // GROUP, GROUP // SLOTS
-    steps = SLOTS // 2
+    half = width // 2
 
     @pl.when(step == 0)
     def _():
@@ -540,34 +541,35 @@
         for g in range(groups):
             pieces = dot(order, extra_ref[g * GROUP : (g + 1) * GROUP, :]).astype(jnp.bfloat16)
             for j in range(SLOTS):
-                piece_ref[j, g * few : (g + 1) * few, :] = pieces[j * few : (j + 1) * few]
-
-    for j in range(steps):
+                piece_ref[g * few : (g + 1) * few, j * small : (j + 1) * small] = pieces[
+                    j * few : (j + 1) * few
+                ]
+
+    for j in range(half // cols):
 
         @pl.when(step == j)
         def _():
             for side, ref in enumerate((first_ref, second_ref)):
-                piece = side * steps + j
+                lanes = slice(side * half + j * cols, side * half + (j + 1) * cols)
                 both = dot(weight_ref[0, side], rows_ref[...]) + dot(
-                    ninth_ref[...], piece_ref[piece]
+                    ninth_ref[...], piece_ref[:, lanes]
                 )
-                out_ref[:, piece * cols : (piece + 1) * cols] = (
-                    ref[...] + (both[:tokens] + both[tokens:])
-                ).astype(jnp.bfloat16)
-
-
-def combine_second(rows, main_weight, ninth_weight, first, second):
+                out_ref[:, lanes] = (ref[...] + (both[:tokens] + both[tokens:])).astype(
+                    jnp.bfloat16
+                )
+
+
+def combine_second(rows, main_weight, ninth_weight, first, second, cols=1024):
     tokens, half = first.shape
     tall = rows.shape[0]
-    cols = 2 * half // SLOTS
-    steps = half // cols
+    small = 2 * half // SLOTS
     part = pl.BlockSpec((tokens, cols), lambda j: (0, j))
     return pl.pallas_call(
         combine_second_kernel,
-        grid=(steps,),
+        grid=(half // cols,),
         in_specs=[
             pl.BlockSpec((tall, cols), lambda j: (0, j)),
-            pl.BlockSpec((tall, cols), lambda j: (0, steps)),
+            pl.BlockSpec((tall, small), lambda j: (0, half // small)),
             pl.BlockSpec((1,) + main_weight.shape[1:], lambda j: (1, 0, 0, 0)),
             pl.BlockSpec(ninth_weight.shape, lambda j: (0, 0)),
             part,
@@ -575,7 +577,7 @@
         ],
         out_specs=pl.BlockSpec((tokens, 2 * half), lambda j: (0, 0)),
         out_shape=jax.ShapeDtypeStruct((tokens, 2 * half), jnp.bfloat16),
-        scratch_shapes=[pltpu.VMEM((SLOTS, tall // SLOTS, cols), jnp.bfloat16)],
+        scratch_shapes=[pltpu.VMEM((tall // SLOTS, 2 * half), jnp.bfloat16)],
         compiler_params=pltpu.CompilerParams(vmem_limit_bytes=32 * MIB),
         name="combine_second",
     )(rows, rows, main_weight, ninth_weight, first, second)

time: 382 us -> 380 us (level)
  transfers between devices with their start and end apart: 6 -> 6, of which waited for: 6 -> 6; matrix products, arithmetic and copies ran while one was open for 0% -> 0% of each run, Pallas kernels for 16% -> 17%
where the time goes in v5:
time: 380 us; the launch traced here: 378 us
  waiting for transfers between devices  237 us (62%)
  Pallas kernels  92.1 us (24%)
  starting transfers between devices  33.3 us (9%)
  between operations  14.1 us (4%)
    all_to_all x4, waiting for transfers between devices, exchange(): lax.all_to_all(blocks, ('seq', 'exp'), split_axis=0, concat_axis=0, tiled...  166 us
    reduce_scatter x1, waiting for transfers between devices, per_device(): lax.psum_scatter(attend(prefix_len, packed, in_hbm(out_weight)), 'seq', s...  48.5 us
    pallas_call x2, Pallas kernels, expert(): pl.pallas_call(functools.partial(expert_kernel, deep=deep, ninth=ninth),...  44.1 us
    all_to_all x4, starting transfers between devices, exchange(): lax.all_to_all(blocks, ('seq', 'exp'), split_axis=0, concat_axis=0, tiled...  28.1 us
    all_to_all x1, waiting for transfers between devices, per_device(): lax.all_to_all(packed, 'seq', split_axis=0, concat_axis=0, tiled=True)  22.9 us
    pallas_call x1, Pallas kernels, attend(): pl.pallas_call(attend_kernel, grid=(span // rows,), in_specs=[pl.BlockSpe...  14.7 us
  transfers between devices with their start and end apart: 6, of which 6 were waited for; matrix products, arithmetic and copies ran while one was open for 0% of the time, Pallas kernels for 17%

profile of v5, /device:TPU:5, one launch (start us, length us, event | category | flops | bytes accessed | tf_op | source)
XLA Modules:
  0.0 377.8 jit_solution(5236738565136228123)
XLA Ops:
  6.5 3.0 pack.1
  9.5 5.2 %all-to-all-start = ((bf16[8,128,896]{2,1,0:T(8,128)(2,1)}), bf16[8,128,896]{2,1,0:T(8,128)(2,1)S(1)}, u32[]{:S(2)}, u32[]{:S(2)}) async-start(bf16[8,128,896]{2,1,0:T(8,128)(2,1)} %pack.1), calls=%async_computation | async-start | bytes 3670016 | tf_op jit(solution)/shard_map/all_to_all | solution.py:608
  14.7 0.0 reduce-scatter.2.cloned.1.call-start
  15.3 22.9 %all-to-all-done.packed_ref = bf16[8,128,896]{2,1,0:T(8,128)(2,1)S(1)} async-done(((bf16[8,128,896]{2,1,0:T(8,128)(2,1)}), bf16[8,128,896]{2,1,0:T(8,128)(2,1)S(1)}, u32[]{:S(2)}, u32[]{:S(2)}) %all-to-all-start) | async-done | bytes 1835040 | tf_op jit(solution)/shard_map/all_to_all | solution.py:608
  38.2 14.7 %attend.1 = bf16[1024,4096]{1,0:T(8,128)(2,1)} custom-call(s32[1]{0:T(128)S(6)} %copy.16.length_ref, bf16[8,128,896]{2,1,0:T(8,128)(2,1)S(1)} %all-to-all-done.packed_ref, bf16[512,4096]{1,0:T(8,128)(2,1)} %out_weight_hbm.1), custom_call_target="tpu_custom_call" | custom-call | tf_op jit(solution)/shard_map/attend/pallas_call | solution.py:150
  52.9 0.0 copy-start.3
  52.9 0.0 copy-start
  52.9 0.0 copy-start.2
  52.9 0.0 reduce-scatter.2.cloned.1.call-update
  53.0 0.6 copy-done.3
  53.6 0.7 copy.15
  54.3 2.7 plan.1
  57.0 48.5 %reduce-scatter.2.cloned.1.call-done.proj_ref.refs_2_.refs_3_ = bf16[128,4096]{1,0:T(8,128)(2,1)} async-done(((bf16[1024,4096]{1,0:T(8,128)(2,1)}), bf16[128,4096]{1,0:T(8,128)(2,1)}) %reduce-scatter.2.cloned.1.call-update) | async-done | bytes 1048592 | tf_op jit(solution)/shard_map/reduce_scatter | solution.py:609
  105.5 0.0 copy-done
  105.5 0.0 copy-done.2
  105.5 5.1 %route_first.1 = (bf16[1024,2048]{1,0:T(8,128)(2,1)}, bf16[256,2048]{1,0:T(8,128)(2,1)}) custom-call(bf16[128,4096]{1,0:T(8,128)(2,1)S(1)} %bitcast.12, bf16[128,4096]{1,0:T(8,128)(2,1)} %reduce-scatter.2.cloned.1.call-done.proj_ref.refs_2_.refs_3_, f32[1,4096]{1,0:T(1,128)S(1)} %bitcast.15, bf16[2,1024,256]{2,1,0:T(8,128)(2,1)} %get-tuple-element.14.pick_ref), custom_call_target="tpu_custom_call" | custom-call | tf_op jit(solution)/shard_map/route_first/pallas_call | solution.py:256
  110.6 9.1 %all-to-all-start.3 = ((bf16[128,8,2048]{2,1,0:T(8,128)(2,1)}), bf16[128,8,2048]{2,1,0:T(8,128)(2,1)}, u32[]{:S(2)}, u32[]{:S(2)}) async-start(bf16[128,8,2048]{2,1,0:T(8,128)(2,1)} %bitcast.19), calls=%async_computation.4 | async-start | bytes 8388608 | tf_op jit(solution)/shard_map/all_to_all | solution.py:619
  119.7 6.0 %route_second.1 = bf16[1024,2560]{1,0:T(8,128)(2,1)} custom-call(bf16[256,2048]{1,0:T(8,128)(2,1)} %get-tuple-element.15.halves_ref, bf16[2,1024,256]{2,1,0:T(8,128)(2,1)} %get-tuple-element.14.pick_ref, bf16[128,128]{1,0:T(8,128)(2,1)} %get-tuple-element.16.ninth_ref), custom_call_target="tpu_custom_call" | custom-call | tf_op jit(solution)/shard_map/route_second/pallas_call | solution.py:306
  125.6 44.6 %all-to-all-done.3 = bf16[128,8,2048]{2,1,0:T(8,128)(2,1)} async-done(((bf16[128,8,2048]{2,1,0:T(8,128)(2,1)}), bf16[128,8,2048]{2,1,0:T(8,128)(2,1)}, u32[]{:S(2)}, u32[]{:S(2)}) %all-to-all-start.3) | async-done | bytes 4194336 | tf_op jit(solution)/shard_map/all_to_all | solution.py:619
  170.2 6.2 %all-to-all-start.1 = ((bf16[128,8,2560]{2,1,0:T(8,128)(2,1)}), bf16[128,8,2560]{2,1,0:T(8,128)(2,1)}, u32[]{:S(2)}, u32[]{:S(2)}) async-start(bf16[128,8,2560]{2,1,0:T(8,128)(2,1)} %bitcast.17), calls=%async_computation.2 | async-start | bytes 10485760 | tf_op jit(solution)/shard_map/all_to_all | solution.py:619
  176.4 20.4 %expert_first.1 = bf16[1024,2048]{1,0:T(8,128)(2,1)} custom-call(bf16[1024,2048]{1,0:T(8,128)(2,1)} %bitcast.8.refs_0_, bf16[1,4096,768]{2,1,0:T(8,128)(2,1)} %refs_1_.3, bf16[1,4096,768]{2,1,0:T(8,128)(2,1)} %refs_2_.3, bf16[1,768,4096]{2,1,0:T(8,128)(2,1)} %refs_4_.3, bf16[1,768,4096]{2,1,0:T(8,128)(2,1)} %refs_4_.3), custom_call_target="tpu_custom_call" | custom-call | tf_op jit(solution)/shard_map/expert_first/pallas_call | solution.py:469
  196.8 41.8 %all-to-all-done.1 = bf16[128,8,2560]{2,1,0:T(8,128)(2,1)} async-done(((bf16[128,8,2560]{2,1,0:T(8,128)(2,1)}), bf16[128,8,2560]{2,1,0:T(8,128)(2,1)}, u32[]{:S(2)}, u32[]{:S(2)}) %all-to-all-start.1) | async-done | bytes 5242912 | tf_op jit(solution)/shard_map/all_to_all | solution.py:619
  238.6 6.6 %all-to-all-start.4 = ((bf16[128,8,2048]{2,1,0:T(8,128)(2,1)}), bf16[128,8,2048]{2,1,0:T(8,128)(2,1)}, u32[]{:S(2)}, u32[]{:S(2)}) async-start(bf16[128,8,2048]{2,1,0:T(8,128)(2,1)} %bitcast.18), calls=%async_computation.5 | async-start | bytes 8388608 | tf_op jit(solution)/shard_map/all_to_all | solution.py:619
  245.2 23.7 %expert_second.1 = bf16[1024,2560]{1,0:T(8,128)(2,1)} custom-call(bf16[1024,2560]{1,0:T(8,128)(2,1)} %bitcast.4.refs_0_, bf16[1,4096,768]{2,1,0:T(8,128)(2,1)} %refs_1_.3, bf16[1,4096,768]{2,1,0:T(8,128)(2,1)} %refs_2_.3, bf16[1,768,4096]{2,1,0:T(8,128)(2,1)} %refs_4_.3, bf16[1,768,4096]{2,1,0:T(8,128)(2,1)} %refs_4_.3), custom_call_target="tpu_custom_call" | custom-call | tf_op jit(solution)/shard_map/expert_second/pallas_call | solution.py:469
  268.9 26.9 %all-to-all-done.4 = bf16[128,8,2048]{2,1,0:T(8,128)(2,1)} async-done(((bf16[128,8,2048]{2,1,0:T(8,128)(2,1)}), bf16[128,8,2048]{2,1,0:T(8,128)(2,1)}, u32[]{:S(2)}, u32[]{:S(2)}) %all-to-all-start.4) | async-done | bytes 4194336 | tf_op jit(solution)/shard_map/all_to_all | solution.py:619
  295.7 0.0 copy-start.1
  295.7 6.2 %all-to-all-start.2 = ((bf16[128,8,2560]{2,1,0:T(8,128)(2,1)}), bf16[128,8,2560]{2,1,0:T(8,128)(2,1)}, u32[]{:S(2)}, u32[]{:S(2)}) async-start(bf16[128,8,2560]{2,1,0:T(8,128)(2,1)} %bitcast.16), calls=%async_computation.3 | async-start | bytes 10485760 | tf_op jit(solution)/shard_map/all_to_all | solution.py:619
  302.0 0.0 copy-done.1
  302.0 3.7 weights.1
  305.7 6.0 %combine_first.1 = (f32[128,2048]{1,0:T(8,128)}, f32[128,2048]{1,0:T(8,128)}) custom-call(bf16[1024,2048]{1,0:T(8,128)(2,1)} %bitcast.10.rows_ref, bf16[2,2,256,1024]{3,2,1,0:T(8,128)(2,1)} %get-tuple-element.18.weight_ref, bf16[128,4096]{1,0:T(8,128)(2,1)S(1)} %bitcast.13, bf16[128,4096]{1,0:T(8,128)(2,1)S(1)} %bitcast.14, ...), custom_call_target="tpu_custom_call" | custom-call | tf_op jit(solution)/shard_map/combine_first/pallas_call | solution.py:510
  311.7 52.4 %all-to-all-done.2 = bf16[128,8,2560]{2,1,0:T(8,128)(2,1)} async-done(((bf16[128,8,2560]{2,1,0:T(8,128)(2,1)}), bf16[128,8,2560]{2,1,0:T(8,128)(2,1)}, u32[]{:S(2)}, u32[]{:S(2)}) %all-to-all-start.2) | async-done | bytes 5242912 | tf_op jit(solution)/shard_map/all_to_all | solution.py:619
  364.1 6.9 %combine_second.1 = bf16[128,4096]{1,0:T(8,128)(2,1)} custom-call(bf16[1024,2560]{1,0:T(8,128)(2,1)} %bitcast.6.rows_ref.extra_ref, bf16[1024,2560]{1,0:T(8,128)(2,1)} %bitcast.6.rows_ref.extra_ref, bf16[2,2,256,1024]{3,2,1,0:T(8,128)(2,1)} %get-tuple-element.18.weight_ref, bf16[256,128]{1,0:T(8,128)(2,1)} %get-tuple-element.19.ninth_ref, ...), custom_call_target="tpu_custom_call" | custom-call | tf_op jit(solution)/shard_map/combine_second/pallas_call | solution.py:567
Async XLA Ops:
  9.5 28.7 %all-to-all-start = ((bf16[8,128,896]{2,1,0:T(8,128)(2,1)}), bf16[8,128,896]{2,1,0:T(8,128)(2,1)S(1)}, u32[]{:S(2)}, u32[]{:S(2)}) async-start(bf16[8,128,896]{2,1,0:T(8,128)(2,1)} %pack.1), calls=%async_computation | async-start | bytes 3670016 | tf_op jit(solution)/shard_map/all_to_all | solution.py:608
  14.7 90.8 %reduce-scatter.2.cloned.1.call-start = ((), (), s32[]{:S(2)}) async-start(), calls=%async_computation.6 | async-start | bytes 9437184 | tf_op jit(solution)/shard_map/reduce_scatter | solution.py:609
  52.9 0.7 copy-start.3
  52.9 52.6 %copy-start = (bf16[1,128,4096]{2,1,0:T(8,128)(2,1)S(1)}, bf16[1,128,4096]{2,1,0:T(8,128)(2,1)}, u32[]{:S(2)}) copy-start(bf16[1,128,4096]{2,1,0:T(8,128)(2,1)} %param.14) | copy-start | bytes 3145732
  52.9 52.6 %copy-start.2 = (f32[4096]{0:T(1024)S(1)}, f32[4096]{0:T(1024)}, u32[]{:S(2)}) copy-start(f32[4096]{0:T(1024)} %param.22) | copy-start | bytes 49156
  110.6 59.6 %all-to-all-start.3 = ((bf16[128,8,2048]{2,1,0:T(8,128)(2,1)}), bf16[128,8,2048]{2,1,0:T(8,128)(2,1)}, u32[]{:S(2)}, u32[]{:S(2)}) async-start(bf16[128,8,2048]{2,1,0:T(8,128)(2,1)} %bitcast.19), calls=%async_computation.4 | async-start | bytes 8388608 | tf_op jit(solution)/shard_map/all_to_all | solution.py:619
  170.2 68.4 %all-to-all-start.1 = ((bf16[128,8,2560]{2,1,0:T(8,128)(2,1)}), bf16[128,8,2560]{2,1,0:T(8,128)(2,1)}, u32[]{:S(2)}, u32[]{:S(2)}) async-start(bf16[128,8,2560]{2,1,0:T(8,128)(2,1)} %bitcast.17), calls=%async_computation.2 | async-start | bytes 10485760 | tf_op jit(solution)/shard_map/all_to_all | solution.py:619
  238.6 57.1 %all-to-all-start.4 = ((bf16[128,8,2048]{2,1,0:T(8,128)(2,1)}), bf16[128,8,2048]{2,1,0:T(8,128)(2,1)}, u32[]{:S(2)}, u32[]{:S(2)}) async-start(bf16[128,8,2048]{2,1,0:T(8,128)(2,1)} %bitcast.18), calls=%async_computation.5 | async-start | bytes 8388608 | tf_op jit(solution)/shard_map/all_to_all | solution.py:619
  295.7 6.2 %copy-start.1 = (bf16[4096,128]{1,0:T(8,128)(2,1)S(1)}, bf16[4096,128]{1,0:T(8,128)(2,1)}, u32[]{:S(2)}) copy-start(bf16[4096,128]{1,0:T(8,128)(2,1)} %router_ref.1) | copy-start | bytes 3145732
  295.7 68.4 %all-to-all-start.2 = ((bf16[128,8,2560]{2,1,0:T(8,128)(2,1)}), bf16[128,8,2560]{2,1,0:T(8,128)(2,1)}, u32[]{:S(2)}, u32[]{:S(2)}) async-start(bf16[128,8,2560]{2,1,0:T(8,128)(2,1)} %bitcast.16), calls=%async_computation.3 | async-start | bytes 10485760 | tf_op jit(solution)/shard_map/all_to_all | solution.py:619
Sparse Core Ops, SparseCore 0:
  53.1 52.3 reduce-scatter.1

commit v6 on v5

--- a/solution.py
+++ b/solution.py
@@ -188,7 +188,7 @@
     return flags(owner == lax.broadcasted_iota(jnp.int32, shape, 1 - axis))
 
 
-def plan_kernel(ids_ref, rank_ref, pick_ref, ninth_ref):
+def plan_kernel(ids_ref, rank_ref, zero_ref, one_ref, ninth_ref):
     tokens, experts = rank_ref.shape
     named = named_mask(ids_ref, experts)
     earlier = flags(
@@ -203,8 +203,9 @@
     slot = (row % HALF).astype(jnp.float32)
     for chunk in range(2):
         hit = wide == slot + float(1 + HALF * chunk)
-        pick_ref[chunk, :, :tokens] = flags(hit & (row < HALF))
-        pick_ref[chunk, :, tokens:] = flags(hit & (row >= HALF))
+        pick_ref = (zero_ref, one_ref)[chunk]
+        pick_ref[:, :tokens] = flags(hit & (row < HALF))
+        pick_ref[:, tokens:] = flags(hit & (row >= HALF))
     same = flags(
         lax.broadcasted_iota(jnp.int32, (experts, experts), 0)
         == lax.broadcasted_iota(jnp.int32, (experts, experts), 1)
@@ -218,7 +219,8 @@
         plan_kernel,
         out_shape=[
             pltpu.HBM((tokens, experts), jnp.float32),
-            pltpu.HBM((2, experts * SLOTS, 2 * tokens), jnp.bfloat16),
+            pltpu.VMEM((experts * SLOTS, 2 * tokens), jnp.bfloat16),
+            pltpu.HBM((experts * SLOTS, 2 * tokens), jnp.bfloat16),
             pltpu.HBM((experts, tokens), jnp.bfloat16),
         ],
         name="plan",
@@ -244,23 +246,23 @@
         @pl.when(step == j)
         def _():
             send_ref[...] = dot(
-                pick_ref[0], halves_ref[:, j * cols : (j + 1) * cols]
+                pick_ref[...], halves_ref[:, j * cols : (j + 1) * cols]
             ).astype(jnp.bfloat16)
 
 
 def route_first(resid, projected, gain, pick, cols=1024):
     tokens, width = resid.shape
-    rows, twice = pick.shape[1:]
+    rows, twice = pick.shape
     half = width // 2
     whole = lambda shape: pl.BlockSpec(shape, lambda j: (0,) * len(shape))
     return pl.pallas_call(
         route_first_kernel,
         grid=(half // cols,),
         in_specs=[
+            pl.BlockSpec(memory_space=pltpu.VMEM),
             whole((tokens, width)),
-            whole((tokens, width)),
-            whole((1, width)),
-            whole((1, rows, twice)),
+            pl.BlockSpec(memory_space=pltpu.VMEM),
+            pl.BlockSpec(memory_space=pltpu.VMEM),
         ],
         out_specs=[pl.BlockSpec((rows, cols), lambda j: (0, j)), whole((twice, half))],
         out_shape=[
@@ -284,7 +286,7 @@
         @pl.when(step == j)
         def _():
             part = halves_ref[:, j * cols : (j + 1) * cols]
-            send_ref[...] = dot(pick_ref[0], part).astype(jnp.bfloat16)
+            send_ref[...] = dot(pick_ref[...], part).astype(jnp.bfloat16)
             for side in range(2):
                 piece = dot(ninth_ref[...], part[side * tokens : (side + 1) * tokens])
                 for b in range(cols // 128):
@@ -300,7 +302,7 @@
 
 def route_second(halves, pick, ninth):
     twice, half = halves.shape
-    rows = pick.shape[1]
+    rows = pick.shape[0]
     cols = 2 * half // SLOTS
     whole = lambda shape: pl.BlockSpec(shape, lambda j: (0,) * len(shape))
     return pl.pallas_call(
@@ -308,7 +310,7 @@
         grid=(half // cols + 1,),
         in_specs=[
             whole((twice, half)),
-            pl.BlockSpec((1, rows, twice), lambda j: (1, 0, 0)),
+            whole(pick.shape),
             whole(ninth.shape),
         ],
         out_specs=pl.BlockSpec((rows, cols), lambda j: (0, j)),
@@ -319,7 +321,7 @@
     )(halves, pick, ninth)
 
 
-def weights_kernel(halves_ref, router_ref, rank_ref, main_ref, ninth_ref):
+def weights_kernel(halves_ref, router_ref, rank_ref, zero_ref, one_ref, ninth_ref):
     tokens, experts = rank_ref.shape
     half = halves_ref.shape[1]
     rank = rank_ref[...]
@@ -341,8 +343,9 @@
         wide = dot(part, spread)
         for chunk in range(2):
             kept = jnp.where(wide_rank == slot + float(1 + HALF * chunk), wide, 0.0)
-            main_ref[chunk, 0, place, :] = jnp.where(row < HALF, kept, 0.0).astype(jnp.bfloat16)
-            main_ref[chunk, 1, place, :] = jnp.where(row >= HALF, kept, 0.0).astype(jnp.bfloat16)
+            main_ref = (zero_ref, one_ref)[chunk]
+            main_ref[0, place, :] = jnp.where(row < HALF, kept, 0.0).astype(jnp.bfloat16)
+            main_ref[1, place, :] = jnp.where(row >= HALF, kept, 0.0).astype(jnp.bfloat16)
         ninth_ref[place, :] = jnp.where(
             rank == SLOTS + 1.0, part.astype(jnp.float32), 0.0
         ).astype(jnp.bfloat16)
@@ -353,8 +356,9 @@
     return pl.pallas_call(
         weights_kernel,
         out_shape=[
-            pltpu.HBM((2, 2, 2 * tokens, experts * SLOTS), jnp.bfloat16),
-            pltpu.HBM((2 * tokens, experts), jnp.bfloat16),
+            pltpu.HBM((2, 2 * tokens, experts * SLOTS), jnp.bfloat16),
+            pltpu.VMEM((2, 2 * tokens, experts * SLOTS), jnp.bfloat16),
+            pltpu.VMEM((2 * tokens, experts), jnp.bfloat16),
         ],
         compiler_params=pltpu.CompilerParams(vmem_limit_bytes=32 * MIB),
         name="weights",
@@ -491,12 +495,12 @@
 
 
 def combine_first_kernel(rows_ref, weight_ref, *refs):
-    resids, projs, outs = refs[:2], refs[2:4], refs[4:]
-    tokens = outs[0].shape[0]
+    resids, projs, out_ref = refs[:2], refs[2:4], refs[4]
+    tokens = out_ref.shape[1]
     for side in range(2):
-        both = dot(weight_ref[0, side], rows_ref[...])
+        both = dot(weight_ref[side], rows_ref[...])
         hidden = resids[side][...].astype(jnp.float32) + projs[side][...].astype(jnp.float32)
-        outs[side][...] = hidden + (both[:tokens] + both[tokens:])
+        out_ref[side] = hidden + (both[:tokens] + both[tokens:])
 
 
 def combine_first(rows, main_weight, resid, projected):
@@ -506,81 +510,100 @@
     steps = half // cols
     first = pl.BlockSpec((tokens, cols), lambda j: (0, j))
     second = pl.BlockSpec((tokens, cols), lambda j: (0, steps + j))
-    shape = pltpu.HBM((tokens, half), jnp.float32)
     return pl.pallas_call(
         combine_first_kernel,
         grid=(steps,),
         in_specs=[
             pl.BlockSpec((tall, cols), lambda j: (0, j)),
-            pl.BlockSpec((1,) + main_weight.shape[1:], lambda j: (0, 0, 0, 0)),
+            pl.BlockSpec(main_weight.shape, lambda j: (0, 0, 0)),
             first,
             second,
             first,
             second,
         ],
-        out_specs=[first, first],
-        out_shape=[shape, shape],
+        out_specs=pl.BlockSpec((2, tokens, cols), lambda j: (0, 0, j)),
+        out_shape=pltpu.HBM((2, tokens, half), jnp.float32),
         compiler_params=pltpu.CompilerParams(vmem_limit_bytes=32 * MIB),
         name="combine_first",
     )(rows, main_weight, resid, resid, projected, projected)
 
 
 def combine_second_kernel(
-    rows_ref, extra_ref, weight_ref, ninth_ref, first_ref, second_ref, out_ref, piece_ref
+    rows_hbm, partial_hbm, weight_ref, ninth_ref, out_hbm,
+    rows_ref, partial_ref, out_ref, piece_ref, row_sems, partial_sems, out_sems,
 ):
-    step = pl.program_id(0)
-    tall, cols = rows_ref.shape
-    small = extra_ref.shape[1]
-    tokens, width = out_ref.shape
+    tall, columns = rows_hbm.shape
+    tokens, width = out_hbm.shape
+    half = width // 2
+    small = columns - half
+    steps = half // small
     groups, few = tall // GROUP, GROUP // SLOTS
-    half = width // 2
-
-    @pl.when(step == 0)
-    def _():
-        order = sort_pieces()
-        for g in range(groups):
-            pieces = dot(order, extra_ref[g * GROUP : (g + 1) * GROUP, :]).astype(jnp.bfloat16)
-            for j in range(SLOTS):
-                piece_ref[g * few : (g + 1) * few, j * small : (j + 1) * small] = pieces[
-                    j * few : (j + 1) * few
-                ]
-
-    for j in range(half // cols):
-
-        @pl.when(step == j)
-        def _():
-            for side, ref in enumerate((first_ref, second_ref)):
-                lanes = slice(side * half + j * cols, side * half + (j + 1) * cols)
-                both = dot(weight_ref[0, side], rows_ref[...]) + dot(
-                    ninth_ref[...], piece_ref[:, lanes]
-                )
-                out_ref[:, lanes] = (ref[...] + (both[:tokens] + both[tokens:])).astype(
-                    jnp.bfloat16
-                )
-
-
-def combine_second(rows, main_weight, ninth_weight, first, second, cols=1024):
-    tokens, half = first.shape
-    tall = rows.shape[0]
-    small = 2 * half // SLOTS
-    part = pl.BlockSpec((tokens, cols), lambda j: (0, j))
+
+    def rows_copy(j):
+        lanes = pl.ds(j * small, small)
+        return pltpu.make_async_copy(rows_hbm.at[:, lanes], rows_ref.at[j], row_sems.at[j])
+
+    def partial_copy(j):
+        lanes = pl.ds(j * small, small)
+        return pltpu.make_async_copy(
+            partial_hbm.at[:, :, lanes], partial_ref.at[j], partial_sems.at[j]
+        )
+
+    def out_copy(piece):
+        lanes = pl.ds(piece * small, small)
+        return pltpu.make_async_copy(out_ref.at[piece], out_hbm.at[:, lanes], out_sems.at[piece])
+
+    rows_copy(steps).start()
+    for j in range(steps):
+        rows_copy(j).start()
+        partial_copy(j).start()
+    rows_copy(steps).wait()
+    order = sort_pieces()
+    for g in range(groups):
+        pieces = dot(order, rows_ref[steps, g * GROUP : (g + 1) * GROUP, :]).astype(jnp.bfloat16)
+        for j in range(SLOTS):
+            piece_ref[j, g * few : (g + 1) * few, :] = pieces[j * few : (j + 1) * few]
+    for j in range(steps):
+        rows_copy(j).wait()
+        partial_copy(j).wait()
+        for side in range(2):
+            piece = side * steps + j
+            both = dot(weight_ref[side], rows_ref[j]) + dot(ninth_ref[...], piece_ref[piece])
+            out_ref[piece] = (partial_ref[j, side] + (both[:tokens] + both[tokens:])).astype(
+                jnp.bfloat16
+            )
+            out_copy(piece).start()
+    for piece in range(2 * steps):
+        out_copy(piece).wait()
+
+
+def combine_second(rows, main_weight, ninth_weight, partial):
+    _, tokens, half = partial.shape
+    tall, columns = rows.shape
+    small = columns - half
+    steps = half // small
     return pl.pallas_call(
         combine_second_kernel,
-        grid=(half // cols,),
         in_specs=[
-            pl.BlockSpec((tall, cols), lambda j: (0, j)),
-            pl.BlockSpec((tall, small), lambda j: (0, half // small)),
-            pl.BlockSpec((1,) + main_weight.shape[1:], lambda j: (1, 0, 0, 0)),
-            pl.BlockSpec(ninth_weight.shape, lambda j: (0, 0)),
-            part,
-            part,
-        ],
-        out_specs=pl.BlockSpec((tokens, 2 * half), lambda j: (0, 0)),
+            pl.BlockSpec(memory_space=pltpu.HBM),
+            pl.BlockSpec(memory_space=pltpu.HBM),
+            pl.BlockSpec(memory_space=pltpu.VMEM),
+            pl.BlockSpec(memory_space=pltpu.VMEM),
+        ],
+        out_specs=pl.BlockSpec(memory_space=pltpu.HBM),
         out_shape=jax.ShapeDtypeStruct((tokens, 2 * half), jnp.bfloat16),
-        scratch_shapes=[pltpu.VMEM((tall // SLOTS, 2 * half), jnp.bfloat16)],
+        scratch_shapes=[
+            pltpu.VMEM((steps + 1, tall, small), jnp.bfloat16),
+            pltpu.VMEM((steps, 2, tokens, small), jnp.float32),
+            pltpu.VMEM((2 * steps, tokens, small), jnp.bfloat16),
+            pltpu.VMEM((SLOTS, tall // SLOTS, small), jnp.bfloat16),
+            pltpu.SemaphoreType.DMA((steps + 1,)),
+            pltpu.SemaphoreType.DMA((steps,)),
+            pltpu.SemaphoreType.DMA((2 * steps,)),
+        ],
         compiler_params=pltpu.CompilerParams(vmem_limit_bytes=32 * MIB),
         name="combine_second",
-    )(rows, rows, main_weight, ninth_weight, first, second)
+    )(rows, partial, main_weight, ninth_weight)
 
 
 def per_device(
@@ -610,8 +633,9 @@
         attend(prefix_len, packed, in_hbm(out_weight)), "seq", scatter_dimension=0, tiled=True
     )
     projected = in_hbm(projected)
-    rank, pick, ninth = [in_hbm(x) for x in plan(expert_ids[0], experts)]
-    send_first, halves = route_first(resid[0], projected, norm_gain.reshape(1, width), pick)
+    rank, pick_first, pick_second, ninth = plan(expert_ids[0], experts)
+    rank, pick_second, ninth = in_hbm(rank), in_hbm(pick_second), in_hbm(ninth)
+    send_first, halves = route_first(resid[0], projected, norm_gain.reshape(1, width), pick_first)
 
     def exchange(rows):
         blocks = rows.reshape(experts, SLOTS, rows.shape[1])
@@ -624,14 +648,12 @@
     halves = in_hbm(halves)
     w_gate, w_up, w_down = in_hbm(w_gate), in_hbm(w_up), in_hbm(w_down)
     got_first = exchange(send_first)
-    got_second = exchange(route_second(halves, pick, ninth))
-    main_weight, ninth_weight = [in_hbm(x) for x in weights(halves, router_weight, rank)]
+    got_second = exchange(route_second(halves, pick_second, ninth))
+    first_weight, second_weight, ninth_weight = weights(halves, router_weight, rank)
     back_first = exchange(expert(got_first, w_gate, w_up, w_down, False))
     back_second = exchange(expert(got_second, w_gate, w_up, w_down, True))
-    first, second = combine_first(back_first, main_weight, resid[0], projected)
-    return combine_second(
-        back_second, main_weight, ninth_weight, in_hbm(first), in_hbm(second)
-    )[None]
+    partial = combine_first(back_first, in_hbm(first_weight), resid[0], projected)
+    return combine_second(back_second, second_weight, ninth_weight, in_hbm(partial))[None]
 
 
 def solution(mesh):

time: 380 us -> 379 us (level)
  no operation moved by 1% of the time
where the time goes in v6:
time: 379 us; the launch traced here: 377 us
  waiting for transfers between devices  236 us (62%)
  Pallas kernels  90.6 us (24%)
  starting transfers between devices  33.3 us (9%)
  between operations  14.1 us (4%)
    all_to_all x4, waiting for transfers between devices, exchange(): lax.all_to_all(blocks, ('seq', 'exp'), split_axis=0, concat_axis=0, tiled...  164 us
    reduce_scatter x1, waiting for transfers between devices, per_device(): lax.psum_scatter(attend(prefix_len, packed, in_hbm(out_weight)), 'seq', s...  48.6 us
    pallas_call x2, Pallas kernels, expert(): pl.pallas_call(functools.partial(expert_kernel, deep=deep, ninth=ninth),...  44.1 us
    all_to_all x4, starting transfers between devices, exchange(): lax.all_to_all(blocks, ('seq', 'exp'), split_axis=0, concat_axis=0, tiled...  28.1 us
    all_to_all x1, waiting for transfers between devices, per_device(): lax.all_to_all(packed, 'seq', split_axis=0, concat_axis=0, tiled=True)  22.9 us
    pallas_call x1, Pallas kernels, attend(): pl.pallas_call(attend_kernel, grid=(span // rows,), in_specs=[pl.BlockSpe...  14.7 us
  transfers between devices with their start and end apart: 6, of which 6 were waited for; matrix products, arithmetic and copies ran while one was open for 0% of the time, Pallas kernels for 17%

profile of v6, /device:TPU:5, one launch (start us, length us, event | category | flops | bytes accessed | tf_op | source)
XLA Modules:
  0.0 376.5 jit_solution(678325466938676077)
XLA Ops:
  6.5 3.0 pack.1
  9.5 5.2 %all-to-all-start = ((bf16[8,128,896]{2,1,0:T(8,128)(2,1)}), bf16[8,128,896]{2,1,0:T(8,128)(2,1)S(1)}, u32[]{:S(2)}, u32[]{:S(2)}) async-start(bf16[8,128,896]{2,1,0:T(8,128)(2,1)} %pack.1), calls=%async_computation | async-start | bytes 3670016 | tf_op jit(solution)/shard_map/all_to_all | solution.py:631
  14.7 0.0 reduce-scatter.2.cloned.1.call-start
  15.3 22.9 %all-to-all-done.packed_ref = bf16[8,128,896]{2,1,0:T(8,128)(2,1)S(1)} async-done(((bf16[8,128,896]{2,1,0:T(8,128)(2,1)}), bf16[8,128,896]{2,1,0:T(8,128)(2,1)S(1)}, u32[]{:S(2)}, u32[]{:S(2)}) %all-to-all-start) | async-done | bytes 1835040 | tf_op jit(solution)/shard_map/all_to_all | solution.py:631
  38.2 14.7 %attend.1 = bf16[1024,4096]{1,0:T(8,128)(2,1)} custom-call(s32[1]{0:T(128)S(6)} %copy.16.length_ref, bf16[8,128,896]{2,1,0:T(8,128)(2,1)S(1)} %all-to-all-done.packed_ref, bf16[512,4096]{1,0:T(8,128)(2,1)} %out_weight_hbm.1), custom_call_target="tpu_custom_call" | custom-call | tf_op jit(solution)/shard_map/attend/pallas_call | solution.py:150
  52.9 0.0 copy-start.3
  52.9 0.0 copy-start
  52.9 0.0 copy-start.2
  52.9 0.0 reduce-scatter.2.cloned.1.call-update
  52.9 0.6 copy-done.3
  53.6 0.7 copy.15
  54.3 2.5 plan.1
  56.8 48.6 %reduce-scatter.2.cloned.1.call-done.proj_ref.refs_2_.refs_3_ = bf16[128,4096]{1,0:T(8,128)(2,1)} async-done(((bf16[1024,4096]{1,0:T(8,128)(2,1)}), bf16[128,4096]{1,0:T(8,128)(2,1)}) %reduce-scatter.2.cloned.1.call-update) | async-done | bytes 1048592 | tf_op jit(solution)/shard_map/reduce_scatter | solution.py:632
  105.5 0.0 copy-done
  105.5 0.0 copy-done.2
  105.5 4.9 %route_first.1 = (bf16[1024,2048]{1,0:T(8,128)(2,1)}, bf16[256,2048]{1,0:T(8,128)(2,1)}) custom-call(bf16[128,4096]{1,0:T(8,128)(2,1)S(1)} %bitcast.12, bf16[128,4096]{1,0:T(8,128)(2,1)} %reduce-scatter.2.cloned.1.call-done.proj_ref.refs_2_.refs_3_, f32[1,4096]{1,0:T(1,128)S(1)} %bitcast.15, bf16[1024,256]{1,0:T(8,128)(2,1)S(1)} %get-tuple-element.14.pick_ref), custom_call_target="tpu_custom_call" | custom-call | tf_op jit(solution)/shard_map/route_first/pallas_call | solution.py:258
  110.3 9.1 %all-to-all-start.3 = ((bf16[128,8,2048]{2,1,0:T(8,128)(2,1)}), bf16[128,8,2048]{2,1,0:T(8,128)(2,1)}, u32[]{:S(2)}, u32[]{:S(2)}) async-start(bf16[128,8,2048]{2,1,0:T(8,128)(2,1)} %bitcast.19), calls=%async_computation.4 | async-start | bytes 8388608 | tf_op jit(solution)/shard_map/all_to_all | solution.py:643
  119.4 6.0 %route_second.1 = bf16[1024,2560]{1,0:T(8,128)(2,1)} custom-call(bf16[256,2048]{1,0:T(8,128)(2,1)} %get-tuple-element.15.halves_ref, bf16[1024,256]{1,0:T(8,128)(2,1)} %get-tuple-element.16.pick_ref, bf16[128,128]{1,0:T(8,128)(2,1)} %get-tuple-element.17.ninth_ref), custom_call_target="tpu_custom_call" | custom-call | tf_op jit(solution)/shard_map/route_second/pallas_call | solution.py:308
  125.4 44.6 %all-to-all-done.3 = bf16[128,8,2048]{2,1,0:T(8,128)(2,1)} async-done(((bf16[128,8,2048]{2,1,0:T(8,128)(2,1)}), bf16[128,8,2048]{2,1,0:T(8,128)(2,1)}, u32[]{:S(2)}, u32[]{:S(2)}) %all-to-all-start.3) | async-done | bytes 4194336 | tf_op jit(solution)/shard_map/all_to_all | solution.py:643
  169.9 6.2 %all-to-all-start.1 = ((bf16[128,8,2560]{2,1,0:T(8,128)(2,1)}), bf16[128,8,2560]{2,1,0:T(8,128)(2,1)}, u32[]{:S(2)}, u32[]{:S(2)}) async-start(bf16[128,8,2560]{2,1,0:T(8,128)(2,1)} %bitcast.17), calls=%async_computation.2 | async-start | bytes 10485760 | tf_op jit(solution)/shard_map/all_to_all | solution.py:643
  176.2 20.4 %expert_first.1 = bf16[1024,2048]{1,0:T(8,128)(2,1)} custom-call(bf16[1024,2048]{1,0:T(8,128)(2,1)} %bitcast.8.refs_0_, bf16[1,4096,768]{2,1,0:T(8,128)(2,1)} %refs_1_.3, bf16[1,4096,768]{2,1,0:T(8,128)(2,1)} %refs_2_.3, bf16[1,768,4096]{2,1,0:T(8,128)(2,1)} %refs_4_.3, bf16[1,768,4096]{2,1,0:T(8,128)(2,1)} %refs_4_.3), custom_call_target="tpu_custom_call" | custom-call | tf_op jit(solution)/shard_map/expert_first/pallas_call | solution.py:473
  196.5 41.8 %all-to-all-done.1 = bf16[128,8,2560]{2,1,0:T(8,128)(2,1)} async-done(((bf16[128,8,2560]{2,1,0:T(8,128)(2,1)}), bf16[128,8,2560]{2,1,0:T(8,128)(2,1)}, u32[]{:S(2)}, u32[]{:S(2)}) %all-to-all-start.1) | async-done | bytes 5242912 | tf_op jit(solution)/shard_map/all_to_all | solution.py:643
  238.3 6.6 %all-to-all-start.4 = ((bf16[128,8,2048]{2,1,0:T(8,128)(2,1)}), bf16[128,8,2048]{2,1,0:T(8,128)(2,1)}, u32[]{:S(2)}, u32[]{:S(2)}) async-start(bf16[128,8,2048]{2,1,0:T(8,128)(2,1)} %bitcast.18), calls=%async_computation.5 | async-start | bytes 8388608 | tf_op jit(solution)/shard_map/all_to_all | solution.py:643
  244.9 23.7 %expert_second.1 = bf16[1024,2560]{1,0:T(8,128)(2,1)} custom-call(bf16[1024,2560]{1,0:T(8,128)(2,1)} %bitcast.4.refs_0_, bf16[1,4096,768]{2,1,0:T(8,128)(2,1)} %refs_1_.3, bf16[1,4096,768]{2,1,0:T(8,128)(2,1)} %refs_2_.3, bf16[1,768,4096]{2,1,0:T(8,128)(2,1)} %refs_4_.3, bf16[1,768,4096]{2,1,0:T(8,128)(2,1)} %refs_4_.3), custom_call_target="tpu_custom_call" | custom-call | tf_op jit(solution)/shard_map/expert_second/pallas_call | solution.py:473
  268.6 26.8 %all-to-all-done.4 = bf16[128,8,2048]{2,1,0:T(8,128)(2,1)} async-done(((bf16[128,8,2048]{2,1,0:T(8,128)(2,1)}), bf16[128,8,2048]{2,1,0:T(8,128)(2,1)}, u32[]{:S(2)}, u32[]{:S(2)}) %all-to-all-start.4) | async-done | bytes 4194336 | tf_op jit(solution)/shard_map/all_to_all | solution.py:643
  295.5 6.2 %all-to-all-start.2 = ((bf16[128,8,2560]{2,1,0:T(8,128)(2,1)}), bf16[128,8,2560]{2,1,0:T(8,128)(2,1)}, u32[]{:S(2)}, u32[]{:S(2)}) async-start(bf16[128,8,2560]{2,1,0:T(8,128)(2,1)} %bitcast.16), calls=%async_computation.3 | async-start | bytes 10485760 | tf_op jit(solution)/shard_map/all_to_all | solution.py:643
  301.7 0.0 copy-start.1
  301.7 1.2 copy-done.1
  302.9 3.4 weights.1
  306.3 6.2 %combine_first.1.partial_hbm = f32[2,128,2048]{2,1,0:T(8,128)} custom-call(bf16[1024,2048]{1,0:T(8,128)(2,1)} %bitcast.10.rows_ref, bf16[2,256,1024]{2,1,0:T(8,128)(2,1)} %get-tuple-element.20.weight_ref, bf16[128,4096]{1,0:T(8,128)(2,1)S(1)} %bitcast.13, bf16[128,4096]{1,0:T(8,128)(2,1)S(1)} %bitcast.14, ...), custom_call_target="tpu_custom_call" | custom-call | tf_op jit(solution)/shard_map/combine_first/pallas_call | solution.py:513
  312.6 51.3 %all-to-all-done.2 = bf16[128,8,2560]{2,1,0:T(8,128)(2,1)} async-done(((bf16[128,8,2560]{2,1,0:T(8,128)(2,1)}), bf16[128,8,2560]{2,1,0:T(8,128)(2,1)}, u32[]{:S(2)}, u32[]{:S(2)}) %all-to-all-start.2) | async-done | bytes 5242912 | tf_op jit(solution)/shard_map/all_to_all | solution.py:643
  363.9 5.8 %combine_second.1 = bf16[128,4096]{1,0:T(8,128)(2,1)} custom-call(bf16[1024,2560]{1,0:T(8,128)(2,1)} %bitcast.6.rows_hbm, f32[2,128,2048]{2,1,0:T(8,128)} %combine_first.1.partial_hbm, bf16[2,256,1024]{2,1,0:T(8,128)(2,1)S(1)} %get-tuple-element.21.weight_ref, bf16[256,128]{1,0:T(8,128)(2,1)S(1)} %get-tuple-element.22.ninth_ref), custom_call_target="tpu_custom_call" | custom-call | tf_op jit(solution)/shard_map/combine_second/pallas_call | solution.py:585
Async XLA Ops:
  9.5 28.7 %all-to-all-start = ((bf16[8,128,896]{2,1,0:T(8,128)(2,1)}), bf16[8,128,896]{2,1,0:T(8,128)(2,1)S(1)}, u32[]{:S(2)}, u32[]{:S(2)}) async-start(bf16[8,128,896]{2,1,0:T(8,128)(2,1)} %pack.1), calls=%async_computation | async-start | bytes 3670016 | tf_op jit(solution)/shard_map/all_to_all | solution.py:631
  14.7 90.8 %reduce-scatter.2.cloned.1.call-start = ((), (), s32[]{:S(2)}) async-start(), calls=%async_computation.6 | async-start | bytes 9437184 | tf_op jit(solution)/shard_map/reduce_scatter | solution.py:632
  52.9 0.7 copy-start.3
  52.9 52.6 %copy-start = (bf16[1,128,4096]{2,1,0:T(8,128)(2,1)S(1)}, bf16[1,128,4096]{2,1,0:T(8,128)(2,1)}, u32[]{:S(2)}) copy-start(bf16[1,128,4096]{2,1,0:T(8,128)(2,1)} %param.14) | copy-start | bytes 3145732
  52.9 52.6 %copy-start.2 = (f32[4096]{0:T(1024)S(1)}, f32[4096]{0:T(1024)}, u32[]{:S(2)}) copy-start(f32[4096]{0:T(1024)} %param.22) | copy-start | bytes 49156
  110.3 59.6 %all-to-all-start.3 = ((bf16[128,8,2048]{2,1,0:T(8,128)(2,1)}), bf16[128,8,2048]{2,1,0:T(8,128)(2,1)}, u32[]{:S(2)}, u32[]{:S(2)}) async-start(bf16[128,8,2048]{2,1,0:T(8,128)(2,1)} %bitcast.19), calls=%async_computation.4 | async-start | bytes 8388608 | tf_op jit(solution)/shard_map/all_to_all | solution.py:643
  169.9 68.4 %all-to-all-start.1 = ((bf16[128,8,2560]{2,1,0:T(8,128)(2,1)}), bf16[128,8,2560]{2,1,0:T(8,128)(2,1)}, u32[]{:S(2)}, u32[]{:S(2)}) async-start(bf16[128,8,2560]{2,1,0:T(8,128)(2,1)} %bitcast.17), calls=%async_computation.2 | async-start | bytes 10485760 | tf_op jit(solution)/shard_map/all_to_all | solution.py:643
  238.3 57.1 %all-to-all-start.4 = ((bf16[128,8,2048]{2,1,0:T(8,128)(2,1)}), bf16[128,8,2048]{2,1,0:T(8,128)(2,1)}, u32[]{:S(2)}, u32[]{:S(2)}) async-start(bf16[128,8,2048]{2,1,0:T(8,128)(2,1)} %bitcast.18), calls=%async_computation.5 | async-start | bytes 8388608 | tf_op jit(solution)/shard_map/all_to_all | solution.py:643
  295.5 68.4 %all-to-all-start.2 = ((bf16[128,8,2560]{2,1,0:T(8,128)(2,1)}), bf16[128,8,2560]{2,1,0:T(8,128)(2,1)}, u32[]{:S(2)}, u32[]{:S(2)}) async-start(bf16[128,8,2560]{2,1,0:T(8,128)(2,1)} %bitcast.16), calls=%async_computation.3 | async-start | bytes 10485760 | tf_op jit(solution)/shard_map/all_to_all | solution.py:643
  301.7 1.2 copy-start.1
Sparse Core Ops, SparseCore 0:
  53.1 52.3 reduce-scatter.1

commit v7 on v6

--- a/solution.py
+++ b/solution.py
@@ -76,93 +76,111 @@
 
 
 def attend_kernel(
-    length_ref, packed_ref, out_weight_hbm, out_ref,
-    key_ref, value_ref, att_ref, out_weight_ref, sem,
+    length_ref, packed_ref, out_weight_hbm, out_hbm,
+    key_ref, value_ref, att_ref, out_weight_ref, out_ref, sem, out_sems,
 ):
-    step = pl.program_id(0)
     parts, tokens, _ = packed_ref.shape
-    lanes = out_weight_ref.shape[0]
+    lanes, width = out_weight_ref.shape
     heads = lanes // HEAD_SIZE
     cached = tokens // 2
     prefix = parts * cached
-    rows = out_ref.shape[0]
-    per_step = rows // tokens
+    blocks, rows, _ = att_ref.shape
+    per_block = rows // tokens
+    cols = width // heads
     rate = HEAD_SIZE ** (-0.5) * float(np.log2(np.e))
     fetch = pltpu.make_async_copy(out_weight_hbm, out_weight_ref, sem)
-
-    @pl.when(step == 0)
-    def _():
-        fetch.start()
-        for t in range(parts):
-            old = pl.ds(t * cached, cached)
-            new = pl.ds(prefix + t * tokens, tokens)
-            key_ref[old, :] = packed_ref[t, :cached, lanes + 2 * HEAD_SIZE :]
-            value_ref[old, :] = packed_ref[t, cached:, lanes + 2 * HEAD_SIZE :]
-            key_ref[new, :] = packed_ref[t, :, lanes : lanes + HEAD_SIZE]
-            value_ref[new, :] = packed_ref[t, :, lanes + HEAD_SIZE : lanes + 2 * HEAD_SIZE]
+    fetch.start()
+    for t in range(parts):
+        old = pl.ds(t * cached, cached)
+        new = pl.ds(prefix + t * tokens, tokens)
+        key_ref[old, :] = packed_ref[t, :cached, lanes + 2 * HEAD_SIZE :]
+        value_ref[old, :] = packed_ref[t, cached:, lanes + 2 * HEAD_SIZE :]
+        key_ref[new, :] = packed_ref[t, :, lanes : lanes + HEAD_SIZE]
+        value_ref[new, :] = packed_ref[t, :, lanes + HEAD_SIZE : lanes + 2 * HEAD_SIZE]
 
     in_prefix = lax.broadcasted_iota(jnp.int32, (rows, prefix), 1) < length_ref[0]
     causal = lax.broadcasted_iota(jnp.int32, (rows, rows), 1) <= lax.broadcasted_iota(
         jnp.int32, (rows, rows), 0
     )
 
-    def block(i):
-        spans = [(0, prefix)]
+    def spans_of(i):
+        middle = [(prefix, i * rows)] if i else []
+        return [(0, prefix)] + middle + [(prefix + i * rows, rows)]
+
+    def score(i, h):
+        query = jnp.concatenate(
+            [
+                packed_ref[i * per_block + t, :, h * HEAD_SIZE : (h + 1) * HEAD_SIZE]
+                for t in range(per_block)
+            ],
+            axis=0,
+        )
+        return [dot_nt(query, key_ref[pl.ds(start, size), :]) for start, size in spans_of(i)]
+
+    def finish(i, h, scores):
+        scores[0] = jnp.where(in_prefix, scores[0], -1e30)
+        scores[-1] = jnp.where(causal, scores[-1], -1e30)
+        top = functools.reduce(jnp.maximum, [jnp.max(s, axis=1, keepdims=True) for s in scores])
+        total, result = 0.0, 0.0
+        for s, (start, size) in zip(scores, spans_of(i), strict=True):
+            raised = jnp.exp2((s - top) * rate)
+            total = total + jnp.sum(raised, axis=1, keepdims=True)
+            result = result + dot(raised.astype(jnp.bfloat16), value_ref[pl.ds(start, size), :])
+        att_ref[i, :, h * HEAD_SIZE : (h + 1) * HEAD_SIZE] = (result / total).astype(jnp.bfloat16)
+
+    def out_copy(i, j):
+        return pltpu.make_async_copy(
+            out_ref.at[i, j],
+            out_hbm.at[pl.ds(i * rows, rows), pl.ds(j * cols, cols)],
+            out_sems.at[i, j],
+        )
+
+    def project(i, j):
+        out_ref[i, j] = dot(att_ref[i], out_weight_ref[:, j * cols : (j + 1) * cols]).astype(
+            jnp.bfloat16
+        )
+        out_copy(i, j).start()
+
+    units = [(i, h) for i in range(blocks) for h in range(heads)]
+    scores = score(*units[0])
+    for u, (i, h) in enumerate(units):
+        following = score(*units[u + 1]) if u + 1 < len(units) else None
         if i:
-            spans.append((prefix, i * rows))
-        spans.append((prefix + i * rows, rows))
-        for h in range(heads):
-            query = jnp.concatenate(
-                [
-                    packed_ref[i * per_step + t, :, h * HEAD_SIZE : (h + 1) * HEAD_SIZE]
-                    for t in range(per_step)
-                ],
-                axis=0,
-            )
-            scores = [dot_nt(query, key_ref[pl.ds(start, size), :]) for start, size in spans]
-            scores[0] = jnp.where(in_prefix, scores[0], -1e30)
-            scores[-1] = jnp.where(causal, scores[-1], -1e30)
-            top = functools.reduce(
-                jnp.maximum, [jnp.max(s, axis=1, keepdims=True) for s in scores]
-            )
-            total, result = 0.0, 0.0
-            for s, (start, size) in zip(scores, spans, strict=True):
-                raised = jnp.exp2((s - top) * rate)
-                total = total + jnp.sum(raised, axis=1, keepdims=True)
-                result = result + dot(
-                    raised.astype(jnp.bfloat16), value_ref[pl.ds(start, size), :]
-                )
-            att_ref[:, h * HEAD_SIZE : (h + 1) * HEAD_SIZE] = (result / total).astype(
-                jnp.bfloat16
-            )
-
-    for i in range(parts // per_step):
-        pl.when(step == i)(functools.partial(block, i))
-    pl.when(step == 0)(fetch.wait)
-    out_ref[...] = dot(att_ref[...], out_weight_ref[...]).astype(jnp.bfloat16)
-
-
-def attend(length, packed, out_weight, rows=512):
-    parts, tokens, columns = packed.shape
+            project(i - 1, h)
+        finish(i, h, scores)
+        scores = following
+        if (i, h) == (0, heads - 1):
+            fetch.wait()
+    for h in range(heads):
+        project(blocks - 1, h)
+    for i in range(blocks):
+        for j in range(heads):
+            out_copy(i, j).wait()
+
+
+def attend(length, packed, out_weight, rows=256):
+    parts, tokens, _ = packed.shape
     lanes, width = out_weight.shape
     span = parts * tokens
     total = span + parts * tokens // 2
+    heads = lanes // HEAD_SIZE
     return pl.pallas_call(
         attend_kernel,
-        grid=(span // rows,),
         in_specs=[
             pl.BlockSpec(memory_space=pltpu.SMEM),
             pl.BlockSpec(memory_space=pltpu.VMEM),
             pl.BlockSpec(memory_space=pltpu.HBM),
         ],
-        out_specs=pl.BlockSpec((rows, width), lambda i: (i, 0)),
+        out_specs=pl.BlockSpec(memory_space=pltpu.HBM),
         out_shape=jax.ShapeDtypeStruct((span, width), jnp.bfloat16),
         scratch_shapes=[
             pltpu.VMEM((total, HEAD_SIZE), jnp.bfloat16),
             pltpu.VMEM((total, HEAD_SIZE), jnp.bfloat16),
-            pltpu.VMEM((rows, lanes), jnp.bfloat16),
+            pltpu.VMEM((span // rows, rows, lanes), jnp.bfloat16),
             pltpu.VMEM((lanes, width), jnp.bfloat16),
+            pltpu.VMEM((span // rows, heads, rows, width // heads), jnp.bfloat16),
             pltpu.SemaphoreType.DMA,
+            pltpu.SemaphoreType.DMA((span // rows, heads)),
         ],
         compiler_params=pltpu.CompilerParams(vmem_limit_bytes=48 * MIB),
         name="attend",

time: 379 us -> 376 us (level)
  no operation moved by 1% of the time
where the time goes in v7:
time: 376 us; the launch traced here: 374 us
  waiting for transfers between devices  236 us (63%)
  Pallas kernels  88.3 us (23%)
  starting transfers between devices  33.2 us (9%)
  between operations  14.1 us (4%)
    all_to_all x4, waiting for transfers between devices, exchange(): lax.all_to_all(blocks, ('seq', 'exp'), split_axis=0, concat_axis=0, tiled...  164 us
    reduce_scatter x1, waiting for transfers between devices, per_device(): lax.psum_scatter(attend(prefix_len, packed, in_hbm(out_weight)), 'seq', s...  48.7 us
    pallas_call x2, Pallas kernels, expert(): pl.pallas_call(functools.partial(expert_kernel, deep=deep, ninth=ninth),...  44.1 us
    all_to_all x4, starting transfers between devices, exchange(): lax.all_to_all(blocks, ('seq', 'exp'), split_axis=0, concat_axis=0, tiled...  28.1 us
    all_to_all x1, waiting for transfers between devices, per_device(): lax.all_to_all(packed, 'seq', split_axis=0, concat_axis=0, tiled=True)  22.9 us
    pallas_call x1, Pallas kernels, attend(): pl.pallas_call(attend_kernel, in_specs=[pl.BlockSpec(memory_space=pltpu.S...  12.4 us
  transfers between devices with their start and end apart: 6, of which 6 were waited for; matrix products, arithmetic and copies ran while one was open for 0% of the time, Pallas kernels for 17%

profile of v7, /device:TPU:5, one launch (start us, length us, event | category | flops | bytes accessed | tf_op | source)
XLA Modules:
  0.0 374.3 jit_solution(5702275931641610987)
XLA Ops:
  6.5 3.0 pack.1
  9.5 5.2 %all-to-all-start = ((bf16[8,128,896]{2,1,0:T(8,128)(2,1)}), bf16[8,128,896]{2,1,0:T(8,128)(2,1)S(1)}, u32[]{:S(2)}, u32[]{:S(2)}) async-start(bf16[8,128,896]{2,1,0:T(8,128)(2,1)} %pack.1), calls=%async_computation | async-start | bytes 3670016 | tf_op jit(solution)/shard_map/all_to_all | solution.py:649
  14.7 0.0 reduce-scatter.2.cloned.1.call-start
  15.3 22.9 %all-to-all-done.packed_ref = bf16[8,128,896]{2,1,0:T(8,128)(2,1)S(1)} async-done(((bf16[8,128,896]{2,1,0:T(8,128)(2,1)}), bf16[8,128,896]{2,1,0:T(8,128)(2,1)S(1)}, u32[]{:S(2)}, u32[]{:S(2)}) %all-to-all-start) | async-done | bytes 1835040 | tf_op jit(solution)/shard_map/all_to_all | solution.py:649
  38.2 12.4 %attend.1 = bf16[1024,4096]{1,0:T(8,128)(2,1)} custom-call(s32[1]{0:T(128)S(6)} %copy.16.length_ref, bf16[8,128,896]{2,1,0:T(8,128)(2,1)S(1)} %all-to-all-done.packed_ref, bf16[512,4096]{1,0:T(8,128)(2,1)} %out_weight_hbm.1), custom_call_target="tpu_custom_call" | custom-call | tf_op jit(solution)/shard_map/attend/pallas_call | solution.py:167
  50.6 0.0 copy-start.3
  50.6 0.0 copy-start
  50.7 0.0 copy-start.2
  50.7 0.0 reduce-scatter.2.cloned.1.call-update
  50.7 0.6 copy-done.3
  51.3 0.7 copy.15
  52.1 2.5 plan.1
  54.6 48.7 %reduce-scatter.2.cloned.1.call-done.proj_ref.refs_2_.refs_3_ = bf16[128,4096]{1,0:T(8,128)(2,1)} async-done(((bf16[1024,4096]{1,0:T(8,128)(2,1)}), bf16[128,4096]{1,0:T(8,128)(2,1)}) %reduce-scatter.2.cloned.1.call-update) | async-done | bytes 1048592 | tf_op jit(solution)/shard_map/reduce_scatter | solution.py:650
  103.2 0.0 copy-done
  103.2 0.0 copy-done.2
  103.2 4.9 %route_first.1 = (bf16[1024,2048]{1,0:T(8,128)(2,1)}, bf16[256,2048]{1,0:T(8,128)(2,1)}) custom-call(bf16[128,4096]{1,0:T(8,128)(2,1)S(1)} %bitcast.12, bf16[128,4096]{1,0:T(8,128)(2,1)} %reduce-scatter.2.cloned.1.call-done.proj_ref.refs_2_.refs_3_, f32[1,4096]{1,0:T(1,128)S(1)} %bitcast.15, bf16[1024,256]{1,0:T(8,128)(2,1)S(1)} %get-tuple-element.14.pick_ref), custom_call_target="tpu_custom_call" | custom-call | tf_op jit(solution)/shard_map/route_first/pallas_call | solution.py:276
  108.1 9.1 %all-to-all-start.3 = ((bf16[128,8,2048]{2,1,0:T(8,128)(2,1)}), bf16[128,8,2048]{2,1,0:T(8,128)(2,1)}, u32[]{:S(2)}, u32[]{:S(2)}) async-start(bf16[128,8,2048]{2,1,0:T(8,128)(2,1)} %bitcast.19), calls=%async_computation.4 | async-start | bytes 8388608 | tf_op jit(solution)/shard_map/all_to_all | solution.py:661
  117.2 6.0 %route_second.1 = bf16[1024,2560]{1,0:T(8,128)(2,1)} custom-call(bf16[256,2048]{1,0:T(8,128)(2,1)} %get-tuple-element.15.halves_ref, bf16[1024,256]{1,0:T(8,128)(2,1)} %get-tuple-element.16.pick_ref, bf16[128,128]{1,0:T(8,128)(2,1)} %get-tuple-element.17.ninth_ref), custom_call_target="tpu_custom_call" | custom-call | tf_op jit(solution)/shard_map/route_second/pallas_call | solution.py:326
  123.1 44.6 %all-to-all-done.3 = bf16[128,8,2048]{2,1,0:T(8,128)(2,1)} async-done(((bf16[128,8,2048]{2,1,0:T(8,128)(2,1)}), bf16[128,8,2048]{2,1,0:T(8,128)(2,1)}, u32[]{:S(2)}, u32[]{:S(2)}) %all-to-all-start.3) | async-done | bytes 4194336 | tf_op jit(solution)/shard_map/all_to_all | solution.py:661
  167.7 6.2 %all-to-all-start.1 = ((bf16[128,8,2560]{2,1,0:T(8,128)(2,1)}), bf16[128,8,2560]{2,1,0:T(8,128)(2,1)}, u32[]{:S(2)}, u32[]{:S(2)}) async-start(bf16[128,8,2560]{2,1,0:T(8,128)(2,1)} %bitcast.17), calls=%async_computation.2 | async-start | bytes 10485760 | tf_op jit(solution)/shard_map/all_to_all | solution.py:661
  173.9 20.4 %expert_first.1 = bf16[1024,2048]{1,0:T(8,128)(2,1)} custom-call(bf16[1024,2048]{1,0:T(8,128)(2,1)} %bitcast.8.refs_0_, bf16[1,4096,768]{2,1,0:T(8,128)(2,1)} %refs_1_.3, bf16[1,4096,768]{2,1,0:T(8,128)(2,1)} %refs_2_.3, bf16[1,768,4096]{2,1,0:T(8,128)(2,1)} %refs_4_.3, bf16[1,768,4096]{2,1,0:T(8,128)(2,1)} %refs_4_.3), custom_call_target="tpu_custom_call" | custom-call | tf_op jit(solution)/shard_map/expert_first/pallas_call | solution.py:491
  194.3 41.8 %all-to-all-done.1 = bf16[128,8,2560]{2,1,0:T(8,128)(2,1)} async-done(((bf16[128,8,2560]{2,1,0:T(8,128)(2,1)}), bf16[128,8,2560]{2,1,0:T(8,128)(2,1)}, u32[]{:S(2)}, u32[]{:S(2)}) %all-to-all-start.1) | async-done | bytes 5242912 | tf_op jit(solution)/shard_map/all_to_all | solution.py:661
  236.1 6.6 %all-to-all-start.4 = ((bf16[128,8,2048]{2,1,0:T(8,128)(2,1)}), bf16[128,8,2048]{2,1,0:T(8,128)(2,1)}, u32[]{:S(2)}, u32[]{:S(2)}) async-start(bf16[128,8,2048]{2,1,0:T(8,128)(2,1)} %bitcast.18), calls=%async_computation.5 | async-start | bytes 8388608 | tf_op jit(solution)/shard_map/all_to_all | solution.py:661
  242.7 23.7 %expert_second.1 = bf16[1024,2560]{1,0:T(8,128)(2,1)} custom-call(bf16[1024,2560]{1,0:T(8,128)(2,1)} %bitcast.4.refs_0_, bf16[1,4096,768]{2,1,0:T(8,128)(2,1)} %refs_1_.3, bf16[1,4096,768]{2,1,0:T(8,128)(2,1)} %refs_2_.3, bf16[1,768,4096]{2,1,0:T(8,128)(2,1)} %refs_4_.3, bf16[1,768,4096]{2,1,0:T(8,128)(2,1)} %refs_4_.3), custom_call_target="tpu_custom_call" | custom-call | tf_op jit(solution)/shard_map/expert_second/pallas_call | solution.py:491
  266.4 26.8 %all-to-all-done.4 = bf16[128,8,2048]{2,1,0:T(8,128)(2,1)} async-done(((bf16[128,8,2048]{2,1,0:T(8,128)(2,1)}), bf16[128,8,2048]{2,1,0:T(8,128)(2,1)}, u32[]{:S(2)}, u32[]{:S(2)}) %all-to-all-start.4) | async-done | bytes 4194336 | tf_op jit(solution)/shard_map/all_to_all | solution.py:661
  293.2 6.2 %all-to-all-start.2 = ((bf16[128,8,2560]{2,1,0:T(8,128)(2,1)}), bf16[128,8,2560]{2,1,0:T(8,128)(2,1)}, u32[]{:S(2)}, u32[]{:S(2)}) async-start(bf16[128,8,2560]{2,1,0:T(8,128)(2,1)} %bitcast.16), calls=%async_computation.3 | async-start | bytes 10485760 | tf_op jit(solution)/shard_map/all_to_all | solution.py:661
  299.5 0.0 copy-start.1
  299.5 1.2 copy-done.1
  300.7 3.4 weights.1
  304.1 6.2 %combine_first.1.partial_hbm = f32[2,128,2048]{2,1,0:T(8,128)} custom-call(bf16[1024,2048]{1,0:T(8,128)(2,1)} %bitcast.10.rows_ref, bf16[2,256,1024]{2,1,0:T(8,128)(2,1)} %get-tuple-element.20.weight_ref, bf16[128,4096]{1,0:T(8,128)(2,1)S(1)} %bitcast.13, bf16[128,4096]{1,0:T(8,128)(2,1)S(1)} %bitcast.14, ...), custom_call_target="tpu_custom_call" | custom-call | tf_op jit(solution)/shard_map/combine_first/pallas_call | solution.py:531
  310.3 51.3 %all-to-all-done.2 = bf16[128,8,2560]{2,1,0:T(8,128)(2,1)} async-done(((bf16[128,8,2560]{2,1,0:T(8,128)(2,1)}), bf16[128,8,2560]{2,1,0:T(8,128)(2,1)}, u32[]{:S(2)}, u32[]{:S(2)}) %all-to-all-start.2) | async-done | bytes 5242912 | tf_op jit(solution)/shard_map/all_to_all | solution.py:661
  361.6 5.8 %combine_second.1 = bf16[128,4096]{1,0:T(8,128)(2,1)} custom-call(bf16[1024,2560]{1,0:T(8,128)(2,1)} %bitcast.6.rows_hbm, f32[2,128,2048]{2,1,0:T(8,128)} %combine_first.1.partial_hbm, bf16[2,256,1024]{2,1,0:T(8,128)(2,1)S(1)} %get-tuple-element.21.weight_ref, bf16[256,128]{1,0:T(8,128)(2,1)S(1)} %get-tuple-element.22.ninth_ref), custom_call_target="tpu_custom_call" | custom-call | tf_op jit(solution)/shard_map/combine_second/pallas_call | solution.py:603
Async XLA Ops:
  9.5 28.7 %all-to-all-start = ((bf16[8,128,896]{2,1,0:T(8,128)(2,1)}), bf16[8,128,896]{2,1,0:T(8,128)(2,1)S(1)}, u32[]{:S(2)}, u32[]{:S(2)}) async-start(bf16[8,128,896]{2,1,0:T(8,128)(2,1)} %pack.1), calls=%async_computation | async-start | bytes 3670016 | tf_op jit(solution)/shard_map/all_to_all | solution.py:649
  14.7 88.6 %reduce-scatter.2.cloned.1.call-start = ((), (), s32[]{:S(2)}) async-start(), calls=%async_computation.6 | async-start | bytes 9437184 | tf_op jit(solution)/shard_map/reduce_scatter | solution.py:650
  50.6 0.7 copy-start.3
  50.6 52.6 %copy-start = (bf16[1,128,4096]{2,1,0:T(8,128)(2,1)S(1)}, bf16[1,128,4096]{2,1,0:T(8,128)(2,1)}, u32[]{:S(2)}) copy-start(bf16[1,128,4096]{2,1,0:T(8,128)(2,1)} %param.14) | copy-start | bytes 3145732
  50.7 52.6 %copy-start.2 = (f32[4096]{0:T(1024)S(1)}, f32[4096]{0:T(1024)}, u32[]{:S(2)}) copy-start(f32[4096]{0:T(1024)} %param.22) | copy-start | bytes 49156
  108.1 59.6 %all-to-all-start.3 = ((bf16[128,8,2048]{2,1,0:T(8,128)(2,1)}), bf16[128,8,2048]{2,1,0:T(8,128)(2,1)}, u32[]{:S(2)}, u32[]{:S(2)}) async-start(bf16[128,8,2048]{2,1,0:T(8,128)(2,1)} %bitcast.19), calls=%async_computation.4 | async-start | bytes 8388608 | tf_op jit(solution)/shard_map/all_to_all | solution.py:661
  167.7 68.4 %all-to-all-start.1 = ((bf16[128,8,2560]{2,1,0:T(8,128)(2,1)}), bf16[128,8,2560]{2,1,0:T(8,128)(2,1)}, u32[]{:S(2)}, u32[]{:S(2)}) async-start(bf16[128,8,2560]{2,1,0:T(8,128)(2,1)} %bitcast.17), calls=%async_computation.2 | async-start | bytes 10485760 | tf_op jit(solution)/shard_map/all_to_all | solution.py:661
  236.1 57.1 %all-to-all-start.4 = ((bf16[128,8,2048]{2,1,0:T(8,128)(2,1)}), bf16[128,8,2048]{2,1,0:T(8,128)(2,1)}, u32[]{:S(2)}, u32[]{:S(2)}) async-start(bf16[128,8,2048]{2,1,0:T(8,128)(2,1)} %bitcast.18), calls=%async_computation.5 | async-start | bytes 8388608 | tf_op jit(solution)/shard_map/all_to_all | solution.py:661
  293.2 68.4 %all-to-all-start.2 = ((bf16[128,8,2560]{2,1,0:T(8,128)(2,1)}), bf16[128,8,2560]{2,1,0:T(8,128)(2,1)}, u32[]{:S(2)}, u32[]{:S(2)}) async-start(bf16[128,8,2560]{2,1,0:T(8,128)(2,1)} %bitcast.16), calls=%async_computation.3 | async-start | bytes 10485760 | tf_op jit(solution)/shard_map/all_to_all | solution.py:661
  299.5 1.2 copy-start.1
Sparse Core Ops, SparseCore 0:
  50.8 52.3 reduce-scatter.1
